TPU v7x, 32 devices: a whole 2x2x4 slice. The times are simulated.
32 devices in a mesh: gx: 4 (over x, core), gy: 8 (over z, y).
Axes of the slice: x: 2, y: 2, z: 4, core: 2. Of those that a mesh axis runs over, the one named last changes fastest.
Arguments:
- text_in: bfloat16 [16384, 768], P(('gx', 'gy')), may hold values from -6 to 6
- layout_in: bfloat16 [16384, 192], P(('gx', 'gy')), may hold values from -6 to 6
- lengths: int32 [32], P(('gx', 'gy')), may hold values from 64 to 512, as said below
- dup_rows: int32 [16384], P(('gx', 'gy')), may hold values from 0 to 1, as said below
- text_attention: float32 [3072, 768], P(('gx', 'gy')), may hold values from -3 to 3
- text_up: float32 [768, 3072], P(None, ('gx', 'gy')), may hold values from -0.21875 to 0.21875
- text_down: float32 [3072, 768], P(('gx', 'gy')), may hold values from -0.109375 to 0.109375
- text_vector: float32 [9216], P(('gx', 'gy')), may hold values from -2 to 2
- layout_attention: float32 [768, 192], P(('gx', 'gy')), may hold values from -3 to 3
- layout_up: float32 [192, 768], P(None, ('gx', 'gy')), may hold values from -0.4375 to 0.4375
- layout_down: float32 [768, 192], P(('gx', 'gy')), may hold values from -0.21875 to 0.21875
- layout_vector: float32 [2304], P(('gx', 'gy')), may hold values from -2 to 2
- text_cotangent: bfloat16 [16384, 768], P(('gx', 'gy')), may hold values from -6 to 6
- layout_cotangent: bfloat16 [16384, 192], P(('gx', 'gy')), may hold values from -6 to 6
Outputs:
- text_out: bfloat16 [16384, 768], P(('gx', 'gy'))
- layout_out: bfloat16 [16384, 192], P(('gx', 'gy'))
- text_in_grad: bfloat16 [16384, 768], P(('gx', 'gy'))
- layout_in_grad: bfloat16 [16384, 192], P(('gx', 'gy'))
- text_attention_grad: float32 [3072, 768], P(('gx', 'gy'))
- text_up_grad: float32 [768, 3072], P(None, ('gx', 'gy'))
- text_down_grad: float32 [3072, 768], P(('gx', 'gy'))
- text_vector_grad: float32 [9216], P(('gx', 'gy'))
- layout_attention_grad: float32 [768, 192], P(('gx', 'gy'))
- layout_up_grad: float32 [192, 768], P(None, ('gx', 'gy'))
- layout_down_grad: float32 [768, 192], P(('gx', 'gy'))
- layout_vector_grad: float32 [2304], P(('gx', 'gy'))
Inputs may be any that keep to these rules, and one draw needn't show every extreme that they name: `lengths`: each stretch has at least 64 live tokens; some stretch is full. `dup_rows`: within a stretch the ones form a prefix of at most 128 rows.
All inputs are finite; a program needn't handle non-finite values.
Results may differ from a plain program's by a relative error of at most 0.013.
The roundings to bfloat16 on the way count: a program that leaves them out, or rounds other values in their place, can miss the bound.
Values may be sent and summed in bfloat16 or wider, within the bound.
No kernel may reach another device: no remote copies, remote signals or barrier semaphores. Data moves between devices by JAX's collectives and lax.ppermute only.
A program may use at most 256 MiB of HBM per device.

v0:
```python
import functools
import math

import jax
import jax.numpy as jnp
from jax import lax
from jax.experimental import pallas as pl
from jax.experimental.pallas import tpu as pltpu
from jax.sharding import PartitionSpec as P


AXES = ("gx", "gy")


def exchange_dims(shape):
    gx, gy = shape["gx"], shape["gy"]
    outer = {8: 4, 32: 4}.get(gy, gy)
    inner = gy // outer
    core = 2 if gx % 2 == 0 else 1
    core_dim = (gy, core)
    x_dim = (gy * core, gx // core)
    if inner <= outer:
        z_dim, y_dim = (inner, outer), (1, inner)
    else:
        z_dim, y_dim = (1, inner), (inner, outer)
    return x_dim, core_dim, z_dim, y_dim


def orders(shape):
    x_dim, core_dim, z_dim, y_dim = exchange_dims(shape)
    return ((z_dim, y_dim, x_dim, core_dim), (z_dim, x_dim, y_dim, core_dim))


def offsets(order):
    table = [0]
    for stride, size in order:
        table = [offset ^ (stride * step) for step in range(size) for offset in table]
    return table


def swap(array, offset, count):
    return lax.ppermute(array, AXES, [(device, device ^ offset) for device in range(count)])


def gather_part(part, order, count):
    held = part[None]
    for stride, size in order:
        pieces = [held] + [swap(held, stride * step, count) for step in range(1, size)]
        held = jnp.concatenate(pieces, 0)
    return held


def scatter_part(parts, order, count):
    held = parts
    for stride, size in reversed(order):
        held = held.reshape((size, held.shape[0] // size) + held.shape[1:])
        total = held[0].astype(jnp.float32)
        for step in range(1, size):
            total = total + swap(held[step], stride * step, count).astype(jnp.float32)
        last = (stride, size) == order[0]
        held = total if last else total.astype(jnp.bfloat16)
    return held[0]


def flat_index(gy):
    return lax.axis_index("gx") * gy + lax.axis_index("gy")


def positions(order, count):
    table = offsets(order)
    inverse = [0] * count
    for position, offset in enumerate(table):
        inverse[offset] = position
    return jnp.array(table, jnp.int32), jnp.array(inverse, jnp.int32)


def gather_rows(shard, shape, me):
    count = shape["gx"] * shape["gy"]
    half = shard.shape[0] // 2
    pieces = []
    for index, order in enumerate(orders(shape)):
        held = gather_part(shard[index * half : (index + 1) * half], order, count)
        inverse = positions(order, count)[1]
        pieces.append(jnp.take(held, inverse[jnp.arange(count) ^ me], axis=0))
    return jnp.concatenate(pieces, 1)


def scatter_rows(grads, shape, me):
    count = shape["gx"] * shape["gy"]
    half = grads.shape[1] // 2
    pieces = []
    for index, order in enumerate(orders(shape)):
        table = positions(order, count)[0]
        parts = jnp.take(grads[:, index * half : (index + 1) * half], me ^ table, axis=0)
        pieces.append(scatter_part(parts, order, count))
    return jnp.concatenate(pieces, 0)


def pad_cols(array, width):
    return jnp.pad(array, ((0, 0),) * (array.ndim - 1) + ((0, width - array.shape[-1]),))


def pack_rows(text_rows, layout_rows, vectors):
    side = D // 3
    layouts = jnp.concatenate([pad_cols(rows, side) for rows in layout_rows], -1)
    packed = jnp.concatenate([text_rows, layouts, pad_cols(vectors, D)[..., None, :]], -2)
    rows = packed.shape[-2]
    extra = -rows % 16
    return jnp.pad(packed, ((0, 0),) * (packed.ndim - 2) + ((0, extra), (0, 0)))


def unpack_rows(packed, text_rows, layout_rows, text_vec, layout_vec):
    side = D // 3
    text = packed[..., :text_rows, :]
    block = packed[..., text_rows : text_rows + layout_rows, :]
    layouts = [block[..., side * index : side * index + DL] for index in range(3)]
    vectors = packed[..., text_rows + layout_rows, :]
    return text, layouts, vectors[..., :text_vec], vectors[..., text_vec : text_vec + layout_vec]


D = 768
DL = 192
HEADS = 12
FF = 4 * D
FFL = 4 * DL


EPS = 1e-05
NEG = -1e30


def matmul(left, right):
    return jnp.dot(left, right, preferred_element_type=jnp.float32)


def contract_rows(left, right):
    return lax.dot_general(
        left, right, (((0,), (0,)), ((), ())), preferred_element_type=jnp.float32
    )


def contract_cols(left, right):
    return lax.dot_general(
        left, right, (((1,), (1,)), ((), ())), preferred_element_type=jnp.float32
    )


def vector_parts(vector, width):
    values = vector.astype(jnp.float32)
    return [values[index * width : (index + 1) * width] for index in range(8)] + [
        values[8 * width :]
    ]


def normalize(resid, gain, shift):
    center = resid - jnp.mean(resid, -1, keepdims=True)
    varian = jnp.mean(center * center, -1, keepdims=True)
    inverse = lax.rsqrt(varian + EPS)
    scaled = center * inverse
    return (scaled * gain + shift, scaled, inverse)


def norm_back(grad, scaled, inverse, gain):
    weighted = grad * gain
    inner = jnp.mean(weighted, -1, keepdims=True)
    across = jnp.mean(weighted * scaled, -1, keepdims=True)
    return inverse * (weighted - inner - scaled * across)


def exact_gelu(value):
    return jax.nn.gelu(value, approximate=False)


def open_stream(inputs, weights, width):
    parts = vector_parts(weights[3], width)
    stacked = weights[0][: 3 * width].reshape(3, width, width)
    projected = jnp.einsum("nd,jde->jne", inputs, stacked, preferred_element_type=jnp.float32)
    query = (projected[0] + parts[0]).astype(jnp.bfloat16)
    keys = projected[1].astype(jnp.bfloat16)
    values = (projected[2] + parts[1]).astype(jnp.bfloat16)
    return (query, keys, values)


def heads_view(array):
    return array.reshape(array.shape[0], HEADS, array.shape[1] // HEADS)


def head_scale(array):
    return 1.0 / math.sqrt(array.shape[1] // HEADS)


def joint_scores(text_query, text_keys, layout_query, layout_keys, length):
    rows = text_query.shape[0]
    text_part = jnp.einsum(
        "qhd,khd->hqk",
        heads_view(text_query),
        heads_view(text_keys),
        preferred_element_type=jnp.float32,
    )
    layout_part = jnp.einsum(
        "qhd,khd->hqk",
        heads_view(layout_query),
        heads_view(layout_keys),
        preferred_element_type=jnp.float32,
    )
    scores = text_part * head_scale(text_query) + layout_part * head_scale(layout_query)
    visible = jnp.arange(rows) < length
    return jnp.where(visible[None, None, :], scores, NEG)


def weigh_values(probs, values):
    mixed = jnp.einsum(
        "hqk,khd->qhd", probs, heads_view(values), preferred_element_type=jnp.float32
    )
    return mixed.reshape(values.shape[0], values.shape[1])


def attend_forward(pieces):
    text_query, text_keys, text_values, layout_query, layout_keys, layout_values, length = pieces
    scores = joint_scores(text_query, text_keys, layout_query, layout_keys, length)
    top = jnp.max(scores, -1, keepdims=True)
    expo = jnp.exp(scores - top)
    total = jnp.sum(expo, -1, keepdims=True)
    probs = (expo / total).astype(jnp.bfloat16)
    text_att = weigh_values(probs, text_values).astype(jnp.bfloat16)
    layout_att = weigh_values(probs, layout_values).astype(jnp.bfloat16)
    return (text_att, layout_att, (top + jnp.log(total))[:, :, 0])


def values_grad(probs_low, grad_out):
    moved = jnp.einsum(
        "hqk,qhd->khd", probs_low, heads_view(grad_out), preferred_element_type=jnp.float32
    )
    return moved.reshape(grad_out.shape[0], grad_out.shape[1]).astype(jnp.bfloat16)


def query_keys_grad(score_grads, query, keys):
    scale = head_scale(query)
    rows, width = query.shape
    query_grad = jnp.zeros((rows, HEADS, width // HEADS), jnp.float32)
    keys_grad = jnp.zeros((rows, HEADS, width // HEADS), jnp.float32)
    for score_grad in score_grads:
        query_grad = query_grad + jnp.einsum(
            "hqk,khd->qhd", score_grad, heads_view(keys), preferred_element_type=jnp.float32
        )
        keys_grad = keys_grad + jnp.einsum(
            "hqk,qhd->khd", score_grad, heads_view(query), preferred_element_type=jnp.float32
        )
    query_grad = query_grad * scale
    keys_grad = keys_grad * scale
    return (
        query_grad.reshape(rows, width).astype(jnp.bfloat16),
        keys_grad.reshape(rows, width).astype(jnp.bfloat16),
    )


def softmax_back(probs, mixed):
    return (probs * (mixed - jnp.sum(probs * mixed, -1, keepdims=True))).astype(jnp.bfloat16)


def attend_backward(pieces):
    (
        text_query,
        text_keys,
        text_values,
        layout_query,
        layout_keys,
        layout_values,
        length,
        log_total,
        text_grad,
        layout_grad,
    ) = pieces
    scores = joint_scores(text_query, text_keys, layout_query, layout_keys, length)
    probs = jnp.exp(scores - log_total[:, :, None])
    probs_low = probs.astype(jnp.bfloat16)
    text_values_grad = values_grad(probs_low, text_grad)
    layout_values_grad = values_grad(probs_low, layout_grad)
    text_mixed = jnp.einsum(
        "qhd,khd->hqk",
        heads_view(text_grad),
        heads_view(text_values),
        preferred_element_type=jnp.float32,
    )
    layout_mixed = jnp.einsum(
        "qhd,khd->hqk",
        heads_view(layout_grad),
        heads_view(layout_values),
        preferred_element_type=jnp.float32,
    )
    text_score_grad = softmax_back(probs, text_mixed)
    layout_score_grad = softmax_back(probs, layout_mixed)
    text_query_grad, text_keys_grad = query_keys_grad((text_score_grad,), text_query, text_keys)
    layout_query_grad, layout_keys_grad = query_keys_grad(
        (text_score_grad, layout_score_grad), layout_query, layout_keys
    )
    return (
        text_query_grad,
        text_keys_grad,
        text_values_grad,
        layout_query_grad,
        layout_keys_grad,
        layout_values_grad,
    )


def close_stream(inputs, attended, weights, width):
    attention_w, up_w, down_w, vector = weights
    parts = vector_parts(vector, width)
    after = matmul(attended, attention_w[3 * width :]) + parts[2]
    first, scaled_one, inverse_one = normalize(
        inputs.astype(jnp.float32) + after, parts[3], parts[4]
    )
    first_low = first.astype(jnp.bfloat16)
    upper = contract_cols(first_low, up_w) + parts[8]
    hidden_act = exact_gelu(upper).astype(jnp.bfloat16)
    final, scaled_two, inverse_two = normalize(
        first + matmul(hidden_act, down_w) + parts[5], parts[6], parts[7]
    )
    return (final, (scaled_one, inverse_one, first_low, upper, hidden_act, scaled_two, inverse_two))


def close_back(cotan, attended, saved, weights, width):
    scaled_one, inverse_one, first_low, upper, hidden_act, scaled_two, inverse_two = saved
    attention_w, up_w, down_w, vector = weights
    parts = vector_parts(vector, width)
    gain_two_grad = jnp.sum(cotan * scaled_two, 0)
    shift_two_grad = jnp.sum(cotan, 0)
    second_grad = norm_back(cotan, scaled_two, inverse_two, parts[6])
    branch_low = second_grad.astype(jnp.bfloat16)
    down_grad = contract_rows(hidden_act, branch_low)
    bias_down_grad = jnp.sum(branch_low.astype(jnp.float32), 0)
    act_grad = contract_cols(branch_low, down_w)
    gelu_back = jax.vjp(exact_gelu, upper)[1]
    upper_low = gelu_back(act_grad)[0].astype(jnp.bfloat16)
    up_grad_flipped = contract_rows(upper_low, first_low)
    bias_up_grad = jnp.sum(upper_low.astype(jnp.float32), 0)
    first_grad = second_grad + matmul(upper_low, up_w)
    gain_one_grad = jnp.sum(first_grad * scaled_one, 0)
    shift_one_grad = jnp.sum(first_grad, 0)
    resid_grad = norm_back(first_grad, scaled_one, inverse_one, parts[3])
    after_low = resid_grad.astype(jnp.bfloat16)
    out_weight_grad = contract_rows(attended, after_low)
    bias_out_grad = jnp.sum(after_low.astype(jnp.float32), 0)
    attended_grad = contract_cols(after_low, attention_w[3 * width :]).astype(jnp.bfloat16)
    tail = (
        bias_out_grad,
        gain_one_grad,
        shift_one_grad,
        bias_down_grad,
        gain_two_grad,
        shift_two_grad,
        bias_up_grad,
    )
    return (resid_grad, attended_grad, out_weight_grad, tail, up_grad_flipped, down_grad)


def open_back(
    inputs,
    resid_grad,
    query_grad,
    keys_grad,
    values_grad,
    out_weight_grad,
    tail,
    attention_w,
    width,
):
    stacked_grad = jnp.stack([query_grad, keys_grad, values_grad])
    weight_grad = jnp.einsum(
        "nd,jne->jde", inputs, stacked_grad, preferred_element_type=jnp.float32
    ).reshape(3 * width, width)
    input_grad = resid_grad + jnp.einsum(
        "jne,jde->nd",
        stacked_grad,
        attention_w[: 3 * width].reshape(3, width, width),
        preferred_element_type=jnp.float32,
    )
    bias_query_grad = jnp.sum(query_grad.astype(jnp.float32), 0)
    bias_value_grad = jnp.sum(values_grad.astype(jnp.float32), 0)
    (
        bias_out_grad,
        gain_one_grad,
        shift_one_grad,
        bias_down_grad,
        gain_two_grad,
        shift_two_grad,
        bias_up_grad,
    ) = tail
    vector_grad = jnp.concatenate(
        [
            bias_query_grad,
            bias_value_grad,
            bias_out_grad,
            gain_one_grad,
            shift_one_grad,
            bias_down_grad,
            gain_two_grad,
            shift_two_grad,
            bias_up_grad,
        ]
    )
    attention_grad = jnp.concatenate([weight_grad, out_weight_grad], 0)
    return (input_grad, attention_grad, vector_grad)


def by_stretch(array, stretches):
    return array.reshape((stretches, array.shape[0] // stretches) + array.shape[1:])


def shards(
    shape,
    text_in,
    layout_in,
    lengths,
    dup_rows,
    text_attention,
    text_up,
    text_down,
    text_vector,
    layout_attention,
    layout_up,
    layout_down,
    layout_vector,
    text_cotangent,
    layout_cotangent,
):
    count = shape["gx"] * shape["gy"]
    me = flat_index(shape["gy"])
    text_rows, layout_rows = text_attention.shape[0], layout_attention.shape[0]
    text_vec, layout_vec = text_vector.shape[0], layout_vector.shape[0]
    packed = pack_rows(
        text_attention,
        [layout_attention, layout_up.T, layout_down],
        jnp.concatenate([text_vector, layout_vector]),
    ).astype(jnp.bfloat16)
    gathered = gather_rows(packed, shape, me)
    up_all = gather_rows(text_up.T.astype(jnp.bfloat16), shape, me).reshape(-1, D)
    down_all = gather_rows(text_down.astype(jnp.bfloat16), shape, me).reshape(-1, D)
    text_all, layouts_all, text_vec_all, layout_vec_all = unpack_rows(
        gathered, text_rows, layout_rows, text_vec, layout_vec
    )
    text_weights = (text_all.reshape(-1, D), up_all, down_all, text_vec_all.reshape(-1))
    layout_weights = tuple(rows.reshape(-1, DL) for rows in layouts_all) + (
        layout_vec_all.reshape(-1),
    )
    stretches = lengths.shape[0]
    text_query, text_keys, text_values = open_stream(text_in, text_weights, D)
    layout_query, layout_keys, layout_values = open_stream(layout_in, layout_weights, DL)
    opened = (text_query, text_keys, text_values, layout_query, layout_keys, layout_values)
    opened_stretches = tuple((by_stretch(array, stretches) for array in opened))
    text_att, layout_att, log_total = lax.map(attend_forward, opened_stretches + (lengths,))
    text_att = text_att.reshape(-1, D)
    layout_att = layout_att.reshape(-1, DL)
    text_final, text_saved = close_stream(text_in, text_att, text_weights, D)
    layout_final, layout_saved = close_stream(layout_in, layout_att, layout_weights, DL)
    text_back, layout_back = text_weights, layout_weights
    span = text_in.shape[0] // stretches
    position = jnp.arange(span)
    keep = (position[None, :] < lengths[:, None]) & (dup_rows.reshape(stretches, span) == 0)
    keep = keep.reshape(-1, 1).astype(jnp.float32)
    text_cot = text_cotangent.astype(jnp.float32) * keep
    layout_cot = layout_cotangent.astype(jnp.float32) * keep
    text_resid, text_att_grad, text_out_w, text_tail, text_up_flipped, text_down_grad = close_back(
        text_cot, text_att, text_saved, text_back, D
    )
    (
        layout_resid,
        layout_att_grad,
        layout_out_w,
        layout_tail,
        layout_up_flipped,
        layout_down_grad,
    ) = close_back(layout_cot, layout_att, layout_saved, layout_back, DL)
    back_pieces = opened_stretches + (
        lengths,
        log_total,
        by_stretch(text_att_grad, stretches),
        by_stretch(layout_att_grad, stretches),
    )
    grads = lax.map(attend_backward, back_pieces)
    (
        text_query_grad,
        text_keys_grad,
        text_values_grad,
        layout_query_grad,
        layout_keys_grad,
        layout_values_grad,
    ) = tuple((array.reshape(-1, array.shape[-1]) for array in grads))
    text_input_grad, text_attention_grad, text_vector_grad = open_back(
        text_in,
        text_resid,
        text_query_grad,
        text_keys_grad,
        text_values_grad,
        text_out_w,
        text_tail,
        text_back[0],
        D,
    )
    layout_input_grad, layout_attention_grad, layout_vector_grad = open_back(
        layout_in,
        layout_resid,
        layout_query_grad,
        layout_keys_grad,
        layout_values_grad,
        layout_out_w,
        layout_tail,
        layout_back[0],
        DL,
    )

    def by_owner(array):
        return array.reshape((count, array.shape[0] // count) + array.shape[1:])

    attention_sum = scatter_rows(
        pack_rows(
            by_owner(text_attention_grad),
            [by_owner(g) for g in (layout_attention_grad, layout_up_flipped, layout_down_grad)],
            jnp.concatenate([by_owner(text_vector_grad), by_owner(layout_vector_grad)], -1),
        ).astype(jnp.bfloat16),
        shape,
        me,
    )
    up_sum = scatter_rows(by_owner(text_up_flipped).astype(jnp.bfloat16), shape, me)
    down_sum = scatter_rows(by_owner(text_down_grad).astype(jnp.bfloat16), shape, me)
    text_attention_sum, layout_sums, text_vec_sum, layout_vec_sum = unpack_rows(
        attention_sum, text_rows, layout_rows, text_vec, layout_vec
    )
    return (
        text_final.astype(jnp.bfloat16),
        layout_final.astype(jnp.bfloat16),
        text_input_grad.astype(jnp.bfloat16),
        layout_input_grad.astype(jnp.bfloat16),
        text_attention_sum,
        up_sum.T,
        down_sum,
        text_vec_sum,
        layout_sums[0],
        layout_sums[1].T,
        layout_sums[2],
        layout_vec_sum,
    )


BF = jnp.bfloat16
F32 = jnp.float32
CAT = 128
TEXT_LANES = D // HEADS
LAYOUT_LANES = DL // HEADS
MASK_LANE = TEXT_LANES + LAYOUT_LANES
VMEM_SPEC = pl.BlockSpec(memory_space=pltpu.VMEM)
SMEM_SPEC = pl.BlockSpec(memory_space=pltpu.SMEM)
ANY_SPEC = pl.BlockSpec(memory_space=pl.ANY)


def nn(left, right):
    return lax.dot_general(left, right, (((1,), (0,)), ((), ())), preferred_element_type=F32)


def nt(left, right):
    return lax.dot_general(left, right, (((1,), (1,)), ((), ())), preferred_element_type=F32)


def tn(left, right):
    return lax.dot_general(left, right, (((0,), (0,)), ((), ())), preferred_element_type=F32)


def row_mean(array):
    return jnp.sum(array, -1, keepdims=True) * (1.0 / array.shape[-1])


def col_sum(array):
    return jnp.sum(array, 0, keepdims=True)


def norm(resid):
    center = resid - row_mean(resid)
    inverse = lax.rsqrt(row_mean(center * center) + EPS)
    return center * inverse, inverse


def norm_grad(grad, scaled, inverse, gain):
    weighted = grad * gain
    return inverse * (weighted - row_mean(weighted) - scaled * row_mean(weighted * scaled))


def kernel_call(body, outs, ins, scratch=()):
    return pl.pallas_call(
        body,
        out_shape=[jax.ShapeDtypeStruct(shape, kind) for shape, kind, _ in outs],
        in_specs=[spec for _, spec in ins],
        out_specs=[spec for _, _, spec in outs],
        scratch_shapes=list(scratch),
        compiler_params=pltpu.CompilerParams(vmem_limit_bytes=60 * 2**20),
    )(*[array for array, _ in ins])


def stack_blocks(blocks):
    count, (_, rows, width) = len(blocks), blocks[0].shape

    def body(*refs):
        out, sems = refs[count], refs[count + 1]
        copies = [
            pltpu.make_async_copy(refs[index].at[0], out.at[index], sems.at[index])
            for index in range(count)
        ]
        for copy in copies:
            copy.start()
        for copy in copies:
            copy.wait()

    return kernel_call(
        body,
        [((count, rows, width), BF, ANY_SPEC)],
        [(block, VMEM_SPEC) for block in blocks],
        [pltpu.SemaphoreType.DMA((count,))],
    )[0]


def turn(dims, core_bit):
    (x, _), _, _, (y, _) = dims
    return (x, y) if core_bit else (y, x)


def swap_turn(array, dims, which, count):
    core = dims[1][0]
    return lax.ppermute(
        array,
        AXES,
        [(device, device ^ turn(dims, device // core % 2)[which]) for device in range(count)],
    )


def gather_pieces(shard, shape):
    count = shape["gx"] * shape["gy"]
    dims = exchange_dims(shape)
    _, (core, _), (z, nz), _ = dims

    blocks = [shard[None]]
    for step in range(1, nz):
        blocks.append(swap(blocks[0], z * step, count))
    held = stack_blocks(blocks)
    near = swap_turn(held, dims, 0, count)
    second = swap_turn(held, dims, 1, count)
    far = swap_turn(near, dims, 1, count)
    pieces = [held, near, second, far]
    for index in range(4):
        pieces.append(swap(pieces[index], core, count))
    return pieces


def offsets_of(me, dims):
    (x, _), (core, _), _, (y, _) = dims
    odd = me // core % 2
    first = jnp.where(odd == 1, x, y)
    second = jnp.where(odd == 1, y, x)
    return [0, first, second, x ^ y, core, core ^ second, core ^ first, core ^ x ^ y]


def fetch_blocks(me, dims, refs, place, sems):
    z, nz = dims[2]
    copies = []
    for offset, ref in zip(offsets_of(me, dims), refs):
        for index in range(nz):
            device = me ^ (offset ^ (z * index))
            for source, target in place(ref.at[index], device):
                copies.append(pltpu.make_async_copy(source, target, sems.at[len(copies)]))
    return copies


def send_blocks(me, dims, source, keep, send, sems, base):
    _, (core, _), (z, nz), _ = dims
    count = 4 * nz
    waits = []
    for device in range(2 * count):
        top, low = turn(dims, device // core % 2)
        away = me ^ device
        slot = (away // top % 2) * 2 * nz + (away // low % 2) * nz + away // z % nz
        far = away // core % 2
        sem = sems.at[base + device]

        @pl.when(far == 0)
        def _():
            pltpu.make_async_copy(source(device), keep.at[slot], sem).start()

        @pl.when(far == 1)
        def _():
            pltpu.make_async_copy(source(device), send.at[slot], sem).start()

        waits.append(pltpu.make_async_copy(source(device), keep.at[slot], sem))
    return waits


def added(terms, start, stop):
    total = terms[0][start:stop].astype(F32)
    for term in terms[1:]:
        total = total + term[start:stop].astype(F32)
    return total


def reduce_part(keep, send, dims, count):
    _, (core, _), (z, nz), _ = dims

    terms = [keep, swap(send, core, count)]
    for which in range(2):
        half = terms[0].shape[0] // 2 if which == 0 else nz
        got = swap_turn(added(terms, half, 2 * half).astype(BF), dims, which, count)
        terms.append(got)
        terms = [term[:half] for term in terms]
    result = added(terms, 0, 1)[0]
    for step in range(1, nz):
        got = swap(added(terms, step, step + 1)[0].astype(BF), z * step, count)
        result = result + got.astype(F32)
    return result


def vector_rows(read, width, segment, count):
    rows = []
    for row in range(segment * count // width):
        at, stop, parts = row * width, (row + 1) * width, []
        while at < stop:
            device, start = at // segment, at % segment
            take = min(segment - start, stop - at)
            parts.append(read(device, start, start + take))
            at += take
        rows.append(parts[0] if len(parts) == 1 else jnp.concatenate(parts, 1))
    return rows


def project(me, length, text_in, layout_in, pieces, sizes, dims):
    count, text_rows, layout_rows, text_vec, layout_vec = sizes
    rows = text_in.shape[0]
    packed = pieces[0].shape[1]

    def body(*refs):
        me_ref, length_ref, x_ref, xl_ref = refs[:4]
        piece_refs = refs[4 : 4 + len(pieces)]
        (
            q_ref,
            k_ref,
            v_ref,
            weight_out,
            layout_ref,
            up_ref,
            down_ref,
            text_vec_ref,
            layout_vec_ref,
            weight,
            tail,
            sems,
            out_sem,
        ) = refs[4 + len(pieces) :]
        mine = me_ref[0]

        def place(source, device):
            base = pl.multiple_of(device * text_rows, 16)
            return [
                (source.at[0:text_rows], weight.at[pl.ds(base, text_rows)]),
                (source.at[text_rows:packed], tail.at[device]),
            ]

        copies = fetch_blocks(mine, dims, piece_refs, place, sems)
        for copy in copies:
            copy.start()
        for copy in copies:
            copy.wait()
        out_copy = pltpu.make_async_copy(weight, weight_out, out_sem)
        out_copy.start()
        side = D // 3
        for device in range(count):
            block = pl.ds(device * layout_rows, layout_rows)
            for index, ref in enumerate((layout_ref, up_ref, down_ref)):
                ref[block, :] = tail[device, 0:layout_rows, side * index : side * index + DL]

        def read_text(device, start, stop):
            return tail[device, layout_rows : layout_rows + 1, start:stop].astype(F32)

        def read_layout(device, start, stop):
            return read_text(device, text_vec + start, text_vec + stop)

        for index, row in enumerate(vector_rows(read_text, D, text_vec, count)):
            text_vec_ref[index] = row
        for index, row in enumerate(vector_rows(read_layout, DL, layout_vec, count)):
            layout_vec_ref[index] = row
        x, xl = x_ref[...], xl_ref[...]
        seen = lax.broadcasted_iota(jnp.int32, (rows, CAT - MASK_LANE), 0) < length_ref[0]
        lane = lax.broadcasted_iota(jnp.int32, (rows, CAT - MASK_LANE), 1)
        ones = jnp.where(lane == 0, 1.0, 0.0).astype(BF)
        hidden = jnp.where((lane == 0) & jnp.logical_not(seen), NEG, 0.0).astype(BF)
        nothing = jnp.zeros((rows, CAT - MASK_LANE), BF)
        for index, (ref, extra) in enumerate(((q_ref, ones), (k_ref, hidden), (v_ref, nothing))):
            text = nn(x, weight[index * D : (index + 1) * D, :])
            layout = nn(xl, layout_ref[index * DL : (index + 1) * DL, :])
            if index != 1:
                text = text + text_vec_ref[index // 2]
                layout = layout + layout_vec_ref[index // 2]
            text, layout = text.astype(BF), layout.astype(BF)
            if index == 0:
                text = text * (1.0 / math.sqrt(TEXT_LANES))
                layout = layout * (1.0 / math.sqrt(LAYOUT_LANES))
            for head in range(HEADS):
                ref[head] = jnp.concatenate(
                    [
                        text[:, TEXT_LANES * head : TEXT_LANES * (head + 1)],
                        layout[:, LAYOUT_LANES * head : LAYOUT_LANES * (head + 1)],
                        extra,
                    ],
                    1,
                )
        out_copy.wait()

    cat = ((HEADS, rows, CAT), BF, VMEM_SPEC)
    return kernel_call(
        body,
        [
            cat,
            cat,
            cat,
            ((4 * D, D), BF, ANY_SPEC),
            ((4 * DL, DL), BF, VMEM_SPEC),
            ((FFL, DL), BF, VMEM_SPEC),
            ((FFL, DL), BF, VMEM_SPEC),
            ((12, 1, D), F32, VMEM_SPEC),
            ((12, 1, DL), F32, VMEM_SPEC),
        ],
        [(me, SMEM_SPEC), (length, SMEM_SPEC), (text_in, VMEM_SPEC), (layout_in, VMEM_SPEC)]
        + [(array, ANY_SPEC) for array in pieces],
        [
            pltpu.VMEM((4 * D, D), BF),
            pltpu.VMEM((count, packed - text_rows, D), BF),
            pltpu.SemaphoreType.DMA((2 * count,)),
            pltpu.SemaphoreType.DMA,
        ],
    )


def heads_out(ref):
    heads = range(ref.shape[0])
    text = jnp.concatenate([ref[head, :, 0:TEXT_LANES] for head in heads], 1)
    layout = jnp.concatenate([ref[head, :, TEXT_LANES:MASK_LANE] for head in heads], 1)
    return text, layout


def attend(text_in, layout_in, query, keys, values, weight, layout_w, text_vec, layout_vec):
    rows = text_in.shape[0]

    def body(
        x_ref,
        xl_ref,
        q_ref,
        k_ref,
        v_ref,
        weight_any,
        layout_ref,
        tv_ref,
        lv_ref,
        out_t,
        out_l,
        lse_ref,
        norm_t,
        inv_t,
        norm_l,
        inv_l,
        mixed,
        weight,
        sem,
    ):
        fetch = pltpu.make_async_copy(weight_any.at[3 * D : 4 * D], weight, sem)
        fetch.start()

        def head_step(head, carry):
            scores = nt(k_ref[head], q_ref[head])
            top = jnp.max(scores, 0, keepdims=True)
            expo = jnp.exp(scores - top)
            total = col_sum(expo)
            probs = (expo * (1.0 / total)).astype(BF)
            mixed[head] = tn(v_ref[head], probs).T.astype(BF)
            lse_ref[head] = top + jnp.log(total)
            return carry

        lax.fori_loop(0, HEADS, head_step, 0)
        text, layout = heads_out(mixed)
        out_t[...] = text
        out_l[...] = layout
        fetch.wait()
        after = nn(text, weight[...]) + tv_ref[2]
        norm_t[...], inv_t[...] = norm(x_ref[...].astype(F32) + after)
        after = nn(layout, layout_ref[3 * DL : 4 * DL, :]) + lv_ref[2]
        norm_l[...], inv_l[...] = norm(xl_ref[...].astype(F32) + after)

    return kernel_call(
        body,
        [
            ((rows, D), BF, VMEM_SPEC),
            ((rows, DL), BF, VMEM_SPEC),
            ((HEADS, 1, rows), F32, VMEM_SPEC),
            ((rows, D), F32, VMEM_SPEC),
            ((rows, 1), F32, VMEM_SPEC),
            ((rows, DL), F32, VMEM_SPEC),
            ((rows, 1), F32, VMEM_SPEC),
        ],
        [
            (text_in, VMEM_SPEC),
            (layout_in, VMEM_SPEC),
            (query, VMEM_SPEC),
            (keys, VMEM_SPEC),
            (values, VMEM_SPEC),
            (weight, ANY_SPEC),
            (layout_w, VMEM_SPEC),
            (text_vec, VMEM_SPEC),
            (layout_vec, VMEM_SPEC),
        ],
        [pltpu.VMEM((HEADS, rows, CAT), BF), pltpu.VMEM((D, D), BF), pltpu.SemaphoreType.DMA],
    )


def erf_of(value):
    value = jnp.clip(value, -4.0, 4.0)
    square = value * value
    top = jnp.full_like(square, -2.72614225801306e-10)
    for factor in (
        2.77068142495902e-08,
        -2.10102402082508e-06,
        -5.69250639462346e-05,
        -7.34990630326855e-04,
        -2.95459980854025e-03,
        -1.60960333262415e-02,
    ):
        top = top * square + factor
    low = jnp.full_like(square, -1.45660718464996e-05)
    for factor in (
        -2.13374055278905e-04,
        -1.68282697438203e-03,
        -7.37332916720468e-03,
        -1.42647390514189e-02,
    ):
        low = low * square + factor
    return value * top / low


def gelu_both(value):
    below = 0.5 * (1.0 + erf_of(value * math.sqrt(0.5)))
    density = jnp.exp(value * value * -0.5) * (1.0 / math.sqrt(2.0 * math.pi))
    return value * below, below + value * density


def feed_stream(norm_ref, vec_ref, cot_ref, keep, up, down, hidden, slope, blocks, write, outs):
    out_ref, grad_ref, vec_out = outs
    first = norm_ref[...] * vec_ref[3] + vec_ref[4]
    low = first.astype(BF)

    def forward(block, total):
        upper = nt(low, up(block)) + vec_ref[8 + block]
        act, rise = gelu_both(upper)
        act = act.astype(BF)
        hidden[block] = act
        slope[block] = rise
        return total + nn(act, down(block))

    branch = lax.fori_loop(0, blocks, forward, jnp.zeros_like(first))
    scaled, inverse = norm(first + branch + vec_ref[5])
    out_ref[...] = (scaled * vec_ref[6] + vec_ref[7]).astype(BF)
    cotan = cot_ref[...].astype(F32) * keep
    vec_out[1] = col_sum(cotan * scaled)
    vec_out[2] = col_sum(cotan)
    second = norm_grad(cotan, scaled, inverse, vec_ref[6])
    branch_low = second.astype(BF)
    vec_out[0] = col_sum(branch_low.astype(F32))

    def backward(block, total):
        act_grad = nt(branch_low, down(block))
        upper_low = (act_grad * slope[block]).astype(BF)
        vec_out[3 + block] = col_sum(upper_low.astype(F32))
        write(block, tn(upper_low, low), tn(hidden[block], branch_low))
        return total + nn(upper_low, up(block))

    grad_ref[...] = lax.fori_loop(0, blocks, backward, second)


def feed(me, keep_rows, norm_t, norm_l, tv, lv, cot_t, cot_l, pieces, lu, ld, dims, text_rows):
    rows = norm_t.shape[0]
    count = 8 * dims[2][1]
    blocks = FF // D

    def body(*refs):
        me_ref, keep_ref, nt_ref, nl_ref, tv_ref, lv_ref, ct_ref, cl_ref, lu_ref, ld_ref = refs[:10]
        piece_refs = refs[10 : 10 + len(pieces)]
        (
            out_t,
            out_l,
            grad_t,
            grad_l,
            vec_t,
            vec_l,
            lu_grad,
            ld_grad,
            both_keep,
            both_send,
            up,
            down,
            hidden,
            slope,
            hidden_l,
            slope_l,
            grads,
            sems,
        ) = refs[10 + len(pieces) :]
        mine = me_ref[0]

        def place(source, device):
            at = pl.ds(pl.multiple_of(device * text_rows, 16), text_rows)
            return [
                (source.at[0:text_rows], up.at[at]),
                (source.at[text_rows : 2 * text_rows], down.at[at]),
            ]

        copies = fetch_blocks(mine, dims, piece_refs, place, sems)
        for copy in copies:
            copy.start()
        keep = keep_ref[...]

        def rows_of(ref, size):
            return lambda block: ref[pl.ds(pl.multiple_of(block * size, 8), size), :]

        def write_l(block, one, two):
            at = pl.ds(pl.multiple_of(block * DL, 8), DL)
            lu_grad[at, :] = one.astype(BF)
            ld_grad[at, :] = two.astype(BF)

        feed_stream(
            nl_ref,
            lv_ref,
            cl_ref,
            keep,
            rows_of(lu_ref, DL),
            rows_of(ld_ref, DL),
            hidden_l,
            slope_l,
            FFL // DL,
            write_l,
            (out_l, grad_l, vec_l),
        )
        for copy in copies:
            copy.wait()

        per_block = D // text_rows

        def write_t(block, one, two):
            for part in range(per_block):
                at = slice(part * text_rows, (part + 1) * text_rows)
                grads[block * per_block + part, 0:text_rows] = one[at].astype(BF)
                grads[block * per_block + part, text_rows:] = two[at].astype(BF)

        feed_stream(
            nt_ref,
            tv_ref,
            ct_ref,
            keep,
            rows_of(up, D),
            rows_of(down, D),
            hidden,
            slope,
            blocks,
            write_t,
            (out_t, grad_t, vec_t),
        )
        waits = send_blocks(
            mine, dims, lambda device: grads.at[device], both_keep, both_send, sems, 0
        )
        for wait in waits:
            wait.wait()

    part = ((count // 2, 2 * text_rows, D), BF, ANY_SPEC)
    return kernel_call(
        body,
        [
            ((rows, D), BF, VMEM_SPEC),
            ((rows, DL), BF, VMEM_SPEC),
            ((rows, D), F32, VMEM_SPEC),
            ((rows, DL), F32, VMEM_SPEC),
            ((3 + blocks, 1, D), F32, VMEM_SPEC),
            ((3 + blocks, 1, DL), F32, VMEM_SPEC),
            ((FFL, DL), BF, VMEM_SPEC),
            ((FFL, DL), BF, VMEM_SPEC),
            part,
            part,
        ],
        [
            (me, SMEM_SPEC),
            (keep_rows, VMEM_SPEC),
            (norm_t, VMEM_SPEC),
            (norm_l, VMEM_SPEC),
            (tv, VMEM_SPEC),
            (lv, VMEM_SPEC),
            (cot_t, VMEM_SPEC),
            (cot_l, VMEM_SPEC),
            (lu, VMEM_SPEC),
            (ld, VMEM_SPEC),
        ]
        + [(array, ANY_SPEC) for array in pieces],
        [
            pltpu.VMEM((FF, D), BF),
            pltpu.VMEM((FF, D), BF),
            pltpu.VMEM((blocks, rows, D), BF),
            pltpu.VMEM((blocks, rows, D), F32),
            pltpu.VMEM((FFL // DL, rows, DL), BF),
            pltpu.VMEM((FFL // DL, rows, DL), F32),
            pltpu.VMEM((count, 2 * text_rows, D), BF),
            pltpu.SemaphoreType.DMA((2 * count,)),
        ],
    )


def close_back_pair(grad_t, grad_l, norms, outs, weight, layout_w, tv, lv):
    rows = grad_t.shape[0]
    norm_t, inv_t, norm_l, inv_l = norms
    out_t, out_l = outs

    def body(
        gt_ref,
        gl_ref,
        nt_ref,
        it_ref,
        nl_ref,
        il_ref,
        ot_ref,
        ol_ref,
        weight_any,
        layout_ref,
        tv_ref,
        lv_ref,
        resid_t,
        resid_l,
        out_wt,
        out_wl,
        vec_t,
        vec_l,
        dout,
        weight,
        sem,
    ):
        fetch = pltpu.make_async_copy(weight_any.at[3 * D : 4 * D], weight, sem)
        fetch.start()

        def close(grad, scaled, inverse, vec, mixed, vec_out, resid_ref, wide):
            vec_out[1] = col_sum(grad * scaled)
            vec_out[2] = col_sum(grad)
            resid = norm_grad(grad, scaled, inverse, vec[3])
            resid_ref[...] = resid
            after = resid.astype(BF)
            vec_out[0] = col_sum(after.astype(F32))
            return after, tn(mixed, after).astype(BF), nt(after, wide()).astype(BF)

        def wide_l():
            return layout_ref[3 * DL : 4 * DL, :]

        def wide_t():
            fetch.wait()
            return weight[...]

        _, out_wl[...], att_l = close(
            gl_ref[...], nl_ref[...], il_ref[...], lv_ref, ol_ref[...], vec_l, resid_l, wide_l
        )
        _, out_wt[...], att_t = close(
            gt_ref[...], nt_ref[...], it_ref[...], tv_ref, ot_ref[...], vec_t, resid_t, wide_t
        )
        nothing = jnp.zeros((rows, CAT - MASK_LANE), BF)
        for head in range(HEADS):
            dout[head] = jnp.concatenate(
                [
                    att_t[:, TEXT_LANES * head : TEXT_LANES * (head + 1)],
                    att_l[:, LAYOUT_LANES * head : LAYOUT_LANES * (head + 1)],
                    nothing,
                ],
                1,
            )

    return kernel_call(
        body,
        [
            ((rows, D), F32, VMEM_SPEC),
            ((rows, DL), F32, VMEM_SPEC),
            ((D, D), BF, VMEM_SPEC),
            ((DL, DL), BF, VMEM_SPEC),
            ((3, 1, D), F32, VMEM_SPEC),
            ((3, 1, DL), F32, VMEM_SPEC),
            ((HEADS, rows, CAT), BF, VMEM_SPEC),
        ],
        [
            (grad_t, VMEM_SPEC),
            (grad_l, VMEM_SPEC),
            (norm_t, VMEM_SPEC),
            (inv_t, VMEM_SPEC),
            (norm_l, VMEM_SPEC),
            (inv_l, VMEM_SPEC),
            (out_t, VMEM_SPEC),
            (out_l, VMEM_SPEC),
            (weight, ANY_SPEC),
            (layout_w, VMEM_SPEC),
            (tv, VMEM_SPEC),
            (lv, VMEM_SPEC),
        ],
        [pltpu.VMEM((D, D), BF), pltpu.SemaphoreType.DMA],
    )


def heads_back(query, keys, values, lse, dout, start, stop):
    rows = query.shape[1]
    size = stop - start

    def body(q_any, k_any, v_any, lse_any, do_any, dq, dk, dv, q_ref, k_ref, v_ref, do_ref, lse_ref, sems):
        copies = [
            pltpu.make_async_copy(source.at[start:stop], target, sems.at[index])
            for index, (source, target) in enumerate(
                (
                    (q_any, q_ref),
                    (k_any, k_ref),
                    (v_any, v_ref),
                    (do_any, do_ref),
                    (lse_any, lse_ref),
                )
            )
        ]
        for copy in copies:
            copy.start()
        for copy in copies:
            copy.wait()
        is_text = lax.broadcasted_iota(jnp.int32, (rows, CAT), 1) < TEXT_LANES
        text_row = lax.broadcasted_iota(jnp.int32, (CAT, rows), 0) < TEXT_LANES

        def head_step(head, carry):
            q, k, v, do = q_ref[head], k_ref[head], v_ref[head], do_ref[head]
            probs = jnp.exp(nt(k, q) - lse_ref[head])
            dv[head] = nn(probs.astype(BF), do).astype(BF)
            none = jnp.zeros_like(v)
            mixed = nt(jnp.where(is_text, v, none), do)
            score_t = (probs * (mixed - col_sum(probs * mixed))).astype(BF)
            mixed = nt(jnp.where(is_text, none, v), do)
            score_l = (probs * (mixed - col_sum(probs * mixed))).astype(BF)
            dk_t = nn(score_t, q)
            dk_l = nn(score_l, q)
            dk[head] = jnp.where(is_text, dk_t, dk_t + dk_l).astype(BF)
            dq_t = tn(k, score_t)
            dq_l = tn(k, score_l)
            scaled = jnp.where(
                text_row,
                dq_t * (1.0 / math.sqrt(TEXT_LANES)),
                (dq_t + dq_l) * (1.0 / math.sqrt(LAYOUT_LANES)),
            )
            dq[head] = scaled.T.astype(BF)
            return carry

        lax.fori_loop(0, size, head_step, 0)

    cat = pltpu.VMEM((size, rows, CAT), BF)
    part = ((size, rows, CAT), BF, VMEM_SPEC)
    return kernel_call(
        body,
        [part, part, part],
        [(array, ANY_SPEC) for array in (query, keys, values, lse, dout)],
        [cat, cat, cat, cat, pltpu.VMEM((size, 1, rows), F32), pltpu.SemaphoreType.DMA((5,))],
    )


def weight_grads(me, text_in, layout_in, backs, out_w, ffn_l, vecs, dims, sizes):
    count, text_rows, layout_rows, text_vec, layout_vec = sizes
    rows = text_in.shape[0]
    packed = text_rows + layout_rows + 8
    groups = len(backs)

    def body(*refs):
        me_ref, x_ref, xl_ref = refs[:3]
        back_refs = refs[3 : 3 + 3 * groups]
        (
            out_wt,
            out_wl,
            lu_grad,
            ld_grad,
            close_t,
            close_l,
            feed_t,
            feed_l,
            joined_t,
            joined_l,
            keep,
            send,
            pack,
            att_l,
            sems,
        ) = refs[3 + 3 * groups :]
        mine = me_ref[0]
        x, xl = x_ref[...], xl_ref[...]
        side = D // 3
        for device in range(count):
            pack[device, text_rows : text_rows + layout_rows, :] = jnp.zeros((layout_rows, D), BF)
        per_block = D // text_rows
        for index in range(3):
            pieces = [heads_out(back_refs[3 * group + index]) for group in range(groups)]
            joined_t[index] = jnp.concatenate([text for text, _ in pieces], 1)
            joined_l[index] = jnp.concatenate([layout for _, layout in pieces], 1)
            grad = tn(x, joined_t[index]).astype(BF)
            for part in range(per_block):
                pack[index * per_block + part, 0:text_rows, :] = grad[
                    part * text_rows : (part + 1) * text_rows
                ]
            att_l[index * DL : (index + 1) * DL, :] = tn(xl, joined_l[index]).astype(BF)
        for part in range(per_block):
            pack[3 * per_block + part, 0:text_rows, :] = out_wt[
                part * text_rows : (part + 1) * text_rows, :
            ]
        att_l[3 * DL : 4 * DL, :] = out_wl[...]
        for device in range(count):
            block = pl.ds(device * layout_rows, layout_rows)
            for index, ref in enumerate((att_l, lu_grad, ld_grad)):
                pack[
                    device,
                    text_rows : text_rows + layout_rows,
                    side * index : side * index + DL,
                ] = ref[block, :]

        def vector(joined, close, feeds):
            rows_of = [col_sum(joined[0].astype(F32)), col_sum(joined[2].astype(F32))]
            rows_of += [close[0], close[1], close[2], feeds[0], feeds[1], feeds[2]]
            return rows_of + [feeds[3 + block] for block in range(FF // D)]

        text_rows_of = vector(joined_t, close_t, feed_t)
        layout_rows_of = vector(joined_l, close_l, feed_l)

        def segment(all_rows, width, start, size):
            parts, stop = [], start + size
            while start < stop:
                row, at = start // width, start % width
                take = min(width - at, stop - start)
                parts.append(all_rows[row][:, at : at + take])
                start += take
            return parts

        row = lax.broadcasted_iota(jnp.int32, (8, D), 0)
        for device in range(count):
            parts = segment(text_rows_of, D, device * text_vec, text_vec)
            parts += segment(layout_rows_of, DL, device * layout_vec, layout_vec)
            parts.append(jnp.zeros((1, D - text_vec - layout_vec), F32))
            line = jnp.concatenate(parts, 1)
            pack[device, text_rows + layout_rows :, :] = jnp.where(
                row == 0, jnp.broadcast_to(line, (8, D)), 0.0
            ).astype(BF)
        waits = send_blocks(mine, dims, lambda device: pack.at[device], keep, send, sems, 0)
        for wait in waits:
            wait.wait()

    part = ((count // 2, packed, D), BF, ANY_SPEC)
    arrays = [text_in, layout_in]
    for back in backs:
        arrays += list(back)
    arrays += [*out_w, *ffn_l, *vecs]
    return kernel_call(
        body,
        [((3, rows, D), BF, VMEM_SPEC), ((3, rows, DL), BF, VMEM_SPEC), part, part],
        [(me, SMEM_SPEC)] + [(array, VMEM_SPEC) for array in arrays],
        [
            pltpu.VMEM((count, packed, D), BF),
            pltpu.VMEM((4 * DL, DL), BF),
            pltpu.SemaphoreType.DMA((count,)),
        ],
    )


def input_grads(joined_t, joined_l, resid_t, resid_l, weight, layout_w):
    rows = resid_t.shape[0]

    def body(jt, jl, rt, rl, weight_any, layout_ref, grad_t, grad_l, weight, sem):
        fetch = pltpu.make_async_copy(weight_any.at[0 : 3 * D], weight, sem)
        fetch.start()
        total = rl[...]
        for index in range(3):
            total = total + nt(jl[index], layout_ref[index * DL : (index + 1) * DL, :])
        grad_l[...] = total.astype(BF)
        fetch.wait()
        total = rt[...]
        for index in range(3):
            total = total + nt(jt[index], weight[index * D : (index + 1) * D, :])
        grad_t[...] = total.astype(BF)

    return kernel_call(
        body,
        [((rows, D), BF, VMEM_SPEC), ((rows, DL), BF, VMEM_SPEC)],
        [(array, VMEM_SPEC) for array in (joined_t, joined_l, resid_t, resid_l)]
        + [(weight, ANY_SPEC), (layout_w, VMEM_SPEC)],
        [pltpu.VMEM((3 * D, D), BF), pltpu.SemaphoreType.DMA],
    )


def shards_fast(
    shape,
    text_in,
    layout_in,
    lengths,
    dup_rows,
    text_attention,
    text_up,
    text_down,
    text_vector,
    layout_attention,
    layout_up,
    layout_down,
    layout_vector,
    text_cotangent,
    layout_cotangent,
):
    count = shape["gx"] * shape["gy"]
    dims = exchange_dims(shape)
    me = flat_index(shape["gy"]).reshape(1).astype(jnp.int32)
    text_rows, layout_rows = text_attention.shape[0], layout_attention.shape[0]
    text_vec, layout_vec = text_vector.shape[0], layout_vector.shape[0]
    packed = pack_rows(
        text_attention,
        [layout_attention, layout_up.T, layout_down],
        jnp.concatenate([text_vector, layout_vector]),
    ).astype(BF)
    sizes = (count, text_rows, layout_rows, text_vec, layout_vec)
    parts = gather_pieces(packed, shape)
    feed_shard = jnp.concatenate([text_up.T, text_down], 0).astype(BF)
    feed_parts = gather_pieces(feed_shard, shape)
    q, k, v, weight, layout_w, lu, ld, tv, lv = project(
        me, lengths, text_in, layout_in, parts, sizes, dims
    )
    out_t, out_l, lse, norm_t, inv_t, norm_l, inv_l = attend(
        text_in, layout_in, q, k, v, weight, layout_w, tv, lv
    )
    span = text_in.shape[0]
    keep = (jnp.arange(span) < lengths[0]) & (dup_rows == 0)
    keep = keep.astype(F32)[:, None]
    (
        text_final,
        layout_final,
        grad_t,
        grad_l,
        feed_vt,
        feed_vl,
        lu_grad,
        ld_grad,
        both_keep,
        both_send,
    ) = feed(
        me,
        keep,
        norm_t,
        norm_l,
        tv,
        lv,
        text_cotangent,
        layout_cotangent,
        feed_parts,
        lu,
        ld,
        dims,
        text_rows,
    )
    resid_t, resid_l, out_wt, out_wl, close_t, close_l, dout = close_back_pair(
        grad_t, grad_l, (norm_t, inv_t, norm_l, inv_l), (out_t, out_l), weight, layout_w, tv, lv
    )
    middle = HEADS // 2
    backs = [
        heads_back(q, k, v, lse, dout, 0, middle), heads_back(q, k, v, lse, dout, middle, HEADS)
    ]
    joined_t, joined_l, keep_packed, send_packed = weight_grads(
        me,
        text_in,
        layout_in,
        backs,
        (out_wt, out_wl),
        (lu_grad, ld_grad),
        (close_t, close_l, feed_vt, feed_vl),
        dims,
        sizes,
    )
    text_input_grad, layout_input_grad = input_grads(
        joined_t, joined_l, resid_t, resid_l, weight, layout_w
    )
    both_sum = reduce_part(both_keep, both_send, dims, count)
    up_sum, down_sum = both_sum[:text_rows], both_sum[text_rows:]
    packed_sum = reduce_part(keep_packed, send_packed, dims, count)
    text_sum, layout_sums, text_vec_sum, layout_vec_sum = unpack_rows(
        packed_sum, text_rows, layout_rows, text_vec, layout_vec
    )
    return (
        text_final,
        layout_final,
        text_input_grad,
        layout_input_grad,
        text_sum,
        up_sum.T,
        down_sum,
        text_vec_sum,
        layout_sums[0],
        layout_sums[1].T,
        layout_sums[2],
        layout_vec_sum,
    )


def fits(shape):
    (_, nx), (_, ncore), (_, nz), (_, ny) = exchange_dims(shape)
    count = shape["gx"] * shape["gy"]
    return (
        (nx, ncore, ny) == (2, 2, 2)
        and (4 * D) % (16 * count) == 0
        and (4 * DL) % (8 * count) == 0
        and D % (4 * D // count) == 0
    )


def layer(fast, shape, *arrays):
    if not fast or arrays[2].shape[0] != 1:
        return shards(shape, *arrays)
    return shards_fast(shape, *arrays)


def solution(mesh):
    placed = (
        P(("gx", "gy"), None),
        P(("gx", "gy"), None),
        P(("gx", "gy")),
        P(("gx", "gy")),
        P(("gx", "gy"), None),
        P(None, ("gx", "gy")),
        P(("gx", "gy"), None),
        P(("gx", "gy")),
        P(("gx", "gy"), None),
        P(None, ("gx", "gy")),
        P(("gx", "gy"), None),
        P(("gx", "gy")),
        P(("gx", "gy"), None),
        P(("gx", "gy"), None),
    )
    shape = dict(mesh.shape)
    fast = fits(shape)
    return jax.shard_map(
        functools.partial(layer, fast, shape),
        mesh=mesh,
        in_specs=placed,
        out_specs=(
            P(("gx", "gy"), None),
            P(("gx", "gy"), None),
            P(("gx", "gy"), None),
            P(("gx", "gy"), None),
            P(("gx", "gy"), None),
            P(None, ("gx", "gy")),
            P(("gx", "gy"), None),
            P(("gx", "gy")),
            P(("gx", "gy"), None),
            P(None, ("gx", "gy")),
            P(("gx", "gy"), None),
            P(("gx", "gy")),
        ),
        check_vma=False,
    )
```

profile of v0, /device:TPU:0, one launch (start us, length us, event | category | flops | bytes accessed | tf_op | source)
XLA Modules:
  0.0 347.4 jit_solution(7921518362004555643)
XLA Ops:
  0.7 1.0 convert_bitcast_fusion.1
  1.7 1.0 convert_bitcast_fusion
  2.8 5.1 %collective-permute-start.12 = (bf16[1,192,768]{2,1,0:T(8,128)(2,1)S(1)}, bf16[1,192,768]{2,1,0:T(8,128)(2,1)S(1)}, u32[]{:S(2)}, u32[]{:S(2)}) collective-permute-start(bf16[1,192,768]{2,1,0:T(8,128)(2,1)S(1)} %pad_maximum_fusion.refs_0_), channel_id=1, source_target_pairs={{0,6},{1,7},{2,4},{3,5},{4,2},{5,3},{6,0},{7,1},{8,14},{9,15},{10,... | collective-permute-start | bytes 884744 | tf_op jit(solution)/shard_map/ppermute | solution.py:42
  7.9 0.6 collective-permute-start.10
  8.6 7.4 %collective-permute-done.12.refs_3_ = bf16[1,192,768]{2,1,0:T(8,128)(2,1)S(1)} collective-permute-done((bf16[1,192,768]{2,1,0:T(8,128)(2,1)S(1)}, bf16[1,192,768]{2,1,0:T(8,128)(2,1)S(1)}, u32[]{:S(2)}, u32[]{:S(2)}) %collective-permute-start.12) | collective-permute-done | bytes 294944 | tf_op jit(solution)/shard_map/ppermute | solution.py:42
  15.9 17.1 %collective-permute-done.11.refs_2_ = bf16[1,192,768]{2,1,0:T(8,128)(2,1)S(1)} collective-permute-done((bf16[1,192,768]{2,1,0:T(8,128)(2,1)S(1)}, bf16[1,192,768]{2,1,0:T(8,128)(2,1)S(1)}, u32[]{:S(2)}, u32[]{:S(2)}) %collective-permute-start.11) | collective-permute-done | bytes 294944 | tf_op jit(solution)/shard_map/ppermute | solution.py:42
  33.1 0.7 copy-done.17
  33.8 0.7 copy-done.18
  34.5 2.3 shard_map.232.refs_10_
  36.8 1.6 collective-permute-start.13
  38.6 2.5 collective-permute-start.2
  41.2 1.9 collective-permute-start
  43.1 5.3 %collective-permute-done.2.refs_3_ = bf16[1,128,768]{2,1,0:T(8,128)(2,1)S(1)} collective-permute-done((bf16[1,128,768]{2,1,0:T(8,128)(2,1)S(1)}, bf16[1,128,768]{2,1,0:T(8,128)(2,1)S(1)}, u32[]{:S(2)}, u32[]{:S(2)}) %collective-permute-start.2) | collective-permute-done | bytes 196640 | tf_op jit(solution)/shard_map/ppermute | solution.py:42
  48.4 7.8 %collective-permute-done.1.refs_2_ = bf16[1,128,768]{2,1,0:T(8,128)(2,1)S(1)} collective-permute-done((bf16[1,128,768]{2,1,0:T(8,128)(2,1)S(1)}, bf16[1,128,768]{2,1,0:T(8,128)(2,1)S(1)}, u32[]{:S(2)}, u32[]{:S(2)}) %collective-permute-start.1) | collective-permute-done | bytes 196640 | tf_op jit(solution)/shard_map/ppermute | solution.py:42
  56.2 0.7 copy-done.22
  56.8 0.7 copy-done.23
  57.5 2.1 shard_map.229.refs_4_
  59.6 1.1 collective-permute-start.4
  60.8 0.9 collective-permute-start.3
  61.7 1.4 collective-permute-start.14
  63.1 0.7 collective-permute-start.15
  63.7 15.6 %collective-permute-done.4.refs_6_ = bf16[4,128,768]{2,1,0:T(8,128)(2,1)S(1)} collective-permute-done((bf16[4,128,768]{2,1,0:T(8,128)(2,1)}, bf16[4,128,768]{2,1,0:T(8,128)(2,1)S(1)}, u32[]{:S(2)}, u32[]{:S(2)}) %collective-permute-start.4) | collective-permute-done | bytes 786464 | tf_op jit(solution)/shard_map/ppermute | solution.py:628
  79.3 2.1 collective-permute-done.3.refs_5_
  81.4 1.0 collective-permute-start.5
  82.4 9.5 %collective-permute-done.14.refs_12_ = bf16[4,192,768]{2,1,0:T(8,128)(2,1)S(1)} collective-permute-done((bf16[4,192,768]{2,1,0:T(8,128)(2,1)S(1)}, bf16[4,192,768]{2,1,0:T(8,128)(2,1)S(1)}, u32[]{:S(2)}, u32[]{:S(2)}) %collective-permute-start.14) | collective-permute-done | bytes 1179680 | tf_op jit(solution)/shard_map/ppermute | solution.py:628
  92.5 12.1 %collective-permute-done.15.refs_13_ = bf16[4,192,768]{2,1,0:T(8,128)(2,1)} collective-permute-done((bf16[4,192,768]{2,1,0:T(8,128)(2,1)S(1)}, bf16[4,192,768]{2,1,0:T(8,128)(2,1)}, u32[]{:S(2)}, u32[]{:S(2)}) %collective-permute-start.15) | collective-permute-done | bytes 1179680 | tf_op jit(solution)/shard_map/ppermute | solution.py:628
  104.7 8.4 %collective-permute-done.5.refs_7_ = bf16[4,128,768]{2,1,0:T(8,128)(2,1)} collective-permute-done((bf16[4,128,768]{2,1,0:T(8,128)(2,1)S(1)}, bf16[4,128,768]{2,1,0:T(8,128)(2,1)}, u32[]{:S(2)}, u32[]{:S(2)}) %collective-permute-start.5) | collective-permute-done | bytes 786464 | tf_op jit(solution)/shard_map/ppermute | solution.py:628
  113.8 0.9 copy.34.refs_1_
  114.6 1.8 copy.33.refs_3_.xl_ref.refs_2_
  116.4 1.8 copy.35.refs_7_
  118.2 9.9 %shard_map.230 = (bf16[12,512,128]{2,1,0:T(8,128)(2,1)}, bf16[12,512,128]{2,1,0:T(8,128)(2,1)}, bf16[12,512,128]{2,1,0:T(8,128)(2,1)}, bf16[3072,768]{1,0:T(8,12...) custom-call(s32[1]{0:T(128)} %bitcast.refs_0_, ...), custom_call_target="tpu_custom_call" | custom-call | tf_op jit(solution)/shard_map/pallas_call | solution.py:589
  128.1 15.8 %shard_map.231 = (bf16[512,768]{1,0:T(8,128)(2,1)}, bf16[512,192]{1,0:T(8,128)(2,1)}, f32[12,1,512]{2,1,0:T(1,128)}, f32[512,768]{1,0:T(8,128)}, f32[512,1]{1,0:...) custom-call(bf16[512,768]{1,0:T(8,128)(2,1)} %refs_1_.2, bf16[512,192]{1,0:T(8,128)(2,1)} %copy.33.refs_3_.xl_ref.refs_2_, ...), custom_call_target="tpu_custom_call" | custom-call | tf_op jit(solution)/shard_map/pallas_call | solution.py:589
  144.0 43.5 %shard_map.233 = (bf16[512,768]{1,0:T(8,128)(2,1)}, bf16[512,192]{1,0:T(8,128)(2,1)}, f32[512,768]{1,0:T(8,128)}, f32[512,192]{1,0:T(8,128)}, f32[7,1,768]{2,1,0...) custom-call(s32[1]{0:T(128)} %bitcast.refs_0_, ...), custom_call_target="tpu_custom_call" | custom-call | tf_op jit(solution)/shard_map/pallas_call | solution.py:589
  187.5 0.7 collective-permute-start.26
  188.2 7.4 %shard_map.234 = (f32[512,768]{1,0:T(8,128)}, f32[512,192]{1,0:T(8,128)}, bf16[768,768]{1,0:T(8,128)(2,1)}, bf16[192,192]{1,0:T(8,128)(2,1)}, f32[3,1,768]{2,1,0...) custom-call(f32[512,768]{1,0:T(8,128)} %get-tuple-element.71.gt_ref, ...), custom_call_target="tpu_custom_call" | custom-call | tf_op jit(solution)/shard_map/pallas_call | solution.py:589
  195.7 12.2 %shard_map.236 = (bf16[6,512,128]{2,1,0:T(8,128)(2,1)}, bf16[6,512,128]{2,1,0:T(8,128)(2,1)}, bf16[6,512,128]{2,1,0:T(8,128)(2,1)}) custom-call(bf16[12,512,128]{2,1,0:T(8,128)(2,1)} %get-tuple-element.57.q_ref.q_any, bf16[12,512,128]{2,1,0:T(8,128)(2,1)} %get-tuple-element.58.k_ref.k_any, bf16[12,512,128]{2,1,0:T(8,128)(2,1)} %get-tuple-element.59.v_ref.v_any, ...), custom_call_target="tpu_custom_call" | custom-call | tf_op jit(solution)/shard_map/pallas_call | solution.py:589
  207.9 12.2 %shard_map.235 = (bf16[6,512,128]{2,1,0:T(8,128)(2,1)}, bf16[6,512,128]{2,1,0:T(8,128)(2,1)}, bf16[6,512,128]{2,1,0:T(8,128)(2,1)}) custom-call(bf16[12,512,128]{2,1,0:T(8,128)(2,1)} %get-tuple-element.57.q_ref.q_any, bf16[12,512,128]{2,1,0:T(8,128)(2,1)} %get-tuple-element.58.k_ref.k_any, bf16[12,512,128]{2,1,0:T(8,128)(2,1)} %get-tuple-element.59.v_ref.v_any, ...), custom_call_target="tpu_custom_call" | custom-call | tf_op jit(solution)/shard_map/pallas_call | solution.py:589
  220.1 10.7 %shard_map.237 = (bf16[3,512,768]{2,1,0:T(8,128)(2,1)}, bf16[3,512,192]{2,1,0:T(8,128)(2,1)}, bf16[16,128,768]{2,1,0:T(8,128)(2,1)}, bf16[16,128,768]{2,1,0:T(8,128)(2,1)}) custom-call(s32[1]{0:T(128)} %bitcast.refs_0_, bf16[512,768]{1,0:T(8,128)(2,1)} %refs_1_.2, bf16[512,192]{1,0:T(8,128)(2,1)} %copy.33.refs_3_.xl_ref.refs_2_, ...), custom_call_target="tpu_custom_call" | custom-call | tf_op jit(solution)/shard_map/pallas_call | solution.py:589
  230.9 3.1 add_convert_fusion
  234.5 2.2 collective-permute-done.20
  237.6 42.2 %collective-permute-done.21 = bf16[8,128,768]{2,1,0:T(8,128)(2,1)S(1)} collective-permute-done((bf16[8,128,768]{2,1,0:T(8,128)(2,1)S(1)}, bf16[8,128,768]{2,1,0:T(8,128)(2,1)S(1)}, u32[]{:S(2)}, u32[]{:S(2)}) %collective-permute-start.21) | collective-permute-done | bytes 1572896 | tf_op jit(solution)/shard_map/ppermute | solution.py:628
  280.6 3.9 %add_convert_fusion.2 = bf16[4,192,768]{2,1,0:T(8,128)(2,1)} fusion(bf16[8,192,768]{2,1,0:T(8,128)(2,1)S(1)} %collective-permute-done.27, bf16[16,192,768]{2,1,0:T(8,128)(2,1)} %collective-permute-done.26, bf16[16,192,768]{2,1,0:T(8,128)(2,1)} %get-tuple-element.100), kind=kLoop, calls=%fused_computation.2 | loop fusion | flops 3538944 | bytes 4718592 | tf_op jit(solution)/shard_map/convert_element_type | solution.py:708
  284.6 1.6 collective-permute-start.28
  286.1 6.0 %collective-permute-done.22 = bf16[4,128,768]{2,1,0:T(8,128)(2,1)S(1)} collective-permute-done((bf16[4,128,768]{2,1,0:T(8,128)(2,1)S(1)}, bf16[4,128,768]{2,1,0:T(8,128)(2,1)S(1)}, u32[]{:S(2)}, u32[]{:S(2)}) %collective-permute-start.22) | collective-permute-done | bytes 786464 | tf_op jit(solution)/shard_map/ppermute | solution.py:628
  292.1 1.2 fusion.19
  293.3 2.2 collective-permute-start.25
  295.6 1.3 collective-permute-start.24
  296.8 0.8 copy.37
  297.6 7.7 %shard_map.238 = (bf16[512,768]{1,0:T(8,128)(2,1)}, bf16[512,192]{1,0:T(8,128)(2,1)}) custom-call(bf16[3,512,768]{2,1,0:T(8,128)(2,1)} %get-tuple-element.92.jt, bf16[3,512,192]{2,1,0:T(8,128)(2,1)} %get-tuple-element.93.jl, f32[512,768]{1,0:T(8,128)} %get-tuple-element.94.rt, f32[512,192]{1,0:T(8,128)} %get-tuple-element.95.rl, ...), custom_call_target="tpu_custom_call" | custom-call | tf_op jit(solution)/shard_map/pallas_call | solution.py:589
  305.3 1.8 copy.38
  307.1 5.9 %collective-permute-done.24 = bf16[128,768]{1,0:T(8,128)(2,1)} collective-permute-done((bf16[128,768]{1,0:T(8,128)(2,1)}, bf16[128,768]{1,0:T(8,128)(2,1)}, u32[]{:S(2)}, u32[]{:S(2)}) %collective-permute-start.24) | collective-permute-done | bytes 196640 | tf_op jit(solution)/shard_map/ppermute | solution.py:42
  313.0 1.5 fusion.3
  314.5 0.7 slice.272
  315.2 0.6 slice_bitcast_fusion.2
  315.8 2.1 fusion.12
  318.0 2.3 collective-permute-start.31
  320.4 1.1 collective-permute-start.30
  321.5 0.6 slice_reduce_fusion
  322.1 0.6 fusion.30
  322.7 8.3 %collective-permute-done.29 = bf16[192,768]{1,0:T(8,128)(2,1)S(1)} collective-permute-done((bf16[192,768]{1,0:T(8,128)(2,1)S(1)}, bf16[192,768]{1,0:T(8,128)(2,1)S(1)}, u32[]{:S(2)}, u32[]{:S(2)}) %collective-permute-start.29) | collective-permute-done | bytes 294944 | tf_op jit(solution)/shard_map/ppermute | solution.py:42
  331.1 3.5 %collective-permute-done.31 = bf16[192,768]{1,0:T(8,128)(2,1)S(1)} collective-permute-done((bf16[192,768]{1,0:T(8,128)(2,1)S(1)}, bf16[192,768]{1,0:T(8,128)(2,1)S(1)}, u32[]{:S(2)}, u32[]{:S(2)}) %collective-permute-start.31) | collective-permute-done | bytes 294944 | tf_op jit(solution)/shard_map/ppermute | solution.py:42
  334.6 10.6 %collective-permute-done.30 = bf16[192,768]{1,0:T(8,128)(2,1)S(1)} collective-permute-done((bf16[192,768]{1,0:T(8,128)(2,1)S(1)}, bf16[192,768]{1,0:T(8,128)(2,1)S(1)}, u32[]{:S(2)}, u32[]{:S(2)}) %collective-permute-start.30) | collective-permute-done | bytes 294944 | tf_op jit(solution)/shard_map/ppermute | solution.py:42
  345.1 1.4 fusion.1
  346.5 0.8 fusion.29
  (102 shorter events, 3.4 us)
Async XLA Ops:
  0.6 37.7 %copy-start.29 = (f32[72]{0:T(128)S(1)}, f32[72]{0:T(128)}, u32[]{:S(2)}) copy-start(f32[72]{0:T(128)} %param.25) | copy-start | bytes 868
  0.7 37.7 %copy-start.27 = (f32[288]{0:T(512)S(1)}, f32[288]{0:T(512)}, u32[]{:S(2)}) copy-start(f32[288]{0:T(512)} %param.21) | copy-start | bytes 3460
  0.7 37.8 %copy-start.24 = (f32[24,192]{1,0:T(8,128)S(1)}, f32[24,192]{1,0:T(8,128)}, u32[]{:S(2)}) copy-start(f32[24,192]{1,0:T(8,128)} %param.22) | copy-start | bytes 55300
  0.7 37.8 %copy-start.25 = (f32[24,192]{1,0:T(8,128)S(1)}, f32[24,192]{1,0:T(8,128)}, u32[]{:S(2)}) copy-start(f32[24,192]{1,0:T(8,128)} %param.24) | copy-start | bytes 55300
  0.7 37.8 %copy-start.19 = (f32[96,768]{1,0:T(8,128)S(1)}, f32[96,768]{1,0:T(8,128)}, u32[]{:S(2)}) copy-start(f32[96,768]{1,0:T(8,128)} %param.18) | copy-start | bytes 884740
  0.7 37.9 %copy-start.26 = (f32[192,24]{0,1:T(8,128)S(1)}, f32[192,24]{0,1:T(8,128)}, u32[]{:S(2)}) copy-start(f32[192,24]{0,1:T(8,128)} %param.23) | copy-start | bytes 55300
  2.7 30.3 %copy-start.6 = (bf16[1,192,768]{2,1,0:T(8,128)(2,1)}, bf16[1,192,768]{2,1,0:T(8,128)(2,1)S(1)}, u32[]{:S(2)}) copy-start(bf16[1,192,768]{2,1,0:T(8,128)(2,1)S(1)} %pad_maximum_fusion.refs_0_) | copy-start | bytes 884740
  2.8 111.0 %copy-start.28 = (s32[512]{0:T(512)S(1)}, s32[512]{0:T(512)}, u32[]{:S(2)}) copy-start(s32[512]{0:T(512)} %param.17) | copy-start | bytes 6148
  2.8 13.1 %collective-permute-start.12 = (bf16[1,192,768]{2,1,0:T(8,128)(2,1)S(1)}, bf16[1,192,768]{2,1,0:T(8,128)(2,1)S(1)}, u32[]{:S(2)}, u32[]{:S(2)}) collective-permute-start(bf16[1,192,768]{2,1,0:T(8,128)(2,1)S(1)} %pad_maximum_fusion.refs_0_), channel_id=1, source_target_pairs={{0,6},{1,7},{2,4},{3,5},{4,2},{5,3},{6,0},{7,1},{8,14},{9,15},{10,... | collective-permute-start | bytes 884744 | tf_op jit(solution)/shard_map/ppermute | solution.py:42
  7.9 25.1 %collective-permute-start.11 = (bf16[1,192,768]{2,1,0:T(8,128)(2,1)S(1)}, bf16[1,192,768]{2,1,0:T(8,128)(2,1)S(1)}, u32[]{:S(2)}, u32[]{:S(2)}) collective-permute-start(bf16[1,192,768]{2,1,0:T(8,128)(2,1)S(1)} %pad_maximum_fusion.refs_0_), channel_id=1, source_target_pairs={{0,4},{1,5},{2,6},{3,7},{4,0},{5,1},{6,2},{7,3},{8,12},{9,13},{10,... | collective-permute-start | bytes 884744 | tf_op jit(solution)/shard_map/ppermute | solution.py:42
  7.9 25.1 %collective-permute-start.10 = (bf16[1,192,768]{2,1,0:T(8,128)(2,1)S(1)}, bf16[1,192,768]{2,1,0:T(8,128)(2,1)S(1)}, u32[]{:S(2)}, u32[]{:S(2)}) collective-permute-start(bf16[1,192,768]{2,1,0:T(8,128)(2,1)S(1)} %pad_maximum_fusion.refs_0_), channel_id=1, source_target_pairs={{0,2},{1,3},{2,0},{3,1},{4,6},{5,7},{6,4},{7,5},{8,10},{9,11},{10,... | collective-permute-start | bytes 884744 | tf_op jit(solution)/shard_map/ppermute | solution.py:42
  15.9 17.1 %copy-start.16 = (bf16[1,192,768]{2,1,0:T(8,128)(2,1)}, bf16[1,192,768]{2,1,0:T(8,128)(2,1)S(1)}, u32[]{:S(2)}) copy-start(bf16[1,192,768]{2,1,0:T(8,128)(2,1)S(1)} %collective-permute-done.12.refs_3_) | copy-start | bytes 884740
  33.0 0.7 copy-start.17
  33.7 0.7 copy-start.18
  36.8 24.9 %copy-start = (bf16[4,192,768]{2,1,0:T(8,128)(2,1)S(1)}, bf16[4,192,768]{2,1,0:T(8,128)(2,1)}, u32[]{:S(2)}) copy-start(bf16[4,192,768]{2,1,0:T(8,128)(2,1)} %shard_map.232.refs_10_) | copy-start | bytes 3538948
  36.8 26.3 %collective-permute-start.13 = (bf16[4,192,768]{2,1,0:T(8,128)(2,1)}, bf16[4,192,768]{2,1,0:T(8,128)(2,1)S(1)}, u32[]{:S(2)}, u32[]{:S(2)}) collective-permute-start(bf16[4,192,768]{2,1,0:T(8,128)(2,1)} %shard_map.232.refs_10_), channel_id=1, source_target_pairs={{0,1},{1,0},{2,3},{3,2},{4,5},{5,4},{6,7},{7,6},{8,24},{9,25},{10,... | collective-permute-start | bytes 3538952 | tf_op jit(solution)/shard_map/ppermute | solution.py:628
  38.6 17.5 %copy-start.9 = (bf16[1,128,768]{2,1,0:T(8,128)(2,1)}, bf16[1,128,768]{2,1,0:T(8,128)(2,1)S(1)}, u32[]{:S(2)}) copy-start(bf16[1,128,768]{2,1,0:T(8,128)(2,1)S(1)} %pad_bitcast_fusion.refs_0_) | copy-start | bytes 589828
  38.6 9.7 %collective-permute-start.2 = (bf16[1,128,768]{2,1,0:T(8,128)(2,1)S(1)}, bf16[1,128,768]{2,1,0:T(8,128)(2,1)S(1)}, u32[]{:S(2)}, u32[]{:S(2)}) collective-permute-start(bf16[1,128,768]{2,1,0:T(8,128)(2,1)S(1)} %pad_bitcast_fusion.refs_0_), channel_id=1, source_target_pairs={{0,6},{1,7},{2,4},{3,5},{4,2},{5,3},{6,0},{7,1},{8,14},{9,15},{10,... | collective-permute-start | bytes 589832 | tf_op jit(solution)/shard_map/ppermute | solution.py:42
  41.2 15.0 %collective-permute-start.1 = (bf16[1,128,768]{2,1,0:T(8,128)(2,1)S(1)}, bf16[1,128,768]{2,1,0:T(8,128)(2,1)S(1)}, u32[]{:S(2)}, u32[]{:S(2)}) collective-permute-start(bf16[1,128,768]{2,1,0:T(8,128)(2,1)S(1)} %pad_bitcast_fusion.refs_0_), channel_id=1, source_target_pairs={{0,4},{1,5},{2,6},{3,7},{4,0},{5,1},{6,2},{7,3},{8,12},{9,13},{10,... | collective-permute-start | bytes 589832 | tf_op jit(solution)/shard_map/ppermute | solution.py:42
  41.2 15.0 %collective-permute-start = (bf16[1,128,768]{2,1,0:T(8,128)(2,1)S(1)}, bf16[1,128,768]{2,1,0:T(8,128)(2,1)S(1)}, u32[]{:S(2)}, u32[]{:S(2)}) collective-permute-start(bf16[1,128,768]{2,1,0:T(8,128)(2,1)S(1)} %pad_bitcast_fusion.refs_0_), channel_id=1, source_target_pairs={{0,2},{1,3},{2,0},{3,1},{4,6},{5,7},{6,4},{7,5},{8,10},{9,11},{10,... | collective-permute-start | bytes 589832 | tf_op jit(solution)/shard_map/ppermute | solution.py:42
  48.4 7.8 %copy-start.21 = (bf16[1,128,768]{2,1,0:T(8,128)(2,1)}, bf16[1,128,768]{2,1,0:T(8,128)(2,1)S(1)}, u32[]{:S(2)}) copy-start(bf16[1,128,768]{2,1,0:T(8,128)(2,1)S(1)} %collective-permute-done.2.refs_3_) | copy-start | bytes 589828
  56.1 0.7 copy-start.22
  56.8 0.7 copy-start.23
  59.6 19.7 %collective-permute-start.4 = (bf16[4,128,768]{2,1,0:T(8,128)(2,1)}, bf16[4,128,768]{2,1,0:T(8,128)(2,1)S(1)}, u32[]{:S(2)}, u32[]{:S(2)}) collective-permute-start(bf16[4,128,768]{2,1,0:T(8,128)(2,1)} %shard_map.229.refs_4_), channel_id=1, source_target_pairs={{0,16},{1,17},{2,18},{3,19},{4,20},{5,21},{6,22},{7,23},{8,9},{9,8... | collective-permute-start | bytes 2359304 | tf_op jit(solution)/shard_map/ppermute | solution.py:628
  60.8 20.6 %collective-permute-start.3 = (bf16[4,128,768]{2,1,0:T(8,128)(2,1)}, bf16[4,128,768]{2,1,0:T(8,128)(2,1)S(1)}, u32[]{:S(2)}, u32[]{:S(2)}) collective-permute-start(bf16[4,128,768]{2,1,0:T(8,128)(2,1)} %shard_map.229.refs_4_), channel_id=1, source_target_pairs={{0,1},{1,0},{2,3},{3,2},{4,5},{5,4},{6,7},{7,6},{8,24},{9,25},{10,... | collective-permute-start | bytes 2359304 | tf_op jit(solution)/shard_map/ppermute | solution.py:628
  61.7 19.7 %collective-permute-start.6 = (bf16[4,128,768]{2,1,0:T(8,128)(2,1)}, bf16[4,128,768]{2,1,0:T(8,128)(2,1)S(1)}, u32[]{:S(2)}, u32[]{:S(2)}) collective-permute-start(bf16[4,128,768]{2,1,0:T(8,128)(2,1)} %shard_map.229.refs_4_), channel_id=1, source_target_pairs={{0,8},{1,9},{2,10},{3,11},{4,12},{5,13},{6,14},{7,15},{8,0},{9,1},... | collective-permute-start | bytes 2359304 | tf_op jit(solution)/shard_map/ppermute | solution.py:42
  61.7 30.2 %collective-permute-start.14 = (bf16[4,192,768]{2,1,0:T(8,128)(2,1)S(1)}, bf16[4,192,768]{2,1,0:T(8,128)(2,1)S(1)}, u32[]{:S(2)}, u32[]{:S(2)}) collective-permute-start(bf16[4,192,768]{2,1,0:T(8,128)(2,1)S(1)} %copy-done), channel_id=1, source_target_pairs={{0,16},{1,17},{2,18},{3,19},{4,20},{5,21},{6,22},{7,23},{8,9},{9,8... | collective-permute-start | bytes 3538952 | tf_op jit(solution)/shard_map/ppermute | solution.py:628
  63.1 65.0 %copy-start.7 = (bf16[4,192,768]{2,1,0:T(8,128)(2,1)}, bf16[4,192,768]{2,1,0:T(8,128)(2,1)S(1)}, u32[]{:S(2)}) copy-start(bf16[4,192,768]{2,1,0:T(8,128)(2,1)S(1)} %collective-permute-done.13.refs_11_) | copy-start | bytes 3538948
  63.1 41.6 %collective-permute-start.15 = (bf16[4,192,768]{2,1,0:T(8,128)(2,1)S(1)}, bf16[4,192,768]{2,1,0:T(8,128)(2,1)}, u32[]{:S(2)}, u32[]{:S(2)}) collective-permute-start(bf16[4,192,768]{2,1,0:T(8,128)(2,1)S(1)} %collective-permute-done.13.refs_11_), channel_id=1, source_target_pairs={{0,16},{1,17},{2,18},{3,19},{4,20},{5,21},{6,22},{7,23},{8,9},{9,8... | collective-permute-start | bytes 3538952 | tf_op jit(solution)/shard_map/ppermute | solution.py:628
  79.3 25.4 %copy-start.11 = (bf16[4,128,768]{2,1,0:T(8,128)(2,1)}, bf16[4,128,768]{2,1,0:T(8,128)(2,1)S(1)}, u32[]{:S(2)}) copy-start(bf16[4,128,768]{2,1,0:T(8,128)(2,1)S(1)} %collective-permute-done.4.refs_6_) | copy-start | bytes 2359300
  79.3 12.6 %collective-permute-start.8 = (bf16[4,128,768]{2,1,0:T(8,128)(2,1)S(1)}, bf16[4,128,768]{2,1,0:T(8,128)(2,1)S(1)}, u32[]{:S(2)}, u32[]{:S(2)}) collective-permute-start(bf16[4,128,768]{2,1,0:T(8,128)(2,1)S(1)} %collective-permute-done.4.refs_6_), channel_id=1, source_target_pairs={{0,8},{1,9},{2,10},{3,11},{4,12},{5,13},{6,14},{7,15},{8,0},{9,1},... | collective-permute-start | bytes 2359304 | tf_op jit(solution)/shard_map/ppermute | solution.py:42
  81.4 23.3 %copy-start.12 = (bf16[4,128,768]{2,1,0:T(8,128)(2,1)}, bf16[4,128,768]{2,1,0:T(8,128)(2,1)S(1)}, u32[]{:S(2)}) copy-start(bf16[4,128,768]{2,1,0:T(8,128)(2,1)S(1)} %collective-permute-done.3.refs_5_) | copy-start | bytes 2359300
  81.4 11.0 %collective-permute-start.7 = (bf16[4,128,768]{2,1,0:T(8,128)(2,1)S(1)}, bf16[4,128,768]{2,1,0:T(8,128)(2,1)S(1)}, u32[]{:S(2)}, u32[]{:S(2)}) collective-permute-start(bf16[4,128,768]{2,1,0:T(8,128)(2,1)S(1)} %collective-permute-done.3.refs_5_), channel_id=1, source_target_pairs={{0,8},{1,9},{2,10},{3,11},{4,12},{5,13},{6,14},{7,15},{8,0},{9,1},... | collective-permute-start | bytes 2359304 | tf_op jit(solution)/shard_map/ppermute | solution.py:42
  81.4 31.7 %copy-start.13 = (bf16[4,128,768]{2,1,0:T(8,128)(2,1)}, bf16[4,128,768]{2,1,0:T(8,128)(2,1)S(1)}, u32[]{:S(2)}) copy-start(bf16[4,128,768]{2,1,0:T(8,128)(2,1)S(1)} %collective-permute-done.6.refs_8_) | copy-start | bytes 2359300
  81.4 31.7 %collective-permute-start.5 = (bf16[4,128,768]{2,1,0:T(8,128)(2,1)S(1)}, bf16[4,128,768]{2,1,0:T(8,128)(2,1)}, u32[]{:S(2)}, u32[]{:S(2)}) collective-permute-start(bf16[4,128,768]{2,1,0:T(8,128)(2,1)S(1)} %collective-permute-done.3.refs_5_), channel_id=1, source_target_pairs={{0,16},{1,17},{2,18},{3,19},{4,20},{5,21},{6,22},{7,23},{8,9},{9,8... | collective-permute-start | bytes 2359304 | tf_op jit(solution)/shard_map/ppermute | solution.py:628
  91.9 36.2 %copy-start.8 = (bf16[4,192,768]{2,1,0:T(8,128)(2,1)}, bf16[4,192,768]{2,1,0:T(8,128)(2,1)S(1)}, u32[]{:S(2)}) copy-start(bf16[4,192,768]{2,1,0:T(8,128)(2,1)S(1)} %collective-permute-done.14.refs_12_) | copy-start | bytes 3538948
  91.9 52.0 %collective-permute-start.16 = (bf16[4,192,768]{2,1,0:T(8,128)(2,1)S(1)}, bf16[4,192,768]{2,1,0:T(8,128)(2,1)}, u32[]{:S(2)}, u32[]{:S(2)}) collective-permute-start(bf16[4,192,768]{2,1,0:T(8,128)(2,1)S(1)} %copy-done), channel_id=1, source_target_pairs={{0,8},{1,9},{2,10},{3,11},{4,12},{5,13},{6,14},{7,15},{8,0},{9,1},... | collective-permute-start | bytes 3538952 | tf_op jit(solution)/shard_map/ppermute | solution.py:42
  91.9 21.2 %copy-start.14 = (bf16[4,128,768]{2,1,0:T(8,128)(2,1)}, bf16[4,128,768]{2,1,0:T(8,128)(2,1)S(1)}, u32[]{:S(2)}) copy-start(bf16[4,128,768]{2,1,0:T(8,128)(2,1)S(1)} %collective-permute-done.8.refs_10_) | copy-start | bytes 2359300
  91.9 52.0 %collective-permute-start.17 = (bf16[4,192,768]{2,1,0:T(8,128)(2,1)S(1)}, bf16[4,192,768]{2,1,0:T(8,128)(2,1)}, u32[]{:S(2)}, u32[]{:S(2)}) collective-permute-start(bf16[4,192,768]{2,1,0:T(8,128)(2,1)S(1)} %collective-permute-done.13.refs_11_), channel_id=1, source_target_pairs={{0,8},{1,9},{2,10},{3,11},{4,12},{5,13},{6,14},{7,15},{8,0},{9,1},... | collective-permute-start | bytes 3538952 | tf_op jit(solution)/shard_map/ppermute | solution.py:42
  92.4 20.7 %copy-start.15 = (bf16[4,128,768]{2,1,0:T(8,128)(2,1)}, bf16[4,128,768]{2,1,0:T(8,128)(2,1)S(1)}, u32[]{:S(2)}) copy-start(bf16[4,128,768]{2,1,0:T(8,128)(2,1)S(1)} %collective-permute-done.7.refs_9_) | copy-start | bytes 2359300
  92.4 51.5 %collective-permute-start.18 = (bf16[4,192,768]{2,1,0:T(8,128)(2,1)S(1)}, bf16[4,192,768]{2,1,0:T(8,128)(2,1)}, u32[]{:S(2)}, u32[]{:S(2)}) collective-permute-start(bf16[4,192,768]{2,1,0:T(8,128)(2,1)S(1)} %collective-permute-done.14.refs_12_), channel_id=1, source_target_pairs={{0,8},{1,9},{2,10},{3,11},{4,12},{5,13},{6,14},{7,15},{8,0},{9,1},... | collective-permute-start | bytes 3538952 | tf_op jit(solution)/shard_map/ppermute | solution.py:42
  104.7 39.3 %collective-permute-start.19 = (bf16[4,192,768]{2,1,0:T(8,128)(2,1)}, bf16[4,192,768]{2,1,0:T(8,128)(2,1)}, u32[]{:S(2)}, u32[]{:S(2)}) collective-permute-start(bf16[4,192,768]{2,1,0:T(8,128)(2,1)} %collective-permute-done.15.refs_13_), channel_id=1, source_target_pairs={{0,8},{1,9},{2,10},{3,11},{4,12},{5,13},{6,14},{7,15},{8,0},{9,1},... | collective-permute-start | bytes 3538952 | tf_op jit(solution)/shard_map/ppermute | solution.py:42
  113.1 5.1 %collective-permute-start.9 = (bf16[4,128,768]{2,1,0:T(8,128)(2,1)}, bf16[4,128,768]{2,1,0:T(8,128)(2,1)}, u32[]{:S(2)}, u32[]{:S(2)}) collective-permute-start(bf16[4,128,768]{2,1,0:T(8,128)(2,1)} %collective-permute-done.5.refs_7_), channel_id=1, source_target_pairs={{0,8},{1,9},{2,10},{3,11},{4,12},{5,13},{6,14},{7,15},{8,0},{9,1},... | collective-permute-start | bytes 2359304 | tf_op jit(solution)/shard_map/ppermute | solution.py:42
  187.5 43.4 %collective-permute-start.26 = (bf16[16,192,768]{2,1,0:T(8,128)(2,1)}, bf16[16,192,768]{2,1,0:T(8,128)(2,1)}, u32[]{:S(2)}, u32[]{:S(2)}) collective-permute-start(bf16[16,192,768]{2,1,0:T(8,128)(2,1)} %get-tuple-element.101), channel_id=1, source_target_pairs={{0,8},{1,9},{2,10},{3,11},{4,12},{5,13},{6,14},{7,15},{8,0},{9,1},... | collective-permute-start | bytes 14155784 | tf_op jit(solution)/shard_map/ppermute | solution.py:42
  230.8 5.9 %collective-permute-start.20 = (bf16[16,128,768]{2,1,0:T(8,128)(2,1)}, bf16[16,128,768]{2,1,0:T(8,128)(2,1)S(1)}, u32[]{:S(2)}, u32[]{:S(2)}) collective-permute-start(bf16[16,128,768]{2,1,0:T(8,128)(2,1)} %get-tuple-element.99), channel_id=1, source_target_pairs={{0,8},{1,9},{2,10},{3,11},{4,12},{5,13},{6,14},{7,15},{8,0},{9,1},... | collective-permute-start | bytes 9437192 | tf_op jit(solution)/shard_map/ppermute | solution.py:42
  230.9 5.8 %copy-start.1 = (bf16[16,128,768]{2,1,0:T(8,128)(2,1)S(1)}, bf16[16,128,768]{2,1,0:T(8,128)(2,1)}, u32[]{:S(2)}) copy-start(bf16[16,128,768]{2,1,0:T(8,128)(2,1)} %get-tuple-element.98) | copy-start | bytes 9437188
  234.0 46.6 %collective-permute-start.27 = (bf16[8,192,768]{2,1,0:T(8,128)(2,1)S(1)}, bf16[8,192,768]{2,1,0:T(8,128)(2,1)S(1)}, u32[]{:S(2)}, u32[]{:S(2)}) collective-permute-start(bf16[8,192,768]{2,1,0:T(8,128)(2,1)S(1)} %add_convert_fusion), channel_id=1, source_target_pairs={{0,1},{1,0},{2,3},{3,2},{4,5},{5,4},{6,7},{7,6},{8,24},{9,25},{10,... | collective-permute-start | bytes 7077896 | tf_op jit(solution)/shard_map/ppermute | solution.py:628
  236.7 55.4 %copy-start.2 = (bf16[16,128,768]{2,1,0:T(8,128)(2,1)}, bf16[16,128,768]{2,1,0:T(8,128)(2,1)S(1)}, u32[]{:S(2)}) copy-start(bf16[16,128,768]{2,1,0:T(8,128)(2,1)S(1)} %collective-permute-done.20) | copy-start | bytes 9437188
  237.1 42.7 %collective-permute-start.21 = (bf16[8,128,768]{2,1,0:T(8,128)(2,1)S(1)}, bf16[8,128,768]{2,1,0:T(8,128)(2,1)S(1)}, u32[]{:S(2)}, u32[]{:S(2)}) collective-permute-start(bf16[8,128,768]{2,1,0:T(8,128)(2,1)S(1)} %add_convert_fusion.1), channel_id=1, source_target_pairs={{0,1},{1,0},{2,3},{3,2},{4,5},{5,4},{6,7},{7,6},{8,24},{9,25},{10,... | collective-permute-start | bytes 4718600 | tf_op jit(solution)/shard_map/ppermute | solution.py:628
  279.8 12.4 %copy-start.5 = (bf16[8,128,768]{2,1,0:T(8,128)(2,1)}, bf16[8,128,768]{2,1,0:T(8,128)(2,1)S(1)}, u32[]{:S(2)}) copy-start(bf16[8,128,768]{2,1,0:T(8,128)(2,1)S(1)} %collective-permute-done.21) | copy-start | bytes 4718596
  280.1 12.1 %collective-permute-start.22 = (bf16[4,128,768]{2,1,0:T(8,128)(2,1)S(1)}, bf16[4,128,768]{2,1,0:T(8,128)(2,1)S(1)}, u32[]{:S(2)}, u32[]{:S(2)}) collective-permute-start(bf16[4,128,768]{2,1,0:T(8,128)(2,1)S(1)} %add_convert_fusion.3), channel_id=1, source_target_pairs={{0,16},{1,17},{2,18},{3,19},{4,20},{5,21},{6,22},{7,23},{8,9},{9,8... | collective-permute-start | bytes 2359304 | tf_op jit(solution)/shard_map/ppermute | solution.py:628
  280.6 3.9 %copy-start.3 = (bf16[8,192,768]{2,1,0:T(8,128)(2,1)}, bf16[8,192,768]{2,1,0:T(8,128)(2,1)S(1)}, u32[]{:S(2)}) copy-start(bf16[8,192,768]{2,1,0:T(8,128)(2,1)S(1)} %collective-permute-done.27) | copy-start | bytes 7077892
  284.6 12.3 %copy-start.20 = (bf16[512,192]{1,0:T(8,128)(2,1)S(1)}, bf16[512,192]{1,0:T(8,128)(2,1)}, u32[]{:S(2)}) copy-start(bf16[512,192]{1,0:T(8,128)(2,1)} %get-tuple-element.115) | copy-start | bytes 589828
  284.6 31.3 %collective-permute-start.28 = (bf16[4,192,768]{2,1,0:T(8,128)(2,1)}, bf16[4,192,768]{2,1,0:T(8,128)(2,1)}, u32[]{:S(2)}, u32[]{:S(2)}) collective-permute-start(bf16[4,192,768]{2,1,0:T(8,128)(2,1)} %add_convert_fusion.2), channel_id=1, source_target_pairs={{0,16},{1,17},{2,18},{3,19},{4,20},{5,21},{6,22},{7,23},{8,9},{9,8... | collective-permute-start | bytes 3538952 | tf_op jit(solution)/shard_map/ppermute | solution.py:628
  292.1 1.2 copy-start.10
  293.3 13.8 %collective-permute-start.23 = (bf16[128,768]{1,0:T(8,128)(2,1)}, bf16[128,768]{1,0:T(8,128)(2,1)}, u32[]{:S(2)}, u32[]{:S(2)}) collective-permute-start(bf16[128,768]{1,0:T(8,128)(2,1)} %get-tuple-element.129), channel_id=1, source_target_pairs={{0,2},{1,3},{2,0},{3,1},{4,6},{5,7},{6,4},{7,5},{8,10},{9,11},{10,... | collective-permute-start | bytes 589832 | tf_op jit(solution)/shard_map/ppermute | solution.py:42
  293.3 13.8 %collective-permute-start.25 = (bf16[128,768]{1,0:T(8,128)(2,1)}, bf16[128,768]{1,0:T(8,128)(2,1)}, u32[]{:S(2)}, u32[]{:S(2)}) collective-permute-start(bf16[128,768]{1,0:T(8,128)(2,1)} %get-tuple-element.130), channel_id=1, source_target_pairs={{0,6},{1,7},{2,4},{3,5},{4,2},{5,3},{6,0},{7,1},{8,14},{9,15},{10,... | collective-permute-start | bytes 589832 | tf_op jit(solution)/shard_map/ppermute | solution.py:42
  295.6 17.4 %collective-permute-start.24 = (bf16[128,768]{1,0:T(8,128)(2,1)}, bf16[128,768]{1,0:T(8,128)(2,1)}, u32[]{:S(2)}, u32[]{:S(2)}) collective-permute-start(bf16[128,768]{1,0:T(8,128)(2,1)} %get-tuple-element.131), channel_id=1, source_target_pairs={{0,4},{1,5},{2,6},{3,7},{4,0},{5,1},{6,2},{7,3},{8,12},{9,13},{10,... | collective-permute-start | bytes 589832 | tf_op jit(solution)/shard_map/ppermute | solution.py:42
  307.1 8.8 %copy-start.4 = (bf16[8,192,768]{2,1,0:T(8,128)(2,1)S(1)}, bf16[8,192,768]{2,1,0:T(8,128)(2,1)}, u32[]{:S(2)}) copy-start(bf16[8,192,768]{2,1,0:T(8,128)(2,1)} %copy-done.3) | copy-start | bytes 7077892
  318.0 13.1 %collective-permute-start.29 = (bf16[192,768]{1,0:T(8,128)(2,1)S(1)}, bf16[192,768]{1,0:T(8,128)(2,1)S(1)}, u32[]{:S(2)}, u32[]{:S(2)}) collective-permute-start(bf16[192,768]{1,0:T(8,128)(2,1)S(1)} %get-tuple-element.126), channel_id=1, source_target_pairs={{0,2},{1,3},{2,0},{3,1},{4,6},{5,7},{6,4},{7,5},{8,10},{9,11},{10,... | collective-permute-start | bytes 884744 | tf_op jit(solution)/shard_map/ppermute | solution.py:42
  318.0 16.5 %collective-permute-start.31 = (bf16[192,768]{1,0:T(8,128)(2,1)S(1)}, bf16[192,768]{1,0:T(8,128)(2,1)S(1)}, u32[]{:S(2)}, u32[]{:S(2)}) collective-permute-start(bf16[192,768]{1,0:T(8,128)(2,1)S(1)} %get-tuple-element.127), channel_id=1, source_target_pairs={{0,6},{1,7},{2,4},{3,5},{4,2},{5,3},{6,0},{7,1},{8,14},{9,15},{10,... | collective-permute-start | bytes 884744 | tf_op jit(solution)/shard_map/ppermute | solution.py:42
  320.4 24.8 %collective-permute-start.30 = (bf16[192,768]{1,0:T(8,128)(2,1)S(1)}, bf16[192,768]{1,0:T(8,128)(2,1)S(1)}, u32[]{:S(2)}, u32[]{:S(2)}) collective-permute-start(bf16[192,768]{1,0:T(8,128)(2,1)S(1)} %get-tuple-element.128), channel_id=1, source_target_pairs={{0,4},{1,5},{2,6},{3,7},{4,0},{5,1},{6,2},{7,3},{8,12},{9,13},{10,... | collective-permute-start | bytes 884744 | tf_op jit(solution)/shard_map/ppermute | solution.py:42
where the time goes:
time: 348 us; the launch traced here: 347 us
  waiting for transfers between devices  164 us (47%)
  Pallas kernels  124 us (36%)
  starting transfers between devices  28.5 us (8%)
  other arithmetic  16.1 us (5%)
  local copies, waits for them, and re-layouts  13.2 us (4%)
    pallas_call x10, Pallas kernels, kernel_call(): pl.pallas_call(body, out_shape=[jax.ShapeDtypeStruct(shape, kind) for sha...  124 us
    ppermute x10, waiting for transfers between devices, swap_turn(): lax.ppermute(array, AXES, [(device, device ^ turn(dims, device // core %...  95.9 us
    ppermute x22, waiting for transfers between devices, swap(): lax.ppermute(array, AXES, [(device, device ^ offset) for device in range(...  68.1 us
    ppermute x22, starting transfers between devices, swap(): lax.ppermute(array, AXES, [(device, device ^ offset) for device in range(...  18.7 us
    ppermute x10, starting transfers between devices, swap_turn(): lax.ppermute(array, AXES, [(device, device ^ turn(dims, device // core %...  9.77 us
    unnamed x64, local copies, waits for them, and re-layouts  8.94 us
    convert_element_type x4, other arithmetic, reduce_part(): got = swap_turn(added(terms, half, 2 * half).astype(BF), dims, which, count)  7.71 us
  transfers between devices with their start and end apart: 32, of which 16 were waited for; matrix products, arithmetic and copies ran while one was open for 6% of the time, Pallas kernels for 22%

commit v1 on v0

--- a/solution.py
+++ b/solution.py
@@ -552,6 +552,7 @@
 VMEM_SPEC = pl.BlockSpec(memory_space=pltpu.VMEM)
 SMEM_SPEC = pl.BlockSpec(memory_space=pltpu.SMEM)
 ANY_SPEC = pl.BlockSpec(memory_space=pl.ANY)
+STAGED = "staged"
 
 
 def nn(left, right):
@@ -585,14 +586,33 @@
     return inverse * (weighted - row_mean(weighted) - scaled * row_mean(weighted * scaled))
 
 
-def kernel_call(body, outs, ins, scratch=()):
+def kernel_call(body, outs, ins, scratch=(), room=60):
+    staged = [index for index, (_, spec) in enumerate(ins) if spec == STAGED]
+
+    def with_copies(*refs):
+        rooms, sems = refs[len(refs) - len(staged) - 1 : -1], refs[-1]
+        given = list(refs[: len(refs) - len(staged) - 1])
+        copies = []
+        for order, (index, target) in enumerate(zip(staged, rooms)):
+            copies.append(pltpu.make_async_copy(given[index], target, sems.at[order]))
+            given[index] = target
+        for copy in copies:
+            copy.start()
+        for copy in copies:
+            copy.wait()
+        body(*given)
+
+    scratch = list(scratch)
+    if staged:
+        scratch += [pltpu.VMEM(ins[index][0].shape, ins[index][0].dtype) for index in staged]
+        scratch.append(pltpu.SemaphoreType.DMA((len(staged),)))
     return pl.pallas_call(
-        body,
+        with_copies if staged else body,
         out_shape=[jax.ShapeDtypeStruct(shape, kind) for shape, kind, _ in outs],
-        in_specs=[spec for _, spec in ins],
+        in_specs=[ANY_SPEC if spec == STAGED else spec for _, spec in ins],
         out_specs=[spec for _, _, spec in outs],
-        scratch_shapes=list(scratch),
-        compiler_params=pltpu.CompilerParams(vmem_limit_bytes=60 * 2**20),
+        scratch_shapes=scratch,
+        compiler_params=pltpu.CompilerParams(vmem_limit_bytes=room * 2**20),
     )(*[array for array, _ in ins])
 
 
@@ -615,6 +635,7 @@
         [((count, rows, width), BF, ANY_SPEC)],
         [(block, VMEM_SPEC) for block in blocks],
         [pltpu.SemaphoreType.DMA((count,))],
+        room=8,
     )[0]
 
 
@@ -632,64 +653,69 @@
     )
 
 
+def spread(held, dims, count):
+    pieces = [held]
+    for source, which in ((0, 0), (0, 1), (1, 1)):
+        pieces.append(swap_turn(pieces[source], dims, which, count))
+    return pieces
+
+
+def gather_own(shard, shape):
+    count = shape["gx"] * shape["gy"]
+    dims = exchange_dims(shape)
+    near = stack_blocks(spread(shard[None], dims, count))
+    return [near, swap(near, dims[1][0], count)]
+
+
 def gather_pieces(shard, shape):
     count = shape["gx"] * shape["gy"]
     dims = exchange_dims(shape)
     _, (core, _), (z, nz), _ = dims
-
-    blocks = [shard[None]]
+    blocks = []
     for step in range(1, nz):
-        blocks.append(swap(blocks[0], z * step, count))
-    held = stack_blocks(blocks)
-    near = swap_turn(held, dims, 0, count)
-    second = swap_turn(held, dims, 1, count)
-    far = swap_turn(near, dims, 1, count)
-    pieces = [held, near, second, far]
+        blocks.append(swap(shard[None], z * step, count))
+    pieces = spread(stack_blocks(blocks), dims, count)
     for index in range(4):
         pieces.append(swap(pieces[index], core, count))
     return pieces
 
 
-def offsets_of(me, dims):
-    (x, _), (core, _), _, (y, _) = dims
+def fetch_blocks(me, dims, refs, place, sems):
+    (x, _), (core, _), (z, nz), (y, _) = dims
     odd = me // core % 2
     first = jnp.where(odd == 1, x, y)
     second = jnp.where(odd == 1, y, x)
-    return [0, first, second, x ^ y, core, core ^ second, core ^ first, core ^ x ^ y]
-
-
-def fetch_blocks(me, dims, refs, place, sems):
-    z, nz = dims[2]
+    mine, partner = [0, first, second, x ^ y], [core, core ^ second, core ^ first, core ^ x ^ y]
+    blocks = []
+    for ref, offsets in zip(refs[:2], (mine, partner)):
+        blocks += [(ref.at[index], offset, True) for index, offset in enumerate(offsets)]
+    for ref, offset in zip(refs[2:], mine + partner):
+        blocks += [(ref.at[step - 1], offset ^ (z * step), False) for step in range(1, nz)]
     copies = []
-    for offset, ref in zip(offsets_of(me, dims), refs):
-        for index in range(nz):
-            device = me ^ (offset ^ (z * index))
-            for source, target in place(ref.at[index], device):
-                copies.append(pltpu.make_async_copy(source, target, sems.at[len(copies)]))
+    for block, offset, own in blocks:
+        for source, target in place(block, me ^ offset, own):
+            copies.append(pltpu.make_async_copy(source, target, sems.at[len(copies)]))
     return copies
 
 
-def send_blocks(me, dims, source, keep, send, sems, base):
-    _, (core, _), (z, nz), _ = dims
-    count = 4 * nz
-    waits = []
-    for device in range(2 * count):
-        top, low = turn(dims, device // core % 2)
-        away = me ^ device
-        slot = (away // top % 2) * 2 * nz + (away // low % 2) * nz + away // z % nz
-        far = away // core % 2
-        sem = sems.at[base + device]
-
-        @pl.when(far == 0)
-        def _():
-            pltpu.make_async_copy(source(device), keep.at[slot], sem).start()
-
-        @pl.when(far == 1)
-        def _():
-            pltpu.make_async_copy(source(device), send.at[slot], sem).start()
-
-        waits.append(pltpu.make_async_copy(source(device), keep.at[slot], sem))
-    return waits
+def send_block(me, dims, device, source, keep, send, sems):
+    (x, _), (core, _), (z, nz), (y, _) = dims
+    odd = device // core % 2
+    away = me ^ device
+    across = [away // stride % 2 for stride in (x, y)]
+    top = odd * across[0] + (1 - odd) * across[1]
+    low = odd * across[1] + (1 - odd) * across[0]
+    slot = top * 2 * nz + low * nz + away // z % nz
+    far = away // core % 2
+    sem = sems.at[device]
+
+    @pl.when(far == 0)
+    def _():
+        pltpu.make_async_copy(source, keep.at[slot], sem).start()
+
+    @pl.when(far == 1)
+    def _():
+        pltpu.make_async_copy(source, send.at[slot], sem).start()
 
 
 def added(terms, start, stop):
@@ -728,45 +754,58 @@
     return rows
 
 
-def project(me, length, text_in, layout_in, pieces, sizes, dims):
+def head_forward(q, k, v):
+    scores = nt(k, q)
+    top = jnp.max(scores, 0, keepdims=True)
+    expo = jnp.exp(scores - top)
+    total = col_sum(expo)
+    probs = (expo * (1.0 / total)).astype(BF)
+    return tn(v, probs).T.astype(BF), top + jnp.log(total)
+
+
+def project(me, length, text_in, layout_in, pieces, sizes, dims, middle):
     count, text_rows, layout_rows, text_vec, layout_vec = sizes
     rows = text_in.shape[0]
-    packed = pieces[0].shape[1]
+    packed = pieces[2].shape[1]
 
     def body(*refs):
         me_ref, length_ref, x_ref, xl_ref = refs[:4]
         piece_refs = refs[4 : 4 + len(pieces)]
         (
-            q_ref,
-            k_ref,
-            v_ref,
+            q_out,
+            k_out,
+            v_out,
             weight_out,
             layout_ref,
             up_ref,
             down_ref,
             text_vec_ref,
             layout_vec_ref,
+            mixed,
+            lse_ref,
+            q_ref,
+            k_ref,
+            v_ref,
             weight,
             tail,
             sems,
-            out_sem,
+            out_sems,
         ) = refs[4 + len(pieces) :]
-        mine = me_ref[0]
-
-        def place(source, device):
+
+        def place(source, device, own):
             base = pl.multiple_of(device * text_rows, 16)
             return [
                 (source.at[0:text_rows], weight.at[pl.ds(base, text_rows)]),
                 (source.at[text_rows:packed], tail.at[device]),
             ]
 
-        copies = fetch_blocks(mine, dims, piece_refs, place, sems)
+        copies = fetch_blocks(me_ref[0], dims, piece_refs, place, sems)
         for copy in copies:
             copy.start()
         for copy in copies:
             copy.wait()
-        out_copy = pltpu.make_async_copy(weight, weight_out, out_sem)
-        out_copy.start()
+        outs = [pltpu.make_async_copy(weight, weight_out, out_sems.at[3])]
+        outs[0].start()
         side = D // 3
         for device in range(count):
             block = pl.ds(device * layout_rows, layout_rows)
@@ -789,7 +828,9 @@
         ones = jnp.where(lane == 0, 1.0, 0.0).astype(BF)
         hidden = jnp.where((lane == 0) & jnp.logical_not(seen), NEG, 0.0).astype(BF)
         nothing = jnp.zeros((rows, CAT - MASK_LANE), BF)
-        for index, (ref, extra) in enumerate(((q_ref, ones), (k_ref, hidden), (v_ref, nothing))):
+        for index, (ref, out, extra) in enumerate(
+            ((q_ref, q_out, ones), (k_ref, k_out, hidden), (v_ref, v_out, nothing))
+        ):
             text = nn(x, weight[index * D : (index + 1) * D, :])
             layout = nn(xl, layout_ref[index * DL : (index + 1) * DL, :])
             if index != 1:
@@ -808,9 +849,19 @@
                     ],
                     1,
                 )
-        out_copy.wait()
-
-    cat = ((HEADS, rows, CAT), BF, VMEM_SPEC)
+            outs.append(pltpu.make_async_copy(ref, out, out_sems.at[index]))
+            outs[-1].start()
+
+        def head_step(head, carry):
+            mixed[head], lse_ref[head] = head_forward(q_ref[head], k_ref[head], v_ref[head])
+            return carry
+
+        lax.fori_loop(0, middle, head_step, 0)
+        for copy in outs:
+            copy.wait()
+
+    cat = ((HEADS, rows, CAT), BF, ANY_SPEC)
+    room = pltpu.VMEM((HEADS, rows, CAT), BF)
     return kernel_call(
         body,
         [
@@ -823,34 +874,42 @@
             ((FFL, DL), BF, VMEM_SPEC),
             ((12, 1, D), F32, VMEM_SPEC),
             ((12, 1, DL), F32, VMEM_SPEC),
+            ((middle, rows, CAT), BF, VMEM_SPEC),
+            ((middle, 1, rows), F32, VMEM_SPEC),
         ],
-        [(me, SMEM_SPEC), (length, SMEM_SPEC), (text_in, VMEM_SPEC), (layout_in, VMEM_SPEC)]
+        [(me, SMEM_SPEC), (length, SMEM_SPEC), (text_in, STAGED), (layout_in, STAGED)]
         + [(array, ANY_SPEC) for array in pieces],
         [
+            room,
+            room,
+            room,
             pltpu.VMEM((4 * D, D), BF),
             pltpu.VMEM((count, packed - text_rows, D), BF),
             pltpu.SemaphoreType.DMA((2 * count,)),
-            pltpu.SemaphoreType.DMA,
+            pltpu.SemaphoreType.DMA((4,)),
         ],
     )
 
 
-def heads_out(ref):
-    heads = range(ref.shape[0])
+def heads_out(ref, start, stop):
+    heads = range(start, stop)
     text = jnp.concatenate([ref[head, :, 0:TEXT_LANES] for head in heads], 1)
     layout = jnp.concatenate([ref[head, :, TEXT_LANES:MASK_LANE] for head in heads], 1)
     return text, layout
 
 
-def attend(text_in, layout_in, query, keys, values, weight, layout_w, text_vec, layout_vec):
+def attend(text_in, layout_in, query, keys, values, first, weight, layout_w, text_vec, layout_vec):
     rows = text_in.shape[0]
+    middle = first.shape[0]
+    late = HEADS - middle
 
     def body(
         x_ref,
         xl_ref,
-        q_ref,
-        k_ref,
-        v_ref,
+        q_any,
+        k_any,
+        v_any,
+        first_ref,
         weight_any,
         layout_ref,
         tv_ref,
@@ -862,103 +921,96 @@
         inv_t,
         norm_l,
         inv_l,
+        q_ref,
+        k_ref,
+        v_ref,
         mixed,
         weight,
-        sem,
+        sems,
     ):
-        fetch = pltpu.make_async_copy(weight_any.at[3 * D : 4 * D], weight, sem)
-        fetch.start()
+        fetches = [
+            pltpu.make_async_copy(source.at[middle:HEADS], target, sems.at[index])
+            for index, (source, target) in enumerate(
+                ((q_any, q_ref), (k_any, k_ref), (v_any, v_ref))
+            )
+        ]
+        fetches.append(pltpu.make_async_copy(weight_any.at[3 * D : 4 * D], weight, sems.at[3]))
+        for fetch in fetches:
+            fetch.start()
+        for fetch in fetches[:3]:
+            fetch.wait()
 
         def head_step(head, carry):
-            scores = nt(k_ref[head], q_ref[head])
-            top = jnp.max(scores, 0, keepdims=True)
-            expo = jnp.exp(scores - top)
-            total = col_sum(expo)
-            probs = (expo * (1.0 / total)).astype(BF)
-            mixed[head] = tn(v_ref[head], probs).T.astype(BF)
-            lse_ref[head] = top + jnp.log(total)
+            mixed[head], lse_ref[head] = head_forward(q_ref[head], k_ref[head], v_ref[head])
             return carry
 
-        lax.fori_loop(0, HEADS, head_step, 0)
-        text, layout = heads_out(mixed)
+        lax.fori_loop(0, late, head_step, 0)
+        parts = [heads_out(first_ref, 0, middle), heads_out(mixed, 0, late)]
+        text = jnp.concatenate([part[0] for part in parts], 1)
+        layout = jnp.concatenate([part[1] for part in parts], 1)
         out_t[...] = text
         out_l[...] = layout
-        fetch.wait()
+        fetches[3].wait()
         after = nn(text, weight[...]) + tv_ref[2]
         norm_t[...], inv_t[...] = norm(x_ref[...].astype(F32) + after)
         after = nn(layout, layout_ref[3 * DL : 4 * DL, :]) + lv_ref[2]
         norm_l[...], inv_l[...] = norm(xl_ref[...].astype(F32) + after)
 
+    room = pltpu.VMEM((late, rows, CAT), BF)
     return kernel_call(
         body,
         [
             ((rows, D), BF, VMEM_SPEC),
             ((rows, DL), BF, VMEM_SPEC),
-            ((HEADS, 1, rows), F32, VMEM_SPEC),
+            ((late, 1, rows), F32, VMEM_SPEC),
             ((rows, D), F32, VMEM_SPEC),
             ((rows, 1), F32, VMEM_SPEC),
             ((rows, DL), F32, VMEM_SPEC),
             ((rows, 1), F32, VMEM_SPEC),
         ],
         [
-            (text_in, VMEM_SPEC),
-            (layout_in, VMEM_SPEC),
-            (query, VMEM_SPEC),
-            (keys, VMEM_SPEC),
-            (values, VMEM_SPEC),
+            (text_in, STAGED),
+            (layout_in, STAGED),
+            (query, ANY_SPEC),
+            (keys, ANY_SPEC),
+            (values, ANY_SPEC),
+            (first, VMEM_SPEC),
             (weight, ANY_SPEC),
             (layout_w, VMEM_SPEC),
             (text_vec, VMEM_SPEC),
             (layout_vec, VMEM_SPEC),
         ],
-        [pltpu.VMEM((HEADS, rows, CAT), BF), pltpu.VMEM((D, D), BF), pltpu.SemaphoreType.DMA],
-    )
-
-
-def erf_of(value):
-    value = jnp.clip(value, -4.0, 4.0)
-    square = value * value
-    top = jnp.full_like(square, -2.72614225801306e-10)
-    for factor in (
-        2.77068142495902e-08,
-        -2.10102402082508e-06,
-        -5.69250639462346e-05,
-        -7.34990630326855e-04,
-        -2.95459980854025e-03,
-        -1.60960333262415e-02,
-    ):
-        top = top * square + factor
-    low = jnp.full_like(square, -1.45660718464996e-05)
-    for factor in (
-        -2.13374055278905e-04,
-        -1.68282697438203e-03,
-        -7.37332916720468e-03,
-        -1.42647390514189e-02,
-    ):
-        low = low * square + factor
-    return value * top / low
+        [room, room, room, room, pltpu.VMEM((D, D), BF), pltpu.SemaphoreType.DMA((4,))],
+    )
 
 
 def gelu_both(value):
-    below = 0.5 * (1.0 + erf_of(value * math.sqrt(0.5)))
-    density = jnp.exp(value * value * -0.5) * (1.0 / math.sqrt(2.0 * math.pi))
-    return value * below, below + value * density
-
-
-def feed_stream(norm_ref, vec_ref, cot_ref, keep, up, down, hidden, slope, blocks, write, outs):
+    bell = jnp.exp2(value * value * (-0.5 / math.log(2.0)))
+    near = 1.0 / (1.0 + jnp.abs(value) * (0.3275911 * math.sqrt(0.5)))
+    tail = jnp.full_like(value, 0.5 * 1.061405429)
+    for factor in (-1.453152027, 1.421413741, -0.284496736, 0.254829592):
+        tail = tail * near + 0.5 * factor
+    tail = tail * near * bell
+    below = jnp.where(value < 0.0, tail, 1.0 - tail)
+    return value * below, below + value * bell * (1.0 / math.sqrt(2.0 * math.pi))
+
+
+def feed_stream(norm_ref, vec_ref, cot_ref, keep, up, down, bias, hidden, slope, blocks, write, outs):
     out_ref, grad_ref, vec_out = outs
     first = norm_ref[...] * vec_ref[3] + vec_ref[4]
     low = first.astype(BF)
 
     def forward(block, total):
-        upper = nt(low, up(block)) + vec_ref[8 + block]
-        act, rise = gelu_both(upper)
+        act, rise = gelu_both(nt(low, up(block)) + bias(block))
         act = act.astype(BF)
         hidden[block] = act
         slope[block] = rise
         return total + nn(act, down(block))
 
-    branch = lax.fori_loop(0, blocks, forward, jnp.zeros_like(first))
+    def loop(body, start):
+        return body(0, start) if blocks == 1 else lax.fori_loop(0, blocks, body, start)
+
+    branch = loop(forward, jnp.zeros_like(first))
     scaled, inverse = norm(first + branch + vec_ref[5])
     out_ref[...] = (scaled * vec_ref[6] + vec_ref[7]).astype(BF)
     cotan = cot_ref[...].astype(F32) * keep
@@ -971,16 +1023,21 @@
     def backward(block, total):
         act_grad = nt(branch_low, down(block))
         upper_low = (act_grad * slope[block]).astype(BF)
-        vec_out[3 + block] = col_sum(upper_low.astype(F32))
-        write(block, tn(upper_low, low), tn(hidden[block], branch_low))
+        write(
+            block,
+            tn(upper_low, low),
+            tn(hidden[block], branch_low),
+            col_sum(upper_low.astype(F32)),
+        )
         return total + nn(upper_low, up(block))
 
-    grad_ref[...] = lax.fori_loop(0, blocks, backward, second)
+    grad_ref[...] = loop(backward, second)
 
 
 def feed(me, keep_rows, norm_t, norm_l, tv, lv, cot_t, cot_l, pieces, lu, ld, dims, text_rows):
     rows = norm_t.shape[0]
     count = 8 * dims[2][1]
+    skip = pieces[0].shape[1] - 2 * text_rows
     blocks = FF // D
 
     def body(*refs):
@@ -1008,11 +1065,12 @@
         ) = refs[10 + len(pieces) :]
         mine = me_ref[0]
 
-        def place(source, device):
+        def place(source, device, own):
             at = pl.ds(pl.multiple_of(device * text_rows, 16), text_rows)
+            base = skip if own else 0
             return [
-                (source.at[0:text_rows], up.at[at]),
-                (source.at[text_rows : 2 * text_rows], down.at[at]),
+                (source.at[base : base + text_rows], up.at[at]),
+                (source.at[base + text_rows : base + 2 * text_rows], down.at[at]),
             ]
 
         copies = fetch_blocks(mine, dims, piece_refs, place, sems)
@@ -1020,56 +1078,64 @@
             copy.start()
         keep = keep_ref[...]
 
-        def rows_of(ref, size):
-            return lambda block: ref[pl.ds(pl.multiple_of(block * size, 8), size), :]
-
-        def write_l(block, one, two):
-            at = pl.ds(pl.multiple_of(block * DL, 8), DL)
-            lu_grad[at, :] = one.astype(BF)
-            ld_grad[at, :] = two.astype(BF)
+        def whole(ref):
+            return lambda block: ref[...]
+
+        parts = FFL // DL
+        bias_l = jnp.concatenate([lv_ref[8 + part] for part in range(parts)], 1)
+
+        def write_l(block, one, two, bias):
+            lu_grad[...] = one.astype(BF)
+            ld_grad[...] = two.astype(BF)
+            for part in range(parts):
+                vec_l[3 + part] = bias[:, part * DL : (part + 1) * DL]
 
         feed_stream(
             nl_ref,
             lv_ref,
             cl_ref,
             keep,
-            rows_of(lu_ref, DL),
-            rows_of(ld_ref, DL),
+            whole(lu_ref),
+            whole(ld_ref),
+            lambda block: bias_l,
             hidden_l,
             slope_l,
-            FFL // DL,
+            1,
             write_l,
             (out_l, grad_l, vec_l),
         )
         for copy in copies:
             copy.wait()
-
         per_block = D // text_rows
 
-        def write_t(block, one, two):
+        def rows_of(ref):
+            return lambda block: ref[pl.ds(pl.multiple_of(block * D, 16), D), :]
+
+        def write_t(block, one, two, bias):
+            vec_t[3 + block] = bias
             for part in range(per_block):
                 at = slice(part * text_rows, (part + 1) * text_rows)
-                grads[block * per_block + part, 0:text_rows] = one[at].astype(BF)
-                grads[block * per_block + part, text_rows:] = two[at].astype(BF)
+                device = block * per_block + part
+                grads[device, 0:text_rows] = one[at].astype(BF)
+                grads[device, text_rows:] = two[at].astype(BF)
+                send_block(mine, dims, device, grads.at[device], both_keep, both_send, sems)
 
         feed_stream(
             nt_ref,
             tv_ref,
             ct_ref,
             keep,
-            rows_of(up, D),
-            rows_of(down, D),
+            rows_of(up),
+            rows_of(down),
+            lambda block: tv_ref[8 + block],
             hidden,
             slope,
             blocks,
             write_t,
             (out_t, grad_t, vec_t),
         )
-        waits = send_blocks(
-            mine, dims, lambda device: grads.at[device], both_keep, both_send, sems, 0
-        )
-        for wait in waits:
-            wait.wait()
+        for device in range(count):
+            pltpu.make_async_copy(grads.at[device], both_keep.at[0], sems.at[device]).wait()
 
     part = ((count // 2, 2 * text_rows, D), BF, ANY_SPEC)
     return kernel_call(
@@ -1088,15 +1154,15 @@
         ],
         [
             (me, SMEM_SPEC),
-            (keep_rows, VMEM_SPEC),
-            (norm_t, VMEM_SPEC),
-            (norm_l, VMEM_SPEC),
+            (keep_rows, STAGED),
+            (norm_t, STAGED),
+            (norm_l, STAGED),
             (tv, VMEM_SPEC),
             (lv, VMEM_SPEC),
-            (cot_t, VMEM_SPEC),
-            (cot_l, VMEM_SPEC),
-            (lu, VMEM_SPEC),
-            (ld, VMEM_SPEC),
+            (cot_t, STAGED),
+            (cot_l, STAGED),
+            (lu, STAGED),
+            (ld, STAGED),
         ]
         + [(array, ANY_SPEC) for array in pieces],
         [
@@ -1104,11 +1170,12 @@
             pltpu.VMEM((FF, D), BF),
             pltpu.VMEM((blocks, rows, D), BF),
             pltpu.VMEM((blocks, rows, D), F32),
-            pltpu.VMEM((FFL // DL, rows, DL), BF),
-            pltpu.VMEM((FFL // DL, rows, DL), F32),
+            pltpu.VMEM((1, rows, FFL), BF),
+            pltpu.VMEM((1, rows, FFL), F32),
             pltpu.VMEM((count, 2 * text_rows, D), BF),
             pltpu.SemaphoreType.DMA((2 * count,)),
         ],
+        room=60,
     )
 
 
@@ -1188,20 +1255,21 @@
             ((HEADS, rows, CAT), BF, VMEM_SPEC),
         ],
         [
-            (grad_t, VMEM_SPEC),
-            (grad_l, VMEM_SPEC),
-            (norm_t, VMEM_SPEC),
-            (inv_t, VMEM_SPEC),
-            (norm_l, VMEM_SPEC),
-            (inv_l, VMEM_SPEC),
-            (out_t, VMEM_SPEC),
-            (out_l, VMEM_SPEC),
+            (grad_t, STAGED),
+            (grad_l, STAGED),
+            (norm_t, STAGED),
+            (inv_t, STAGED),
+            (norm_l, STAGED),
+            (inv_l, STAGED),
+            (out_t, STAGED),
+            (out_l, STAGED),
             (weight, ANY_SPEC),
-            (layout_w, VMEM_SPEC),
+            (layout_w, STAGED),
             (tv, VMEM_SPEC),
             (lv, VMEM_SPEC),
         ],
         [pltpu.VMEM((D, D), BF), pltpu.SemaphoreType.DMA],
+        room=60,
     )
 
 
@@ -1213,15 +1281,10 @@
         copies = [
             pltpu.make_async_copy(source.at[start:stop], target, sems.at[index])
             for index, (source, target) in enumerate(
-                (
-                    (q_any, q_ref),
-                    (k_any, k_ref),
-                    (v_any, v_ref),
-                    (do_any, do_ref),
-                    (lse_any, lse_ref),
-                )
+                ((q_any, q_ref), (k_any, k_ref), (v_any, v_ref), (do_any, do_ref))
             )
         ]
+        copies.append(pltpu.make_async_copy(lse_any, lse_ref, sems.at[4]))
         for copy in copies:
             copy.start()
         for copy in copies:
@@ -1258,8 +1321,9 @@
     return kernel_call(
         body,
         [part, part, part],
-        [(array, ANY_SPEC) for array in (query, keys, values, lse, dout)],
+        [(array, ANY_SPEC) for array in (query, keys, values, lse)] + [(dout, ANY_SPEC)],
         [cat, cat, cat, cat, pltpu.VMEM((size, 1, rows), F32), pltpu.SemaphoreType.DMA((5,))],
+        room=16,
     )
 
 
@@ -1296,7 +1360,7 @@
             pack[device, text_rows : text_rows + layout_rows, :] = jnp.zeros((layout_rows, D), BF)
         per_block = D // text_rows
         for index in range(3):
-            pieces = [heads_out(back_refs[3 * group + index]) for group in range(groups)]
+            pieces = [heads_out(back_refs[3 * group + index], 0, back_refs[3 * group + index].shape[0]) for group in range(groups)]
             joined_t[index] = jnp.concatenate([text for text, _ in pieces], 1)
             joined_l[index] = jnp.concatenate([layout for _, layout in pieces], 1)
             grad = tn(x, joined_t[index]).astype(BF)
@@ -1345,24 +1409,27 @@
             pack[device, text_rows + layout_rows :, :] = jnp.where(
                 row == 0, jnp.broadcast_to(line, (8, D)), 0.0
             ).astype(BF)
-        waits = send_blocks(mine, dims, lambda device: pack.at[device], keep, send, sems, 0)
-        for wait in waits:
-            wait.wait()
+        for device in range(count):
+            send_block(mine, dims, device, pack.at[device], keep, send, sems)
+        for device in range(count):
+            pltpu.make_async_copy(pack.at[device], keep.at[0], sems.at[device]).wait()
 
     part = ((count // 2, packed, D), BF, ANY_SPEC)
-    arrays = [text_in, layout_in]
+    arrays = []
     for back in backs:
         arrays += list(back)
     arrays += [*out_w, *ffn_l, *vecs]
     return kernel_call(
         body,
         [((3, rows, D), BF, VMEM_SPEC), ((3, rows, DL), BF, VMEM_SPEC), part, part],
-        [(me, SMEM_SPEC)] + [(array, VMEM_SPEC) for array in arrays],
+        [(me, SMEM_SPEC), (text_in, STAGED), (layout_in, STAGED)]
+        + [(array, VMEM_SPEC) for array in arrays],
         [
             pltpu.VMEM((count, packed, D), BF),
             pltpu.VMEM((4 * DL, DL), BF),
             pltpu.SemaphoreType.DMA((count,)),
         ],
+        room=60,
     )
 
 
@@ -1386,8 +1453,9 @@
         body,
         [((rows, D), BF, VMEM_SPEC), ((rows, DL), BF, VMEM_SPEC)],
         [(array, VMEM_SPEC) for array in (joined_t, joined_l, resid_t, resid_l)]
-        + [(weight, ANY_SPEC), (layout_w, VMEM_SPEC)],
+        + [(weight, ANY_SPEC), (layout_w, STAGED)],
         [pltpu.VMEM((3 * D, D), BF), pltpu.SemaphoreType.DMA],
+        room=20,
     )
 
 
@@ -1419,14 +1487,16 @@
         jnp.concatenate([text_vector, layout_vector]),
     ).astype(BF)
     sizes = (count, text_rows, layout_rows, text_vec, layout_vec)
-    parts = gather_pieces(packed, shape)
     feed_shard = jnp.concatenate([text_up.T, text_down], 0).astype(BF)
-    feed_parts = gather_pieces(feed_shard, shape)
-    q, k, v, weight, layout_w, lu, ld, tv, lv = project(
-        me, lengths, text_in, layout_in, parts, sizes, dims
-    )
-    out_t, out_l, lse, norm_t, inv_t, norm_l, inv_l = attend(
-        text_in, layout_in, q, k, v, weight, layout_w, tv, lv
+    own = gather_own(jnp.concatenate([packed, feed_shard], 0), shape)
+    parts = own + gather_pieces(packed, shape)
+    feed_parts = own + gather_pieces(feed_shard, shape)
+    middle = HEADS // 2
+    q, k, v, weight, layout_w, lu, ld, tv, lv, first, lse_a = project(
+        me, lengths, text_in, layout_in, parts, sizes, dims, middle
+    )
+    out_t, out_l, lse_b, norm_t, inv_t, norm_l, inv_l = attend(
+        text_in, layout_in, q, k, v, first, weight, layout_w, tv, lv
     )
     span = text_in.shape[0]
     keep = (jnp.arange(span) < lengths[0]) & (dup_rows == 0)
@@ -1460,9 +1530,8 @@
     resid_t, resid_l, out_wt, out_wl, close_t, close_l, dout = close_back_pair(
         grad_t, grad_l, (norm_t, inv_t, norm_l, inv_l), (out_t, out_l), weight, layout_w, tv, lv
     )
-    middle = HEADS // 2
     backs = [
-        heads_back(q, k, v, lse, dout, 0, middle), heads_back(q, k, v, lse, dout, middle, HEADS)
+        heads_back(q, k, v, lse_a, dout, 0, middle), heads_back(q, k, v, lse_b, dout, middle, HEADS)
     ]
     joined_t, joined_l, keep_packed, send_packed = weight_grads(
         me,

time: 348 us -> 338 us (0.971)
  waiting for transfers between devices: 164 us -> 128 us
  starting transfers between devices: 28.5 us -> 52.4 us
  Pallas kernels: 124 us -> 110 us
  local copies, waits for them, and re-layouts: 13.2 us -> 24.4 us
  other arithmetic: 16.1 us -> 20.7 us
    ppermute x10 -> x13, waiting for transfers between devices: 95.9 us -> 77 us  [swap_turn(): lax.ppermute(array, AXES, [(device, device ^ turn(dims, device // core %...]
    ppermute x22 -> x23, waiting for transfers between devices: 68.1 us -> 50.7 us  [swap(): lax.ppermute(array, AXES, [(device, device ^ offset) for device in range(...]
    ppermute x22 -> x23, starting transfers between devices: 18.7 us -> 34.1 us  [swap(): lax.ppermute(array, AXES, [(device, device ^ offset) for device in range(...]
    pallas_call x10 -> x11, Pallas kernels: 124 us -> 110 us  [kernel_call(): pl.pallas_call(with_copies if staged else body, out_shape=[jax.ShapeDtype...]
    unnamed x64 -> x78, local copies, waits for them, and re-layouts: 8.94 us -> 20.1 us
    ppermute x10 -> x13, starting transfers between devices: 9.77 us -> 18.2 us  [swap_turn(): lax.ppermute(array, AXES, [(device, device ^ turn(dims, device // core %...]
    another operation x5 -> x6, other arithmetic: 0.03 us -> 4.82 us
  transfers between devices with their start and end apart: 32 -> 36, of which waited for: 16 -> 16; matrix products, arithmetic and copies ran while one was open for 6% -> 7% of each run, Pallas kernels for 22% -> 21%
where the time goes in v1:
time: 338 us; the launch traced here: 337 us
  waiting for transfers between devices  128 us (38%)
  Pallas kernels  110 us (33%)
  starting transfers between devices  52.4 us (16%)
  local copies, waits for them, and re-layouts  24.4 us (7%)
  other arithmetic  20.7 us (6%)
    pallas_call x11, Pallas kernels, kernel_call(): pl.pallas_call(with_copies if staged else body, out_shape=[jax.ShapeDtype...  110 us
    ppermute x13, waiting for transfers between devices, swap_turn(): lax.ppermute(array, AXES, [(device, device ^ turn(dims, device // core %...  77 us
    ppermute x23, waiting for transfers between devices, swap(): lax.ppermute(array, AXES, [(device, device ^ offset) for device in range(...  50.7 us
    ppermute x23, starting transfers between devices, swap(): lax.ppermute(array, AXES, [(device, device ^ offset) for device in range(...  34.1 us
    unnamed x78, local copies, waits for them, and re-layouts  20.1 us
    ppermute x13, starting transfers between devices, swap_turn(): lax.ppermute(array, AXES, [(device, device ^ turn(dims, device // core %...  18.2 us
    convert_element_type x4, other arithmetic, reduce_part(): got = swap_turn(added(terms, half, 2 * half).astype(BF), dims, which, count)  7.75 us
  transfers between devices with their start and end apart: 36, of which 16 were waited for; matrix products, arithmetic and copies ran while one was open for 7% of the time, Pallas kernels for 21%

profile of v1, /device:TPU:0, one launch (start us, length us, event | category | flops | bytes accessed | tf_op | source)
XLA Modules:
  0.0 336.9 jit_solution(6655475362103583133)
XLA Ops:
  4.3 1.0 convert.43
  5.4 5.1 %collective-permute-start.6 = (bf16[1,128,768]{2,1,0:T(8,128)(2,1)S(1)}, bf16[1,128,768]{2,1,0:T(8,128)(2,1)S(1)}, u32[]{:S(2)}, u32[]{:S(2)}) collective-permute-start(bf16[1,128,768]{2,1,0:T(8,128)(2,1)S(1)} %get-tuple-element.143), channel_id=1, source_target_pairs={{0,6},{1,7},{2,4},{3,5},{4,2},{5,3},{6,0},{7,1},{8,14},{9,15},{10,... | collective-permute-start | bytes 589832 | tf_op jit(solution)/shard_map/ppermute | solution.py:42
  11.2 1.0 convert.50
  12.2 1.0 convert_bitcast_fusion
  13.2 1.7 collective-permute-start
  15.0 3.7 %collective-permute-start.16 = (bf16[1,192,768]{2,1,0:T(8,128)(2,1)S(1)}, bf16[1,192,768]{2,1,0:T(8,128)(2,1)S(1)}, u32[]{:S(2)}, u32[]{:S(2)}) collective-permute-start(bf16[1,192,768]{2,1,0:T(8,128)(2,1)S(1)} %pad_maximum_fusion), channel_id=1, source_target_pairs={{0,6},{1,7},{2,4},{3,5},{4,2},{5,3},{6,0},{7,1},{8,14},{9,15},{10,... | collective-permute-start | bytes 884744 | tf_op jit(solution)/shard_map/ppermute | solution.py:42
  18.6 7.3 %collective-permute-start.15 = (bf16[1,192,768]{2,1,0:T(8,128)(2,1)S(1)}, bf16[1,192,768]{2,1,0:T(8,128)(2,1)S(1)}, u32[]{:S(2)}, u32[]{:S(2)}) collective-permute-start(bf16[1,192,768]{2,1,0:T(8,128)(2,1)S(1)} %pad_maximum_fusion), channel_id=1, source_target_pairs={{0,4},{1,5},{2,6},{3,7},{4,0},{5,1},{6,2},{7,3},{8,12},{9,13},{10,... | collective-permute-start | bytes 884744 | tf_op jit(solution)/shard_map/ppermute | solution.py:42
  25.9 14.9 %collective-permute-done.5.refs_1_ = bf16[1,128,768]{2,1,0:T(8,128)(2,1)S(1)} collective-permute-done((bf16[1,128,768]{2,1,0:T(8,128)(2,1)S(1)}, bf16[1,128,768]{2,1,0:T(8,128)(2,1)S(1)}, u32[]{:S(2)}, u32[]{:S(2)}) %collective-permute-start.5) | collective-permute-done | bytes 196640 | tf_op jit(solution)/shard_map/ppermute | solution.py:42
  40.8 1.5 collective-permute-start.1
  43.1 1.6 collective-permute-start.7
  44.7 7.9 %collective-permute-done.15.refs_1_ = bf16[1,192,768]{2,1,0:T(8,128)(2,1)S(1)} collective-permute-done((bf16[1,192,768]{2,1,0:T(8,128)(2,1)S(1)}, bf16[1,192,768]{2,1,0:T(8,128)(2,1)S(1)}, u32[]{:S(2)}, u32[]{:S(2)}) %collective-permute-start.15) | collective-permute-done | bytes 294944 | tf_op jit(solution)/shard_map/ppermute | solution.py:42
  52.6 1.7 collective-permute-done.14.refs_0_
  54.5 1.6 collective-permute-start.17
  56.1 1.5 collective-permute-start.2
  58.1 1.5 collective-permute-start.8
  59.6 10.4 %collective-permute-done.2.refs_3_ = bf16[1,320,768]{2,1,0:T(8,128)(2,1)S(1)} collective-permute-done((bf16[1,320,768]{2,1,0:T(8,128)(2,1)S(1)}, bf16[1,320,768]{2,1,0:T(8,128)(2,1)S(1)}, u32[]{:S(2)}, u32[]{:S(2)}) %collective-permute-start.2) | collective-permute-done | bytes 491552 | tf_op jit(solution)/shard_map/ppermute | solution.py:649
  70.1 1.5 collective-permute-start.9
  71.6 1.3 shard_map.229.refs_4_.refs_10_
  73.0 3.2 collective-permute-done.17.refs_13_
  76.1 1.5 collective-permute-start.19
  77.6 8.2 %collective-permute-done.8.refs_8_ = bf16[3,128,768]{2,1,0:T(8,128)(2,1)S(1)} collective-permute-done((bf16[3,128,768]{2,1,0:T(8,128)(2,1)S(1)}, bf16[3,128,768]{2,1,0:T(8,128)(2,1)S(1)}, u32[]{:S(2)}, u32[]{:S(2)}) %collective-permute-start.8) | collective-permute-done | bytes 589856 | tf_op jit(solution)/shard_map/ppermute | solution.py:649
  85.9 2.9 collective-permute-start.12
  88.9 3.3 collective-permute-done.9.refs_9_
  92.2 3.0 collective-permute-start.13
  95.8 1.0 collective-permute-done.13.refs_13_
  97.2 4.5 %collective-permute-done.19.refs_15_ = bf16[3,192,768]{2,1,0:T(8,128)(2,1)} collective-permute-done((bf16[3,192,768]{2,1,0:T(8,128)(2,1)}, bf16[3,192,768]{2,1,0:T(8,128)(2,1)}, u32[]{:S(2)}, u32[]{:S(2)}) %collective-permute-start.19) | collective-permute-done | bytes 884768 | tf_op jit(solution)/shard_map/ppermute | solution.py:649
  101.8 2.6 collective-permute-start.23
  105.9 1.8 copy.33.refs_3_.refs_1_.refs_2_
  107.7 1.8 copy.35.refs_7_
  109.5 13.5 %shard_map.231 = (bf16[12,512,128]{2,1,0:T(8,128)(2,1)}, bf16[12,512,128]{2,1,0:T(8,128)(2,1)}, bf16[12,512,128]{2,1,0:T(8,128)(2,1)}, bf16[3072,768]{1,0:T(8,12...) custom-call(s32[1]{0:T(128)} %bitcast.refs_0_, ...), custom_call_target="tpu_custom_call" | custom-call | tf_op jit(solution)/shard_map/pallas_call | solution.py:609
  123.0 12.3 %shard_map.232 = (bf16[512,768]{1,0:T(8,128)(2,1)}, bf16[512,192]{1,0:T(8,128)(2,1)}, f32[6,1,512]{2,1,0:T(1,128)}, f32[512,768]{1,0:T(8,128)}, f32[512,1]{1,0:T...) custom-call(bf16[512,768]{1,0:T(8,128)(2,1)} %refs_1_.3, bf16[512,192]{1,0:T(8,128)(2,1)} %copy.33.refs_3_.refs_1_.refs_2_, ...), custom_call_target="tpu_custom_call" | custom-call | tf_op jit(solution)/shard_map/pallas_call | solution.py:609
  135.3 38.6 %shard_map.234 = (bf16[512,768]{1,0:T(8,128)(2,1)}, bf16[512,192]{1,0:T(8,128)(2,1)}, f32[512,768]{1,0:T(8,128)}, f32[512,192]{1,0:T(8,128)}, f32[7,1,768]{2,1,0...) custom-call(s32[1]{0:T(128)} %bitcast.refs_0_, ...), custom_call_target="tpu_custom_call" | custom-call | tf_op jit(solution)/shard_map/pallas_call | solution.py:609
  174.0 8.4 %shard_map.235 = (f32[512,768]{1,0:T(8,128)}, f32[512,192]{1,0:T(8,128)}, bf16[768,768]{1,0:T(8,128)(2,1)}, bf16[192,192]{1,0:T(8,128)(2,1)}, f32[3,1,768]{2,1,0...) custom-call(f32[512,768]{1,0:T(8,128)} %get-tuple-element.74.refs_0_, ...), custom_call_target="tpu_custom_call" | custom-call | tf_op jit(solution)/shard_map/pallas_call | solution.py:609
  182.5 1.4 copy-done.4
  183.9 1.4 copy-done.5
  185.3 9.4 %shard_map.237 = (bf16[6,512,128]{2,1,0:T(8,128)(2,1)S(1)}, bf16[6,512,128]{2,1,0:T(8,128)(2,1)S(1)}, bf16[6,512,128]{2,1,0:T(8,128)(2,1)S(1)}) custom-call(bf16[12,512,128]{2,1,0:T(8,128)(2,1)S(1)} %copy-done.2, bf16[12,512,128]{2,1,0:T(8,128)(2,1)S(1)} %copy-done.3, bf16[12,512,128]{2,1,0:T(8,128)(2,1)S(1)} %copy-done.4, f32[6,1,512]{2,1,0:T(1,128)S(1)} %copy-done.21, ...), custom_call_target="tpu_custom_call" | custom-call | tf_op jit(solution)/shard_map/pallas_call | solution.py:609
  195.6 0.9 copy-done.13
  196.5 9.6 %shard_map.236 = (bf16[6,512,128]{2,1,0:T(8,128)(2,1)S(1)}, bf16[6,512,128]{2,1,0:T(8,128)(2,1)S(1)}, bf16[6,512,128]{2,1,0:T(8,128)(2,1)S(1)}) custom-call(bf16[12,512,128]{2,1,0:T(8,128)(2,1)S(1)} %copy-done.2, bf16[12,512,128]{2,1,0:T(8,128)(2,1)S(1)} %copy-done.3, bf16[12,512,128]{2,1,0:T(8,128)(2,1)S(1)} %copy-done.4, f32[6,1,512]{2,1,0:T(1,128)S(1)} %copy-done.20, ...), custom_call_target="tpu_custom_call" | custom-call | tf_op jit(solution)/shard_map/pallas_call | solution.py:609
  207.0 1.0 copy-done.16
  208.9 11.7 %shard_map.238 = (bf16[3,512,768]{2,1,0:T(8,128)(2,1)}, bf16[3,512,192]{2,1,0:T(8,128)(2,1)}, bf16[16,128,768]{2,1,0:T(8,128)(2,1)}, bf16[16,128,768]{2,1,0:T(8,128)(2,1)}) custom-call(s32[1]{0:T(128)} %bitcast.refs_0_, bf16[512,768]{1,0:T(8,128)(2,1)} %refs_1_.3, bf16[512,192]{1,0:T(8,128)(2,1)} %copy.33.refs_3_.refs_1_.refs_2_, ...), custom_call_target="tpu_custom_call" | custom-call | tf_op jit(solution)/shard_map/pallas_call | solution.py:609
  221.2 3.1 add_convert_fusion
  224.3 1.6 collective-permute-start.31
  227.1 1.6 collective-permute-start.25
  228.7 41.4 %collective-permute-done.25 = bf16[8,128,768]{2,1,0:T(8,128)(2,1)S(1)} collective-permute-done((bf16[8,128,768]{2,1,0:T(8,128)(2,1)S(1)}, bf16[8,128,768]{2,1,0:T(8,128)(2,1)S(1)}, u32[]{:S(2)}, u32[]{:S(2)}) %collective-permute-start.25) | collective-permute-done | bytes 1572896 | tf_op jit(solution)/shard_map/ppermute | solution.py:649
  270.4 1.5 collective-permute-start.26
  271.9 4.0 %add_convert_fusion.2 = bf16[4,192,768]{2,1,0:T(8,128)(2,1)} fusion(bf16[8,192,768]{2,1,0:T(8,128)(2,1)S(1)} %collective-permute-done.31, bf16[16,192,768]{2,1,0:T(8,128)(2,1)} %collective-permute-done.30, bf16[16,192,768]{2,1,0:T(8,128)(2,1)} %get-tuple-element.104), kind=kLoop, calls=%fused_computation.2 | loop fusion | flops 3538944 | bytes 4718592 | tf_op jit(solution)/shard_map/convert_element_type | solution.py:734
  276.5 5.9 %collective-permute-done.26 = bf16[4,128,768]{2,1,0:T(8,128)(2,1)S(1)} collective-permute-done((bf16[4,128,768]{2,1,0:T(8,128)(2,1)S(1)}, bf16[4,128,768]{2,1,0:T(8,128)(2,1)S(1)}, u32[]{:S(2)}, u32[]{:S(2)}) %collective-permute-start.26) | collective-permute-done | bytes 786464 | tf_op jit(solution)/shard_map/ppermute | solution.py:649
  282.5 1.2 fusion.19
  283.7 2.6 collective-permute-start.29
  287.2 1.8 copy.37
  288.9 2.3 copy-done
  291.3 1.4 copy-done.10
  292.7 1.0 copy-done.18
  293.7 4.3 %shard_map.239 = (bf16[512,768]{1,0:T(8,128)(2,1)}, bf16[512,192]{1,0:T(8,128)(2,1)S(1)}) custom-call(bf16[3,512,768]{2,1,0:T(8,128)(2,1)S(1)} %copy-done.9, bf16[3,512,192]{2,1,0:T(8,128)(2,1)S(1)} %copy-done.11, f32[512,768]{1,0:T(8,128)S(1)} %copy-done.10, f32[512,192]{1,0:T(8,128)S(1)} %copy-done.18, bf16[3072,768]{1,0:T(8,128)(2,1)S(1)} %copy-done, ...), custom_call_target="tpu_custom_call" | custom-call | tf_op jit(solution)/shard_map/pallas_call | solution.py:609
  298.7 1.9 copy.38
  300.6 2.3 collective-permute-done.28
  302.9 1.6 fusion.3
  305.8 2.1 fusion.12
  308.0 2.3 collective-permute-start.35
  310.3 1.2 collective-permute-start.34
  312.7 8.2 %collective-permute-done.33 = bf16[192,768]{1,0:T(8,128)(2,1)S(1)} collective-permute-done((bf16[192,768]{1,0:T(8,128)(2,1)S(1)}, bf16[192,768]{1,0:T(8,128)(2,1)S(1)}, u32[]{:S(2)}, u32[]{:S(2)}) %collective-permute-start.33) | collective-permute-done | bytes 294944 | tf_op jit(solution)/shard_map/ppermute | solution.py:42
  320.9 3.7 %collective-permute-done.35 = bf16[192,768]{1,0:T(8,128)(2,1)S(1)} collective-permute-done((bf16[192,768]{1,0:T(8,128)(2,1)S(1)}, bf16[192,768]{1,0:T(8,128)(2,1)S(1)}, u32[]{:S(2)}, u32[]{:S(2)}) %collective-permute-start.35) | collective-permute-done | bytes 294944 | tf_op jit(solution)/shard_map/ppermute | solution.py:42
  324.5 10.2 %collective-permute-done.34 = bf16[192,768]{1,0:T(8,128)(2,1)S(1)} collective-permute-done((bf16[192,768]{1,0:T(8,128)(2,1)S(1)}, bf16[192,768]{1,0:T(8,128)(2,1)S(1)}, u32[]{:S(2)}, u32[]{:S(2)}) %collective-permute-start.34) | collective-permute-done | bytes 294944 | tf_op jit(solution)/shard_map/ppermute | solution.py:42
  334.7 1.4 fusion.1
  (127 shorter events, 18.6 us)
Async XLA Ops:
  0.6 14.3 %copy-start.27 = (f32[96,768]{1,0:T(8,128)S(1)}, f32[96,768]{1,0:T(8,128)}, u32[]{:S(2)}) copy-start(f32[96,768]{1,0:T(8,128)} %param.20) | copy-start | bytes 884740
  5.4 13.3 %collective-permute-start.6 = (bf16[1,128,768]{2,1,0:T(8,128)(2,1)S(1)}, bf16[1,128,768]{2,1,0:T(8,128)(2,1)S(1)}, u32[]{:S(2)}, u32[]{:S(2)}) collective-permute-start(bf16[1,128,768]{2,1,0:T(8,128)(2,1)S(1)} %get-tuple-element.143), channel_id=1, source_target_pairs={{0,6},{1,7},{2,4},{3,5},{4,2},{5,3},{6,0},{7,1},{8,14},{9,15},{10,... | collective-permute-start | bytes 589832 | tf_op jit(solution)/shard_map/ppermute | solution.py:42
  10.5 30.3 %collective-permute-start.5 = (bf16[1,128,768]{2,1,0:T(8,128)(2,1)S(1)}, bf16[1,128,768]{2,1,0:T(8,128)(2,1)S(1)}, u32[]{:S(2)}, u32[]{:S(2)}) collective-permute-start(bf16[1,128,768]{2,1,0:T(8,128)(2,1)S(1)} %get-tuple-element.143), channel_id=1, source_target_pairs={{0,4},{1,5},{2,6},{3,7},{4,0},{5,1},{6,2},{7,3},{8,12},{9,13},{10,... | collective-permute-start | bytes 589832 | tf_op jit(solution)/shard_map/ppermute | solution.py:42
  10.5 30.3 %collective-permute-start.4 = (bf16[1,128,768]{2,1,0:T(8,128)(2,1)S(1)}, bf16[1,128,768]{2,1,0:T(8,128)(2,1)S(1)}, u32[]{:S(2)}, u32[]{:S(2)}) collective-permute-start(bf16[1,128,768]{2,1,0:T(8,128)(2,1)S(1)} %get-tuple-element.143), channel_id=1, source_target_pairs={{0,2},{1,3},{2,0},{3,1},{4,6},{5,7},{6,4},{7,5},{8,10},{9,11},{10,... | collective-permute-start | bytes 589832 | tf_op jit(solution)/shard_map/ppermute | solution.py:42
  13.2 42.9 %collective-permute-start = (bf16[1,320,768]{2,1,0:T(8,128)(2,1)S(1)}, bf16[1,320,768]{2,1,0:T(8,128)(2,1)S(1)}, u32[]{:S(2)}, u32[]{:S(2)}) collective-permute-start(bf16[1,320,768]{2,1,0:T(8,128)(2,1)S(1)} %maximum_bitcast_fusion.refs_0_), channel_id=1, source_target_pairs={{0,1},{1,0},{2,3},{3,2},{4,5},{5,4},{6,7},{7,6},{8,24},{9,25},{10,... | collective-permute-start | bytes 1474568 | tf_op jit(solution)/shard_map/ppermute | solution.py:649
  15.0 28.1 %collective-permute-start.16 = (bf16[1,192,768]{2,1,0:T(8,128)(2,1)S(1)}, bf16[1,192,768]{2,1,0:T(8,128)(2,1)S(1)}, u32[]{:S(2)}, u32[]{:S(2)}) collective-permute-start(bf16[1,192,768]{2,1,0:T(8,128)(2,1)S(1)} %pad_maximum_fusion), channel_id=1, source_target_pairs={{0,6},{1,7},{2,4},{3,5},{4,2},{5,3},{6,0},{7,1},{8,14},{9,15},{10,... | collective-permute-start | bytes 884744 | tf_op jit(solution)/shard_map/ppermute | solution.py:42
  18.6 34.0 %collective-permute-start.15 = (bf16[1,192,768]{2,1,0:T(8,128)(2,1)S(1)}, bf16[1,192,768]{2,1,0:T(8,128)(2,1)S(1)}, u32[]{:S(2)}, u32[]{:S(2)}) collective-permute-start(bf16[1,192,768]{2,1,0:T(8,128)(2,1)S(1)} %pad_maximum_fusion), channel_id=1, source_target_pairs={{0,4},{1,5},{2,6},{3,7},{4,0},{5,1},{6,2},{7,3},{8,12},{9,13},{10,... | collective-permute-start | bytes 884744 | tf_op jit(solution)/shard_map/ppermute | solution.py:42
  40.8 13.5 %collective-permute-start.14 = (bf16[1,192,768]{2,1,0:T(8,128)(2,1)S(1)}, bf16[1,192,768]{2,1,0:T(8,128)(2,1)S(1)}, u32[]{:S(2)}, u32[]{:S(2)}) collective-permute-start(bf16[1,192,768]{2,1,0:T(8,128)(2,1)S(1)} %pad_maximum_fusion), channel_id=1, source_target_pairs={{0,2},{1,3},{2,0},{3,1},{4,6},{5,7},{6,4},{7,5},{8,10},{9,11},{10,... | collective-permute-start | bytes 884744 | tf_op jit(solution)/shard_map/ppermute | solution.py:42
  40.8 16.8 %collective-permute-start.1 = (bf16[1,320,768]{2,1,0:T(8,128)(2,1)S(1)}, bf16[1,320,768]{2,1,0:T(8,128)(2,1)S(1)}, u32[]{:S(2)}, u32[]{:S(2)}) collective-permute-start(bf16[1,320,768]{2,1,0:T(8,128)(2,1)S(1)} %maximum_bitcast_fusion.refs_0_), channel_id=1, source_target_pairs={{0,16},{1,17},{2,18},{3,19},{4,20},{5,21},{6,22},{7,23},{8,9},{9,8... | collective-permute-start | bytes 1474568 | tf_op jit(solution)/shard_map/ppermute | solution.py:649
  43.1 29.8 %copy-start.8 = (bf16[3,128,768]{2,1,0:T(8,128)(2,1)}, bf16[3,128,768]{2,1,0:T(8,128)(2,1)S(1)}, u32[]{:S(2)}) copy-start(bf16[3,128,768]{2,1,0:T(8,128)(2,1)S(1)} %shard_map.230.refs_6_) | copy-start | bytes 1769476
  43.1 15.0 %collective-permute-start.7 = (bf16[3,128,768]{2,1,0:T(8,128)(2,1)S(1)}, bf16[3,128,768]{2,1,0:T(8,128)(2,1)S(1)}, u32[]{:S(2)}, u32[]{:S(2)}) collective-permute-start(bf16[3,128,768]{2,1,0:T(8,128)(2,1)S(1)} %shard_map.230.refs_6_), channel_id=1, source_target_pairs={{0,1},{1,0},{2,3},{3,2},{4,5},{5,4},{6,7},{7,6},{8,24},{9,25},{10,... | collective-permute-start | bytes 1769480 | tf_op jit(solution)/shard_map/ppermute | solution.py:649
  54.5 55.0 %copy-start.7 = (bf16[3,192,768]{2,1,0:T(8,128)(2,1)}, bf16[3,192,768]{2,1,0:T(8,128)(2,1)S(1)}, u32[]{:S(2)}) copy-start(bf16[3,192,768]{2,1,0:T(8,128)(2,1)S(1)} %shard_map.233.refs_12_) | copy-start | bytes 2654212
  54.5 50.6 %copy-start.36 = (s32[512]{0:T(512)S(1)}, s32[512]{0:T(512)}, u32[]{:S(2)}) copy-start(s32[512]{0:T(512)} %param.17) | copy-start | bytes 6148
  54.5 21.6 %collective-permute-start.17 = (bf16[3,192,768]{2,1,0:T(8,128)(2,1)S(1)}, bf16[3,192,768]{2,1,0:T(8,128)(2,1)}, u32[]{:S(2)}, u32[]{:S(2)}) collective-permute-start(bf16[3,192,768]{2,1,0:T(8,128)(2,1)S(1)} %shard_map.233.refs_12_), channel_id=1, source_target_pairs={{0,1},{1,0},{2,3},{3,2},{4,5},{5,4},{6,7},{7,6},{8,24},{9,25},{10,... | collective-permute-start | bytes 2654216 | tf_op jit(solution)/shard_map/ppermute | solution.py:649
  56.1 16.8 %collective-permute-start.10 = (bf16[3,128,768]{2,1,0:T(8,128)(2,1)S(1)}, bf16[3,128,768]{2,1,0:T(8,128)(2,1)S(1)}, u32[]{:S(2)}, u32[]{:S(2)}) collective-permute-start(bf16[3,128,768]{2,1,0:T(8,128)(2,1)S(1)} %shard_map.230.refs_6_), channel_id=1, source_target_pairs={{0,8},{1,9},{2,10},{3,11},{4,12},{5,13},{6,14},{7,15},{8,0},{9,1},... | collective-permute-start | bytes 1769480 | tf_op jit(solution)/shard_map/ppermute | solution.py:42
  56.1 14.0 %collective-permute-start.2 = (bf16[1,320,768]{2,1,0:T(8,128)(2,1)S(1)}, bf16[1,320,768]{2,1,0:T(8,128)(2,1)S(1)}, u32[]{:S(2)}, u32[]{:S(2)}) collective-permute-start(bf16[1,320,768]{2,1,0:T(8,128)(2,1)S(1)} %collective-permute-done.refs_1_), channel_id=1, source_target_pairs={{0,16},{1,17},{2,18},{3,19},{4,20},{5,21},{6,22},{7,23},{8,9},{9,8... | collective-permute-start | bytes 1474568 | tf_op jit(solution)/shard_map/ppermute | solution.py:649
  57.6 31.2 %collective-permute-start.18 = (bf16[3,192,768]{2,1,0:T(8,128)(2,1)S(1)}, bf16[3,192,768]{2,1,0:T(8,128)(2,1)}, u32[]{:S(2)}, u32[]{:S(2)}) collective-permute-start(bf16[3,192,768]{2,1,0:T(8,128)(2,1)S(1)} %shard_map.233.refs_12_), channel_id=1, source_target_pairs={{0,16},{1,17},{2,18},{3,19},{4,20},{5,21},{6,22},{7,23},{8,9},{9,8... | collective-permute-start | bytes 2654216 | tf_op jit(solution)/shard_map/ppermute | solution.py:649
  58.1 51.3 %copy-start.29 = (bf16[3,128,768]{2,1,0:T(8,128)(2,1)}, bf16[3,128,768]{2,1,0:T(8,128)(2,1)S(1)}, u32[]{:S(2)}) copy-start(bf16[3,128,768]{2,1,0:T(8,128)(2,1)S(1)} %collective-permute-done.7.refs_7_) | copy-start | bytes 1769476
  58.1 27.7 %collective-permute-start.8 = (bf16[3,128,768]{2,1,0:T(8,128)(2,1)S(1)}, bf16[3,128,768]{2,1,0:T(8,128)(2,1)S(1)}, u32[]{:S(2)}, u32[]{:S(2)}) collective-permute-start(bf16[3,128,768]{2,1,0:T(8,128)(2,1)S(1)} %shard_map.230.refs_6_), channel_id=1, source_target_pairs={{0,16},{1,17},{2,18},{3,19},{4,20},{5,21},{6,22},{7,23},{8,9},{9,8... | collective-permute-start | bytes 1769480 | tf_op jit(solution)/shard_map/ppermute | solution.py:649
  70.1 22.1 %collective-permute-start.9 = (bf16[3,128,768]{2,1,0:T(8,128)(2,1)S(1)}, bf16[3,128,768]{2,1,0:T(8,128)(2,1)S(1)}, u32[]{:S(2)}, u32[]{:S(2)}) collective-permute-start(bf16[3,128,768]{2,1,0:T(8,128)(2,1)S(1)} %collective-permute-done.7.refs_7_), channel_id=1, source_target_pairs={{0,16},{1,17},{2,18},{3,19},{4,20},{5,21},{6,22},{7,23},{8,9},{9,8... | collective-permute-start | bytes 1769480 | tf_op jit(solution)/shard_map/ppermute | solution.py:649
  72.9 36.6 %copy-start.1 = (bf16[4,320,768]{2,1,0:T(8,128)(2,1)}, bf16[4,320,768]{2,1,0:T(8,128)(2,1)S(1)}, u32[]{:S(2)}) copy-start(bf16[4,320,768]{2,1,0:T(8,128)(2,1)S(1)} %shard_map.229.refs_4_.refs_10_) | copy-start | bytes 5898244
  72.9 22.4 %copy-start.30 = (bf16[3,128,768]{2,1,0:T(8,128)(2,1)}, bf16[3,128,768]{2,1,0:T(8,128)(2,1)S(1)}, u32[]{:S(2)}) copy-start(bf16[3,128,768]{2,1,0:T(8,128)(2,1)S(1)} %collective-permute-done.10.refs_10_) | copy-start | bytes 1769476
  72.9 36.6 %collective-permute-start.3 = (bf16[4,320,768]{2,1,0:T(8,128)(2,1)S(1)}, bf16[4,320,768]{2,1,0:T(8,128)(2,1)}, u32[]{:S(2)}, u32[]{:S(2)}) collective-permute-start(bf16[4,320,768]{2,1,0:T(8,128)(2,1)S(1)} %shard_map.229.refs_4_.refs_10_), channel_id=1, source_target_pairs={{0,8},{1,9},{2,10},{3,11},{4,12},{5,13},{6,14},{7,15},{8,0},{9,1},... | collective-permute-start | bytes 5898248 | tf_op jit(solution)/shard_map/ppermute | solution.py:42
  76.1 25.6 %collective-permute-start.19 = (bf16[3,192,768]{2,1,0:T(8,128)(2,1)}, bf16[3,192,768]{2,1,0:T(8,128)(2,1)}, u32[]{:S(2)}, u32[]{:S(2)}) collective-permute-start(bf16[3,192,768]{2,1,0:T(8,128)(2,1)} %collective-permute-done.17.refs_13_), channel_id=1, source_target_pairs={{0,16},{1,17},{2,18},{3,19},{4,20},{5,21},{6,22},{7,23},{8,9},{9,8... | collective-permute-start | bytes 2654216 | tf_op jit(solution)/shard_map/ppermute | solution.py:649
  85.9 9.9 %copy-start.31 = (bf16[3,128,768]{2,1,0:T(8,128)(2,1)}, bf16[3,128,768]{2,1,0:T(8,128)(2,1)S(1)}, u32[]{:S(2)}) copy-start(bf16[3,128,768]{2,1,0:T(8,128)(2,1)S(1)} %collective-permute-done.8.refs_8_) | copy-start | bytes 1769476
  85.9 9.4 %collective-permute-start.12 = (bf16[3,128,768]{2,1,0:T(8,128)(2,1)S(1)}, bf16[3,128,768]{2,1,0:T(8,128)(2,1)S(1)}, u32[]{:S(2)}, u32[]{:S(2)}) collective-permute-start(bf16[3,128,768]{2,1,0:T(8,128)(2,1)S(1)} %collective-permute-done.8.refs_8_), channel_id=1, source_target_pairs={{0,8},{1,9},{2,10},{3,11},{4,12},{5,13},{6,14},{7,15},{8,0},{9,1},... | collective-permute-start | bytes 1769480 | tf_op jit(solution)/shard_map/ppermute | solution.py:42
  88.8 6.5 %collective-permute-start.11 = (bf16[3,128,768]{2,1,0:T(8,128)(2,1)S(1)}, bf16[3,128,768]{2,1,0:T(8,128)(2,1)S(1)}, u32[]{:S(2)}, u32[]{:S(2)}) collective-permute-start(bf16[3,128,768]{2,1,0:T(8,128)(2,1)S(1)} %collective-permute-done.7.refs_7_), channel_id=1, source_target_pairs={{0,8},{1,9},{2,10},{3,11},{4,12},{5,13},{6,14},{7,15},{8,0},{9,1},... | collective-permute-start | bytes 1769480 | tf_op jit(solution)/shard_map/ppermute | solution.py:42
  92.2 4.7 %copy-start.32 = (bf16[3,128,768]{2,1,0:T(8,128)(2,1)}, bf16[3,128,768]{2,1,0:T(8,128)(2,1)S(1)}, u32[]{:S(2)}) copy-start(bf16[3,128,768]{2,1,0:T(8,128)(2,1)S(1)} %collective-permute-done.9.refs_9_) | copy-start | bytes 1769476
  92.2 4.7 %collective-permute-start.13 = (bf16[3,128,768]{2,1,0:T(8,128)(2,1)S(1)}, bf16[3,128,768]{2,1,0:T(8,128)(2,1)S(1)}, u32[]{:S(2)}, u32[]{:S(2)}) collective-permute-start(bf16[3,128,768]{2,1,0:T(8,128)(2,1)S(1)} %collective-permute-done.9.refs_9_), channel_id=1, source_target_pairs={{0,8},{1,9},{2,10},{3,11},{4,12},{5,13},{6,14},{7,15},{8,0},{9,1},... | collective-permute-start | bytes 1769480 | tf_op jit(solution)/shard_map/ppermute | solution.py:42
  95.2 2.0 copy-start.33
  95.2 40.1 %collective-permute-start.20 = (bf16[3,192,768]{2,1,0:T(8,128)(2,1)S(1)}, bf16[3,192,768]{2,1,0:T(8,128)(2,1)}, u32[]{:S(2)}, u32[]{:S(2)}) collective-permute-start(bf16[3,192,768]{2,1,0:T(8,128)(2,1)S(1)} %shard_map.233.refs_12_), channel_id=1, source_target_pairs={{0,8},{1,9},{2,10},{3,11},{4,12},{5,13},{6,14},{7,15},{8,0},{9,1},... | collective-permute-start | bytes 2654216 | tf_op jit(solution)/shard_map/ppermute | solution.py:42
  95.3 6.5 %copy-start.34 = (bf16[3,128,768]{2,1,0:T(8,128)(2,1)}, bf16[3,128,768]{2,1,0:T(8,128)(2,1)S(1)}, u32[]{:S(2)}) copy-start(bf16[3,128,768]{2,1,0:T(8,128)(2,1)S(1)} %collective-permute-done.11.refs_11_) | copy-start | bytes 1769476
  95.3 40.0 %collective-permute-start.21 = (bf16[3,192,768]{2,1,0:T(8,128)(2,1)}, bf16[3,192,768]{2,1,0:T(8,128)(2,1)}, u32[]{:S(2)}, u32[]{:S(2)}) collective-permute-start(bf16[3,192,768]{2,1,0:T(8,128)(2,1)} %collective-permute-done.17.refs_13_), channel_id=1, source_target_pairs={{0,8},{1,9},{2,10},{3,11},{4,12},{5,13},{6,14},{7,15},{8,0},{9,1},... | collective-permute-start | bytes 2654216 | tf_op jit(solution)/shard_map/ppermute | solution.py:42
  96.9 7.6 %copy-start.35 = (bf16[3,128,768]{2,1,0:T(8,128)(2,1)}, bf16[3,128,768]{2,1,0:T(8,128)(2,1)S(1)}, u32[]{:S(2)}) copy-start(bf16[3,128,768]{2,1,0:T(8,128)(2,1)S(1)} %collective-permute-done.13.refs_13_) | copy-start | bytes 1769476
  96.9 38.4 %collective-permute-start.22 = (bf16[3,192,768]{2,1,0:T(8,128)(2,1)}, bf16[3,192,768]{2,1,0:T(8,128)(2,1)}, u32[]{:S(2)}, u32[]{:S(2)}) collective-permute-start(bf16[3,192,768]{2,1,0:T(8,128)(2,1)} %collective-permute-done.18.refs_14_), channel_id=1, source_target_pairs={{0,8},{1,9},{2,10},{3,11},{4,12},{5,13},{6,14},{7,15},{8,0},{9,1},... | collective-permute-start | bytes 2654216 | tf_op jit(solution)/shard_map/ppermute | solution.py:42
  101.8 33.6 %collective-permute-start.23 = (bf16[3,192,768]{2,1,0:T(8,128)(2,1)}, bf16[3,192,768]{2,1,0:T(8,128)(2,1)}, u32[]{:S(2)}, u32[]{:S(2)}) collective-permute-start(bf16[3,192,768]{2,1,0:T(8,128)(2,1)} %collective-permute-done.19.refs_15_), channel_id=1, source_target_pairs={{0,8},{1,9},{2,10},{3,11},{4,12},{5,13},{6,14},{7,15},{8,0},{9,1},... | collective-permute-start | bytes 2654216 | tf_op jit(solution)/shard_map/ppermute | solution.py:42
  173.9 47.3 %collective-permute-start.30 = (bf16[16,192,768]{2,1,0:T(8,128)(2,1)}, bf16[16,192,768]{2,1,0:T(8,128)(2,1)}, u32[]{:S(2)}, u32[]{:S(2)}) collective-permute-start(bf16[16,192,768]{2,1,0:T(8,128)(2,1)} %get-tuple-element.105), channel_id=1, source_target_pairs={{0,8},{1,9},{2,10},{3,11},{4,12},{5,13},{6,14},{7,15},{8,0},{9,1},... | collective-permute-start | bytes 14155784 | tf_op jit(solution)/shard_map/ppermute | solution.py:42
  174.0 8.5 %copy-start.2 = (bf16[12,512,128]{2,1,0:T(8,128)(2,1)S(1)}, bf16[12,512,128]{2,1,0:T(8,128)(2,1)}, u32[]{:S(2)}) copy-start(bf16[12,512,128]{2,1,0:T(8,128)(2,1)} %get-tuple-element.59.refs_2_.q_any) | copy-start | bytes 4718596
  174.0 8.5 %copy-start.3 = (bf16[12,512,128]{2,1,0:T(8,128)(2,1)S(1)}, bf16[12,512,128]{2,1,0:T(8,128)(2,1)}, u32[]{:S(2)}) copy-start(bf16[12,512,128]{2,1,0:T(8,128)(2,1)} %get-tuple-element.60.refs_3_.k_any) | copy-start | bytes 4718596
  174.0 8.5 %copy-start.21 = (f32[6,1,512]{2,1,0:T(1,128)S(1)}, f32[6,1,512]{2,1,0:T(1,128)}, u32[]{:S(2)}) copy-start(f32[6,1,512]{2,1,0:T(1,128)} %get-tuple-element.84.lse_any) | copy-start | bytes 36868
  182.5 1.4 copy-start.4
  183.9 1.4 copy-start.5
  185.3 11.2 %copy-start.20 = (f32[6,1,512]{2,1,0:T(1,128)S(1)}, f32[6,1,512]{2,1,0:T(1,128)}, u32[]{:S(2)}) copy-start(f32[6,1,512]{2,1,0:T(1,128)} %get-tuple-element.73.lse_any) | copy-start | bytes 36868
  196.5 9.6 %copy-start.14 = (bf16[6,512,128]{2,1,0:T(8,128)(2,1)}, bf16[6,512,128]{2,1,0:T(8,128)(2,1)S(1)}, u32[]{:S(2)}) copy-start(bf16[6,512,128]{2,1,0:T(8,128)(2,1)S(1)} %get-tuple-element.87.refs_8_) | copy-start | bytes 2359300
  220.6 6.1 %collective-permute-start.24 = (bf16[16,128,768]{2,1,0:T(8,128)(2,1)}, bf16[16,128,768]{2,1,0:T(8,128)(2,1)S(1)}, u32[]{:S(2)}, u32[]{:S(2)}) collective-permute-start(bf16[16,128,768]{2,1,0:T(8,128)(2,1)} %get-tuple-element.103), channel_id=1, source_target_pairs={{0,8},{1,9},{2,10},{3,11},{4,12},{5,13},{6,14},{7,15},{8,0},{9,1},... | collective-permute-start | bytes 9437192 | tf_op jit(solution)/shard_map/ppermute | solution.py:42
  221.2 5.5 %copy-start.22 = (bf16[16,128,768]{2,1,0:T(8,128)(2,1)S(1)}, bf16[16,128,768]{2,1,0:T(8,128)(2,1)}, u32[]{:S(2)}) copy-start(bf16[16,128,768]{2,1,0:T(8,128)(2,1)} %get-tuple-element.102) | copy-start | bytes 9437188
  224.3 47.5 %collective-permute-start.31 = (bf16[8,192,768]{2,1,0:T(8,128)(2,1)S(1)}, bf16[8,192,768]{2,1,0:T(8,128)(2,1)S(1)}, u32[]{:S(2)}, u32[]{:S(2)}) collective-permute-start(bf16[8,192,768]{2,1,0:T(8,128)(2,1)S(1)} %add_convert_fusion), channel_id=1, source_target_pairs={{0,1},{1,0},{2,3},{3,2},{4,5},{5,4},{6,7},{7,6},{8,24},{9,25},{10,... | collective-permute-start | bytes 7077896 | tf_op jit(solution)/shard_map/ppermute | solution.py:649
  226.7 55.7 %copy-start.23 = (bf16[16,128,768]{2,1,0:T(8,128)(2,1)}, bf16[16,128,768]{2,1,0:T(8,128)(2,1)S(1)}, u32[]{:S(2)}) copy-start(bf16[16,128,768]{2,1,0:T(8,128)(2,1)S(1)} %collective-permute-done.24) | copy-start | bytes 9437188
  227.1 43.0 %collective-permute-start.25 = (bf16[8,128,768]{2,1,0:T(8,128)(2,1)S(1)}, bf16[8,128,768]{2,1,0:T(8,128)(2,1)S(1)}, u32[]{:S(2)}, u32[]{:S(2)}) collective-permute-start(bf16[8,128,768]{2,1,0:T(8,128)(2,1)S(1)} %add_convert_fusion.1), channel_id=1, source_target_pairs={{0,1},{1,0},{2,3},{3,2},{4,5},{5,4},{6,7},{7,6},{8,24},{9,25},{10,... | collective-permute-start | bytes 4718600 | tf_op jit(solution)/shard_map/ppermute | solution.py:649
  270.1 12.4 %copy-start.26 = (bf16[8,128,768]{2,1,0:T(8,128)(2,1)}, bf16[8,128,768]{2,1,0:T(8,128)(2,1)S(1)}, u32[]{:S(2)}) copy-start(bf16[8,128,768]{2,1,0:T(8,128)(2,1)S(1)} %collective-permute-done.25) | copy-start | bytes 4718596
  270.4 12.1 %collective-permute-start.26 = (bf16[4,128,768]{2,1,0:T(8,128)(2,1)S(1)}, bf16[4,128,768]{2,1,0:T(8,128)(2,1)S(1)}, u32[]{:S(2)}, u32[]{:S(2)}) collective-permute-start(bf16[4,128,768]{2,1,0:T(8,128)(2,1)S(1)} %add_convert_fusion.3), channel_id=1, source_target_pairs={{0,16},{1,17},{2,18},{3,19},{4,20},{5,21},{6,22},{7,23},{8,9},{9,8... | collective-permute-start | bytes 2359304 | tf_op jit(solution)/shard_map/ppermute | solution.py:649
  271.9 4.0 %copy-start.24 = (bf16[8,192,768]{2,1,0:T(8,128)(2,1)}, bf16[8,192,768]{2,1,0:T(8,128)(2,1)S(1)}, u32[]{:S(2)}) copy-start(bf16[8,192,768]{2,1,0:T(8,128)(2,1)S(1)} %collective-permute-done.31) | copy-start | bytes 7077892
  271.9 17.0 %copy-start.11 = (bf16[3,512,192]{2,1,0:T(8,128)(2,1)S(1)}, bf16[3,512,192]{2,1,0:T(8,128)(2,1)}, u32[]{:S(2)}) copy-start(bf16[3,512,192]{2,1,0:T(8,128)(2,1)} %get-tuple-element.97.refs_1_) | copy-start | bytes 1769476
  275.9 13.1 %copy-start.6 = (bf16[768,192]{1,0:T(8,128)(2,1)S(1)}, bf16[768,192]{1,0:T(8,128)(2,1)}, u32[]{:S(2)}) copy-start(bf16[768,192]{1,0:T(8,128)(2,1)} %get-tuple-element.64.refs_7_.refs_9_.refs_5_) | copy-start | bytes 884740
  275.9 13.1 %copy-start.9 = (bf16[3,512,768]{2,1,0:T(8,128)(2,1)S(1)}, bf16[3,512,768]{2,1,0:T(8,128)(2,1)}, u32[]{:S(2)}) copy-start(bf16[3,512,768]{2,1,0:T(8,128)(2,1)} %get-tuple-element.96.refs_0_) | copy-start | bytes 7077892
  275.9 30.0 %collective-permute-start.32 = (bf16[4,192,768]{2,1,0:T(8,128)(2,1)}, bf16[4,192,768]{2,1,0:T(8,128)(2,1)}, u32[]{:S(2)}, u32[]{:S(2)}) collective-permute-start(bf16[4,192,768]{2,1,0:T(8,128)(2,1)} %add_convert_fusion.2), channel_id=1, source_target_pairs={{0,16},{1,17},{2,18},{3,19},{4,20},{5,21},{6,22},{7,23},{8,9},{9,8... | collective-permute-start | bytes 3538952 | tf_op jit(solution)/shard_map/ppermute | solution.py:649
  283.7 16.9 %collective-permute-start.27 = (bf16[128,768]{1,0:T(8,128)(2,1)}, bf16[128,768]{1,0:T(8,128)(2,1)}, u32[]{:S(2)}, u32[]{:S(2)}) collective-permute-start(bf16[128,768]{1,0:T(8,128)(2,1)} %get-tuple-element.133), channel_id=1, source_target_pairs={{0,2},{1,3},{2,0},{3,1},{4,6},{5,7},{6,4},{7,5},{8,10},{9,11},{10,... | collective-permute-start | bytes 589832 | tf_op jit(solution)/shard_map/ppermute | solution.py:42
  283.7 16.9 %collective-permute-start.29 = (bf16[128,768]{1,0:T(8,128)(2,1)}, bf16[128,768]{1,0:T(8,128)(2,1)}, u32[]{:S(2)}, u32[]{:S(2)}) collective-permute-start(bf16[128,768]{1,0:T(8,128)(2,1)} %get-tuple-element.134), channel_id=1, source_target_pairs={{0,6},{1,7},{2,4},{3,5},{4,2},{5,3},{6,0},{7,1},{8,14},{9,15},{10,... | collective-permute-start | bytes 589832 | tf_op jit(solution)/shard_map/ppermute | solution.py:42
  286.4 16.6 %collective-permute-start.28 = (bf16[128,768]{1,0:T(8,128)(2,1)}, bf16[128,768]{1,0:T(8,128)(2,1)}, u32[]{:S(2)}, u32[]{:S(2)}) collective-permute-start(bf16[128,768]{1,0:T(8,128)(2,1)} %get-tuple-element.135), channel_id=1, source_target_pairs={{0,4},{1,5},{2,6},{3,7},{4,0},{5,1},{6,2},{7,3},{8,12},{9,13},{10,... | collective-permute-start | bytes 589832 | tf_op jit(solution)/shard_map/ppermute | solution.py:42
  288.9 2.3 copy-start
  298.7 7.1 %copy-start.25 = (bf16[8,192,768]{2,1,0:T(8,128)(2,1)S(1)}, bf16[8,192,768]{2,1,0:T(8,128)(2,1)}, u32[]{:S(2)}) copy-start(bf16[8,192,768]{2,1,0:T(8,128)(2,1)} %copy-done.24) | copy-start | bytes 7077892
  307.9 12.9 %collective-permute-start.33 = (bf16[192,768]{1,0:T(8,128)(2,1)S(1)}, bf16[192,768]{1,0:T(8,128)(2,1)S(1)}, u32[]{:S(2)}, u32[]{:S(2)}) collective-permute-start(bf16[192,768]{1,0:T(8,128)(2,1)S(1)} %get-tuple-element.130), channel_id=1, source_target_pairs={{0,2},{1,3},{2,0},{3,1},{4,6},{5,7},{6,4},{7,5},{8,10},{9,11},{10,... | collective-permute-start | bytes 884744 | tf_op jit(solution)/shard_map/ppermute | solution.py:42
  308.0 16.5 %collective-permute-start.35 = (bf16[192,768]{1,0:T(8,128)(2,1)S(1)}, bf16[192,768]{1,0:T(8,128)(2,1)S(1)}, u32[]{:S(2)}, u32[]{:S(2)}) collective-permute-start(bf16[192,768]{1,0:T(8,128)(2,1)S(1)} %get-tuple-element.131), channel_id=1, source_target_pairs={{0,6},{1,7},{2,4},{3,5},{4,2},{5,3},{6,0},{7,1},{8,14},{9,15},{10,... | collective-permute-start | bytes 884744 | tf_op jit(solution)/shard_map/ppermute | solution.py:42
  310.3 24.4 %collective-permute-start.34 = (bf16[192,768]{1,0:T(8,128)(2,1)S(1)}, bf16[192,768]{1,0:T(8,128)(2,1)S(1)}, u32[]{:S(2)}, u32[]{:S(2)}) collective-permute-start(bf16[192,768]{1,0:T(8,128)(2,1)S(1)} %get-tuple-element.132), channel_id=1, source_target_pairs={{0,4},{1,5},{2,6},{3,7},{4,0},{5,1},{6,2},{7,3},{8,12},{9,13},{10,... | collective-permute-start | bytes 884744 | tf_op jit(solution)/shard_map/ppermute | solution.py:42
  (9 other events, 8.9 us)

commit v2 on v1

--- a/solution.py
+++ b/solution.py
@@ -553,6 +553,7 @@
 SMEM_SPEC = pl.BlockSpec(memory_space=pltpu.SMEM)
 ANY_SPEC = pl.BlockSpec(memory_space=pl.ANY)
 STAGED = "staged"
+LATE = "late"
 
 
 def nn(left, right):
@@ -587,54 +588,64 @@
 
 
 def kernel_call(body, outs, ins, scratch=(), room=60):
-    staged = [index for index, (_, spec) in enumerate(ins) if spec == STAGED]
+    copied = [index for index, (_, spec) in enumerate(ins) if spec in (STAGED, LATE)]
+    late = [index for index, (_, spec) in enumerate(ins) if spec == LATE]
 
     def with_copies(*refs):
-        rooms, sems = refs[len(refs) - len(staged) - 1 : -1], refs[-1]
-        given = list(refs[: len(refs) - len(staged) - 1])
-        copies = []
-        for order, (index, target) in enumerate(zip(staged, rooms)):
-            copies.append(pltpu.make_async_copy(given[index], target, sems.at[order]))
+        rooms, sems = refs[len(refs) - len(copied) - 1 : -1], refs[-1]
+        given = list(refs[: len(refs) - len(copied) - 1])
+        copies = {}
+        for index, target in zip(copied, rooms):
+            copies[index] = pltpu.make_async_copy(given[index], target, sems.at[len(copies)])
             given[index] = target
+        for copy in copies.values():
+            copy.start()
+        for index in copied:
+            if index not in late:
+                copies[index].wait()
+
+        def settle():
+            for index in late:
+                copies[index].wait()
+
+        body(*([settle] if late else []), *given)
+
+    scratch = list(scratch)
+    if copied:
+        scratch += [pltpu.VMEM(ins[index][0].shape, ins[index][0].dtype) for index in copied]
+        scratch.append(pltpu.SemaphoreType.DMA((len(copied),)))
+    return pl.pallas_call(
+        with_copies if copied else body,
+        out_shape=[jax.ShapeDtypeStruct(shape, kind) for shape, kind, _ in outs],
+        in_specs=[ANY_SPEC if spec in (STAGED, LATE) else spec for _, spec in ins],
+        out_specs=[spec for _, _, spec in outs],
+        scratch_shapes=scratch,
+        compiler_params=pltpu.CompilerParams(vmem_limit_bytes=room * 2**20),
+    )(*[array for array, _ in ins])
+
+
+def stack_rows(parts):
+    rows = [part.shape[0] for part in parts]
+    width = parts[0].shape[1]
+
+    def body(*refs):
+        out, sems = refs[len(parts)], refs[len(parts) + 1]
+        copies, base = [], 0
+        for index, size in enumerate(rows):
+            copies.append(
+                pltpu.make_async_copy(refs[index], out.at[base : base + size], sems.at[index])
+            )
+            base += size
         for copy in copies:
             copy.start()
         for copy in copies:
             copy.wait()
-        body(*given)
-
-    scratch = list(scratch)
-    if staged:
-        scratch += [pltpu.VMEM(ins[index][0].shape, ins[index][0].dtype) for index in staged]
-        scratch.append(pltpu.SemaphoreType.DMA((len(staged),)))
-    return pl.pallas_call(
-        with_copies if staged else body,
-        out_shape=[jax.ShapeDtypeStruct(shape, kind) for shape, kind, _ in outs],
-        in_specs=[ANY_SPEC if spec == STAGED else spec for _, spec in ins],
-        out_specs=[spec for _, _, spec in outs],
-        scratch_shapes=scratch,
-        compiler_params=pltpu.CompilerParams(vmem_limit_bytes=room * 2**20),
-    )(*[array for array, _ in ins])
-
-
-def stack_blocks(blocks):
-    count, (_, rows, width) = len(blocks), blocks[0].shape
-
-    def body(*refs):
-        out, sems = refs[count], refs[count + 1]
-        copies = [
-            pltpu.make_async_copy(refs[index].at[0], out.at[index], sems.at[index])
-            for index in range(count)
-        ]
-        for copy in copies:
-            copy.start()
-        for copy in copies:
-            copy.wait()
 
     return kernel_call(
         body,
-        [((count, rows, width), BF, ANY_SPEC)],
-        [(block, VMEM_SPEC) for block in blocks],
-        [pltpu.SemaphoreType.DMA((count,))],
+        [((sum(rows), width), BF, ANY_SPEC)],
+        [(part, VMEM_SPEC) for part in parts],
+        [pltpu.SemaphoreType.DMA((len(parts),))],
         room=8,
     )[0]
 
@@ -660,53 +671,66 @@
     return pieces
 
 
-def gather_own(shard, shape):
-    count = shape["gx"] * shape["gy"]
-    dims = exchange_dims(shape)
-    near = stack_blocks(spread(shard[None], dims, count))
-    return [near, swap(near, dims[1][0], count)]
-
-
-def gather_pieces(shard, shape):
+def gather_parts(attention, feed, shape):
     count = shape["gx"] * shape["gy"]
     dims = exchange_dims(shape)
     _, (core, _), (z, nz), _ = dims
-    blocks = []
-    for step in range(1, nz):
-        blocks.append(swap(shard[None], z * step, count))
-    pieces = spread(stack_blocks(blocks), dims, count)
-    for index in range(4):
-        pieces.append(swap(pieces[index], core, count))
-    return pieces
-
-
-def fetch_blocks(me, dims, refs, place, sems):
+    both = jnp.concatenate([attention, feed], 0)
+
+    def shifted(shard, step):
+        return swap(shard, z * step, count)
+
+    def exchanged(held):
+        pieces = spread(held, dims, count)
+        for index in range(4):
+            pieces.append(swap(pieces[index], core, count))
+        return pieces
+
+    firsts = [shifted(attention, step) for step in range(1, nz)]
+    own = stack_rows(spread(both, dims, count))
+    own = [own, swap(own, core, count)]
+    first = exchanged(stack_rows(firsts))
+    seconds = [shifted(feed, step) for step in range(1, nz)]
+    return own, first, exchanged(stack_rows(seconds))
+
+
+def part_blocks(me, dims, own, others, skip, rows, both):
     (x, _), (core, _), (z, nz), (y, _) = dims
     odd = me // core % 2
-    first = jnp.where(odd == 1, x, y)
-    second = jnp.where(odd == 1, y, x)
-    mine, partner = [0, first, second, x ^ y], [core, core ^ second, core ^ first, core ^ x ^ y]
+    low = jnp.where(odd == 1, x, y)
+    top = jnp.where(odd == 1, y, x)
+    mine, partner = [0, low, top, x ^ y], [core, core ^ top, core ^ low, core ^ x ^ y]
     blocks = []
-    for ref, offsets in zip(refs[:2], (mine, partner)):
-        blocks += [(ref.at[index], offset, True) for index, offset in enumerate(offsets)]
-    for ref, offset in zip(refs[2:], mine + partner):
-        blocks += [(ref.at[step - 1], offset ^ (z * step), False) for step in range(1, nz)]
+    for ref, offsets in zip(own, (mine, partner)):
+        for index, offset in enumerate(offsets):
+            base = both * index + skip
+            blocks.append((ref.at[base : base + rows], me ^ offset))
+    for ref, offset in zip(others, mine + partner):
+        for step in range(1, nz):
+            blocks.append((ref.at[(step - 1) * rows : step * rows], me ^ (offset ^ (z * step))))
+    return blocks
+
+
+def fetch_blocks(blocks, place, sems):
     copies = []
-    for block, offset, own in blocks:
-        for source, target in place(block, me ^ offset, own):
+    for block, device in blocks:
+        for source, target in place(block, device):
             copies.append(pltpu.make_async_copy(source, target, sems.at[len(copies)]))
     return copies
 
 
-def send_block(me, dims, device, source, keep, send, sems):
+def exchange_slot(me, dims, device):
     (x, _), (core, _), (z, nz), (y, _) = dims
     odd = device // core % 2
     away = me ^ device
     across = [away // stride % 2 for stride in (x, y)]
     top = odd * across[0] + (1 - odd) * across[1]
     low = odd * across[1] + (1 - odd) * across[0]
-    slot = top * 2 * nz + low * nz + away // z % nz
-    far = away // core % 2
+    return away // z % nz * 4 + top * 2 + low, away // core % 2
+
+
+def send_block(me, dims, device, source, keep, send, sems):
+    slot, far = exchange_slot(me, dims, device)
     sem = sems.at[device]
 
     @pl.when(far == 0)
@@ -718,27 +742,54 @@
         pltpu.make_async_copy(source, send.at[slot], sem).start()
 
 
-def added(terms, start, stop):
-    total = terms[0][start:stop].astype(F32)
+def store_block(me, dims, device, block, keep, send):
+    slot, far = exchange_slot(me, dims, device)
+
+    @pl.when(far == 0)
+    def _():
+        keep[slot] = block[...]
+
+    @pl.when(far == 1)
+    def _():
+        send[slot] = block[...]
+
+
+def added(*terms):
+    total = terms[0].astype(F32)
     for term in terms[1:]:
-        total = total + term[start:stop].astype(F32)
+        total = total + term.astype(F32)
     return total
 
 
 def reduce_part(keep, send, dims, count):
     _, (core, _), (z, nz), _ = dims
-
-    terms = [keep, swap(send, core, count)]
-    for which in range(2):
-        half = terms[0].shape[0] // 2 if which == 0 else nz
-        got = swap_turn(added(terms, half, 2 * half).astype(BF), dims, which, count)
-        terms.append(got)
-        terms = [term[:half] for term in terms]
-    result = added(terms, 0, 1)[0]
+    rows, width = keep.shape[1:]
+
+    def sent(how, array, *offsets):
+        return how(array.astype(BF), *offsets, count)
+
+    def turned(which):
+        return lambda array, total: swap_turn(array, dims, which, total)
+
+    def gated(*tokens):
+        held = lax.optimization_barrier((keep, got, *tokens))[:2]
+        return [array.reshape(nz, 2, 2, rows, width) for array in held]
+
+    got = swap(send, core, count)
+    kept = gated()
+    far = sent(turned(0), added(*[a[1:, 1] for a in kept]).reshape(-1, rows, width))
+    own = sent(turned(0), added(*[a[0, 1] for a in kept]))
+    kept = gated(far)
+    far = far.reshape(nz - 1, 2, rows, width)
+    far_next = sent(turned(1), added(*[a[1:, 0, 1] for a in kept], far[:, 1]))
+    kept = gated(own, far_next)
+    own_next = sent(turned(1), added(*[a[0, 0, 1] for a in kept], own[1]))
+    kept = gated(far_next)
+    result = 0.0
     for step in range(1, nz):
-        got = swap(added(terms, step, step + 1)[0].astype(BF), z * step, count)
-        result = result + got.astype(F32)
-    return result
+        part = added(*[a[step, 0, 0] for a in kept], far[step - 1, 0], far_next[step - 1])
+        result = result + sent(swap, part, z * step).astype(F32)
+    return result + added(*[a[0, 0, 0] for a in kept], own[0], own_next)
 
 
 def vector_rows(read, width, segment, count):
@@ -766,7 +817,7 @@
 def project(me, length, text_in, layout_in, pieces, sizes, dims, middle):
     count, text_rows, layout_rows, text_vec, layout_vec = sizes
     rows = text_in.shape[0]
-    packed = pieces[2].shape[1]
+    packed = pieces[0].shape[0] // 4 - 2 * text_rows
 
     def body(*refs):
         me_ref, length_ref, x_ref, xl_ref = refs[:4]
@@ -792,14 +843,17 @@
             out_sems,
         ) = refs[4 + len(pieces) :]
 
-        def place(source, device, own):
+        def place(source, device):
             base = pl.multiple_of(device * text_rows, 16)
             return [
                 (source.at[0:text_rows], weight.at[pl.ds(base, text_rows)]),
                 (source.at[text_rows:packed], tail.at[device]),
             ]
 
-        copies = fetch_blocks(me_ref[0], dims, piece_refs, place, sems)
+        blocks = part_blocks(
+            me_ref[0], dims, piece_refs[:2], piece_refs[2:], 0, packed, packed + 2 * text_rows
+        )
+        copies = fetch_blocks(blocks, place, sems)
         for copy in copies:
             copy.start()
         for copy in copies:
@@ -995,12 +1049,15 @@
     return value * below, below + value * bell * (1.0 / math.sqrt(2.0 * math.pi))
 
 
-def feed_stream(norm_ref, vec_ref, cot_ref, keep, up, down, bias, hidden, slope, blocks, write, outs):
+def feed_stream(
+    norm_ref, vec_ref, cot_ref, keep, up, down, bias, arrived, hidden, slope, blocks, write, outs
+):
     out_ref, grad_ref, vec_out = outs
     first = norm_ref[...] * vec_ref[3] + vec_ref[4]
     low = first.astype(BF)
 
     def forward(block, total):
+        arrived(block)
         act, rise = gelu_both(nt(low, up(block)) + bias(block))
         act = act.astype(BF)
         hidden[block] = act
@@ -1034,79 +1091,46 @@
     grad_ref[...] = loop(backward, second)
 
 
-def feed(me, keep_rows, norm_t, norm_l, tv, lv, cot_t, cot_l, pieces, lu, ld, dims, text_rows):
+def feed(me, keep_rows, norm_t, tv, cot_t, pieces, dims, text_rows):
     rows = norm_t.shape[0]
     count = 8 * dims[2][1]
-    skip = pieces[0].shape[1] - 2 * text_rows
     blocks = FF // D
+    per_block = D // text_rows
+    both = pieces[0].shape[0] // 4
+    skip = both - 2 * text_rows
 
     def body(*refs):
-        me_ref, keep_ref, nt_ref, nl_ref, tv_ref, lv_ref, ct_ref, cl_ref, lu_ref, ld_ref = refs[:10]
-        piece_refs = refs[10 : 10 + len(pieces)]
+        me_ref, keep_ref, nt_ref, tv_ref, ct_ref = refs[:5]
+        piece_refs = refs[5 : 5 + len(pieces)]
         (
             out_t,
-            out_l,
             grad_t,
-            grad_l,
             vec_t,
-            vec_l,
-            lu_grad,
-            ld_grad,
             both_keep,
             both_send,
             up,
             down,
             hidden,
             slope,
-            hidden_l,
-            slope_l,
             grads,
+            weight_sems,
             sems,
-        ) = refs[10 + len(pieces) :]
+        ) = refs[5 + len(pieces) :]
         mine = me_ref[0]
-
-        def place(source, device, own):
+        listed = part_blocks(
+            mine, dims, piece_refs[:2], piece_refs[2:], skip, 2 * text_rows, both
+        )
+        for source, device in listed:
             at = pl.ds(pl.multiple_of(device * text_rows, 16), text_rows)
-            base = skip if own else 0
-            return [
-                (source.at[base : base + text_rows], up.at[at]),
-                (source.at[base + text_rows : base + 2 * text_rows], down.at[at]),
-            ]
-
-        copies = fetch_blocks(mine, dims, piece_refs, place, sems)
-        for copy in copies:
-            copy.start()
-        keep = keep_ref[...]
-
-        def whole(ref):
-            return lambda block: ref[...]
-
-        parts = FFL // DL
-        bias_l = jnp.concatenate([lv_ref[8 + part] for part in range(parts)], 1)
-
-        def write_l(block, one, two, bias):
-            lu_grad[...] = one.astype(BF)
-            ld_grad[...] = two.astype(BF)
-            for part in range(parts):
-                vec_l[3 + part] = bias[:, part * DL : (part + 1) * DL]
-
-        feed_stream(
-            nl_ref,
-            lv_ref,
-            cl_ref,
-            keep,
-            whole(lu_ref),
-            whole(ld_ref),
-            lambda block: bias_l,
-            hidden_l,
-            slope_l,
-            1,
-            write_l,
-            (out_l, grad_l, vec_l),
-        )
-        for copy in copies:
-            copy.wait()
-        per_block = D // text_rows
+            sem = weight_sems.at[device]
+            pltpu.make_async_copy(source.at[0:text_rows], up.at[at], sem).start()
+            pltpu.make_async_copy(source.at[text_rows:], down.at[at], sem).start()
+
+        def arrived(block):
+            for part in range(per_block):
+                sem = weight_sems.at[block * per_block + part]
+                for ref in (up, down):
+                    pltpu.make_async_copy(ref.at[0:text_rows], ref.at[0:text_rows], sem).wait()
 
         def rows_of(ref):
             return lambda block: ref[pl.ds(pl.multiple_of(block * D, 16), D), :]
@@ -1124,10 +1148,11 @@
             nt_ref,
             tv_ref,
             ct_ref,
-            keep,
+            keep_ref[...],
             rows_of(up),
             rows_of(down),
             lambda block: tv_ref[8 + block],
+            arrived,
             hidden,
             slope,
             blocks,
@@ -1142,13 +1167,8 @@
         body,
         [
             ((rows, D), BF, VMEM_SPEC),
-            ((rows, DL), BF, VMEM_SPEC),
             ((rows, D), F32, VMEM_SPEC),
-            ((rows, DL), F32, VMEM_SPEC),
             ((3 + blocks, 1, D), F32, VMEM_SPEC),
-            ((3 + blocks, 1, DL), F32, VMEM_SPEC),
-            ((FFL, DL), BF, VMEM_SPEC),
-            ((FFL, DL), BF, VMEM_SPEC),
             part,
             part,
         ],
@@ -1156,13 +1176,8 @@
             (me, SMEM_SPEC),
             (keep_rows, STAGED),
             (norm_t, STAGED),
-            (norm_l, STAGED),
             (tv, VMEM_SPEC),
-            (lv, VMEM_SPEC),
             (cot_t, STAGED),
-            (cot_l, STAGED),
-            (lu, STAGED),
-            (ld, STAGED),
         ]
         + [(array, ANY_SPEC) for array in pieces],
         [
@@ -1170,33 +1185,39 @@
             pltpu.VMEM((FF, D), BF),
             pltpu.VMEM((blocks, rows, D), BF),
             pltpu.VMEM((blocks, rows, D), F32),
-            pltpu.VMEM((1, rows, FFL), BF),
-            pltpu.VMEM((1, rows, FFL), F32),
             pltpu.VMEM((count, 2 * text_rows, D), BF),
-            pltpu.SemaphoreType.DMA((2 * count,)),
+            pltpu.SemaphoreType.DMA((count,)),
+            pltpu.SemaphoreType.DMA((count,)),
         ],
-        room=60,
-    )
-
-
-def close_back_pair(grad_t, grad_l, norms, outs, weight, layout_w, tv, lv):
-    rows = grad_t.shape[0]
-    norm_t, inv_t, norm_l, inv_l = norms
-    out_t, out_l = outs
+    )
+
+
+def close_back_pair(keep_rows, layout_feed, text_side, layout_side, weight, layout_w, tv, lv):
+    norm_l, cot_l, lu, ld = layout_feed
+    rows = norm_l.shape[0]
+    parts = FFL // DL
 
     def body(
+        settle,
+        keep_ref,
+        nl_ref,
+        cl_ref,
+        lu_ref,
+        ld_ref,
+        il_ref,
+        ol_ref,
         gt_ref,
-        gl_ref,
         nt_ref,
         it_ref,
-        nl_ref,
-        il_ref,
         ot_ref,
-        ol_ref,
+        layout_ref,
         weight_any,
-        layout_ref,
         tv_ref,
         lv_ref,
+        out_l,
+        feed_l,
+        lu_grad,
+        ld_grad,
         resid_t,
         resid_l,
         out_wt,
@@ -1204,11 +1225,38 @@
         vec_t,
         vec_l,
         dout,
+        gl_ref,
+        hidden_l,
+        slope_l,
         weight,
         sem,
     ):
         fetch = pltpu.make_async_copy(weight_any.at[3 * D : 4 * D], weight, sem)
         fetch.start()
+        bias_l = jnp.concatenate([lv_ref[8 + part] for part in range(parts)], 1)
+
+        def write_l(block, one, two, bias):
+            lu_grad[...] = one.astype(BF)
+            ld_grad[...] = two.astype(BF)
+            for part in range(parts):
+                feed_l[3 + part] = bias[:, part * DL : (part + 1) * DL]
+
+        feed_stream(
+            nl_ref,
+            lv_ref,
+            cl_ref,
+            keep_ref[...],
+            lambda block: lu_ref[...],
+            lambda block: ld_ref[...],
+            lambda block: bias_l,
+            lambda block: None,
+            hidden_l,
+            slope_l,
+            1,
+            write_l,
+            (out_l, gl_ref, feed_l),
+        )
+        settle()
 
         def close(grad, scaled, inverse, vec, mixed, vec_out, resid_ref, wide):
             vec_out[1] = col_sum(grad * scaled)
@@ -1246,6 +1294,10 @@
     return kernel_call(
         body,
         [
+            ((rows, DL), BF, VMEM_SPEC),
+            ((3 + parts, 1, DL), F32, VMEM_SPEC),
+            ((FFL, DL), BF, VMEM_SPEC),
+            ((FFL, DL), BF, VMEM_SPEC),
             ((rows, D), F32, VMEM_SPEC),
             ((rows, DL), F32, VMEM_SPEC),
             ((D, D), BF, VMEM_SPEC),
@@ -1254,22 +1306,16 @@
             ((3, 1, DL), F32, VMEM_SPEC),
             ((HEADS, rows, CAT), BF, VMEM_SPEC),
         ],
+        [(array, STAGED) for array in (keep_rows, norm_l, cot_l, lu, ld)]
+        + [(array, LATE) for array in (*layout_side, *text_side, layout_w)]
+        + [(weight, ANY_SPEC), (tv, VMEM_SPEC), (lv, VMEM_SPEC)],
         [
-            (grad_t, STAGED),
-            (grad_l, STAGED),
-            (norm_t, STAGED),
-            (inv_t, STAGED),
-            (norm_l, STAGED),
-            (inv_l, STAGED),
-            (out_t, STAGED),
-            (out_l, STAGED),
-            (weight, ANY_SPEC),
-            (layout_w, STAGED),
-            (tv, VMEM_SPEC),
-            (lv, VMEM_SPEC),
+            pltpu.VMEM((rows, DL), F32),
+            pltpu.VMEM((1, rows, FFL), BF),
+            pltpu.VMEM((1, rows, FFL), F32),
+            pltpu.VMEM((D, D), BF),
+            pltpu.SemaphoreType.DMA,
         ],
-        [pltpu.VMEM((D, D), BF), pltpu.SemaphoreType.DMA],
-        room=60,
     )
 
 
@@ -1351,7 +1397,6 @@
             send,
             pack,
             att_l,
-            sems,
         ) = refs[3 + 3 * groups :]
         mine = me_ref[0]
         x, xl = x_ref[...], xl_ref[...]
@@ -1360,19 +1405,11 @@
             pack[device, text_rows : text_rows + layout_rows, :] = jnp.zeros((layout_rows, D), BF)
         per_block = D // text_rows
         for index in range(3):
-            pieces = [heads_out(back_refs[3 * group + index], 0, back_refs[3 * group + index].shape[0]) for group in range(groups)]
+            refs_of = [back_refs[3 * group + index] for group in range(groups)]
+            pieces = [heads_out(ref, 0, ref.shape[0]) for ref in refs_of]
             joined_t[index] = jnp.concatenate([text for text, _ in pieces], 1)
             joined_l[index] = jnp.concatenate([layout for _, layout in pieces], 1)
-            grad = tn(x, joined_t[index]).astype(BF)
-            for part in range(per_block):
-                pack[index * per_block + part, 0:text_rows, :] = grad[
-                    part * text_rows : (part + 1) * text_rows
-                ]
             att_l[index * DL : (index + 1) * DL, :] = tn(xl, joined_l[index]).astype(BF)
-        for part in range(per_block):
-            pack[3 * per_block + part, 0:text_rows, :] = out_wt[
-                part * text_rows : (part + 1) * text_rows, :
-            ]
         att_l[3 * DL : 4 * DL, :] = out_wl[...]
         for device in range(count):
             block = pl.ds(device * layout_rows, layout_rows)
@@ -1409,12 +1446,19 @@
             pack[device, text_rows + layout_rows :, :] = jnp.where(
                 row == 0, jnp.broadcast_to(line, (8, D)), 0.0
             ).astype(BF)
-        for device in range(count):
-            send_block(mine, dims, device, pack.at[device], keep, send, sems)
-        for device in range(count):
-            pltpu.make_async_copy(pack.at[device], keep.at[0], sems.at[device]).wait()
-
-    part = ((count // 2, packed, D), BF, ANY_SPEC)
+        for index in (3, 0, 1, 2):
+            grad = out_wt[...] if index == 3 else tn(x, joined_t[index]).astype(BF)
+            for part in range(per_block):
+                device = index * per_block + part
+                pack[device, 0:text_rows, :] = grad[part * text_rows : (part + 1) * text_rows]
+
+        def place(device, carry):
+            store_block(mine, dims, device, pack.at[device], keep, send)
+            return carry
+
+        lax.fori_loop(0, count, place, 0)
+
+    part = ((count // 2, packed, D), BF, VMEM_SPEC)
     arrays = []
     for back in backs:
         arrays += list(back)
@@ -1427,9 +1471,8 @@
         [
             pltpu.VMEM((count, packed, D), BF),
             pltpu.VMEM((4 * DL, DL), BF),
-            pltpu.SemaphoreType.DMA((count,)),
         ],
-        room=60,
+        room=22,
     )
 
 
@@ -1488,12 +1531,10 @@
     ).astype(BF)
     sizes = (count, text_rows, layout_rows, text_vec, layout_vec)
     feed_shard = jnp.concatenate([text_up.T, text_down], 0).astype(BF)
-    own = gather_own(jnp.concatenate([packed, feed_shard], 0), shape)
-    parts = own + gather_pieces(packed, shape)
-    feed_parts = own + gather_pieces(feed_shard, shape)
+    own, first_parts, second_parts = gather_parts(packed, feed_shard, shape)
     middle = HEADS // 2
     q, k, v, weight, layout_w, lu, ld, tv, lv, first, lse_a = project(
-        me, lengths, text_in, layout_in, parts, sizes, dims, middle
+        me, lengths, text_in, layout_in, own + first_parts, sizes, dims, middle
     )
     out_t, out_l, lse_b, norm_t, inv_t, norm_l, inv_l = attend(
         text_in, layout_in, q, k, v, first, weight, layout_w, tv, lv
@@ -1501,34 +1542,37 @@
     span = text_in.shape[0]
     keep = (jnp.arange(span) < lengths[0]) & (dup_rows == 0)
     keep = keep.astype(F32)[:, None]
+    text_final, grad_t, feed_vt, both_keep, both_send = feed(
+        me,
+        keep,
+        norm_t,
+        tv,
+        text_cotangent,
+        own + second_parts,
+        dims,
+        text_rows,
+    )
     (
-        text_final,
         layout_final,
-        grad_t,
-        grad_l,
-        feed_vt,
         feed_vl,
         lu_grad,
         ld_grad,
-        both_keep,
-        both_send,
-    ) = feed(
-        me,
+        resid_t,
+        resid_l,
+        out_wt,
+        out_wl,
+        close_t,
+        close_l,
+        dout,
+    ) = close_back_pair(
         keep,
-        norm_t,
-        norm_l,
+        (norm_l, layout_cotangent, lu, ld),
+        (grad_t, norm_t, inv_t, out_t),
+        (inv_l, out_l),
+        weight,
+        layout_w,
         tv,
         lv,
-        text_cotangent,
-        layout_cotangent,
-        feed_parts,
-        lu,
-        ld,
-        dims,
-        text_rows,
-    )
-    resid_t, resid_l, out_wt, out_wl, close_t, close_l, dout = close_back_pair(
-        grad_t, grad_l, (norm_t, inv_t, norm_l, inv_l), (out_t, out_l), weight, layout_w, tv, lv
     )
     backs = [
         heads_back(q, k, v, lse_a, dout, 0, middle), heads_back(q, k, v, lse_b, dout, middle, HEADS)
@@ -1573,7 +1617,7 @@
     (_, nx), (_, ncore), (_, nz), (_, ny) = exchange_dims(shape)
     count = shape["gx"] * shape["gy"]
     return (
-        (nx, ncore, ny) == (2, 2, 2)
+        (nx, ncore, ny, nz) == (2, 2, 2, 4)
         and (4 * D) % (16 * count) == 0
         and (4 * DL) % (8 * count) == 0
         and D % (4 * D // count) == 0

time: 338 us -> 313 us (0.926)
  waiting for transfers between devices: 128 us -> 112 us
  local copies, waits for them, and re-layouts: 24.4 us -> 12.4 us
  Pallas kernels: 110 us -> 101 us
  starting transfers between devices: 52.4 us -> 59.2 us
  other arithmetic: 20.7 us -> 25 us
    ppermute x13 -> x17, waiting for transfers between devices: 77 us -> 58.7 us  [swap_turn(): lax.ppermute(array, AXES, [(device, device ^ turn(dims, device // core %...]
    unnamed x78 -> x74, local copies, waits for them, and re-layouts: 20.1 us -> 8.11 us
    pallas_call x11, Pallas kernels: 110 us -> 101 us  [kernel_call(): pl.pallas_call(with_copies if copied else body, out_shape=[jax.ShapeDtype...]
    convert_element_type x6 -> x10, other arithmetic: 11.1 us -> 15.9 us  [sent(): return how(array.astype(BF), *offsets, count)]
    ppermute x13 -> x17, starting transfers between devices: 18.2 us -> 21.8 us  [swap_turn(): lax.ppermute(array, AXES, [(device, device ^ turn(dims, device // core %...]
  transfers between devices with their start and end apart: 36 -> 40, of which waited for: 16 -> 16; matrix products, arithmetic and copies ran while one was open for 7% -> 9% of each run, Pallas kernels for 21% -> 22%
where the time goes in v2:
time: 313 us; the launch traced here: 312 us
  waiting for transfers between devices  112 us (36%)
  Pallas kernels  101 us (32%)
  starting transfers between devices  59.2 us (19%)
  other arithmetic  25 us (8%)
  local copies, waits for them, and re-layouts  12.4 us (4%)
    pallas_call x11, Pallas kernels, kernel_call(): pl.pallas_call(with_copies if copied else body, out_shape=[jax.ShapeDtype...  101 us
    ppermute x17, waiting for transfers between devices, swap_turn(): lax.ppermute(array, AXES, [(device, device ^ turn(dims, device // core %...  58.7 us
    ppermute x23, waiting for transfers between devices, swap(): lax.ppermute(array, AXES, [(device, device ^ offset) for device in range(...  52.9 us
    ppermute x23, starting transfers between devices, swap(): lax.ppermute(array, AXES, [(device, device ^ offset) for device in range(...  37.4 us
    ppermute x17, starting transfers between devices, swap_turn(): lax.ppermute(array, AXES, [(device, device ^ turn(dims, device // core %...  21.8 us
    convert_element_type x10, other arithmetic, sent(): return how(array.astype(BF), *offsets, count)  15.9 us
    unnamed x74, local copies, waits for them, and re-layouts  8.11 us
  transfers between devices with their start and end apart: 40, of which 16 were waited for; matrix products, arithmetic and copies ran while one was open for 9% of the time, Pallas kernels for 22%

profile of v2, /device:TPU:0, one launch (start us, length us, event | category | flops | bytes accessed | tf_op | source)
XLA Modules:
  0.0 311.7 jit_solution(4902295763390782202)
XLA Ops:
  5.3 3.1 %collective-permute-start.4 = (bf16[128,768]{1,0:T(8,128)(2,1)S(1)}, bf16[128,768]{1,0:T(8,128)(2,1)S(1)}, u32[]{:S(2)}, u32[]{:S(2)}) collective-permute-start(bf16[128,768]{1,0:T(8,128)(2,1)S(1)} %pad.27), channel_id=1, source_target_pairs={{0,2},{1,3},{2,0},{3,1},{4,6},{5,7},{6,4},{7,5},{8,10},{9,11},{10,... | collective-permute-start | bytes 589832 | tf_op jit(solution)/shard_map/ppermute | solution.py:42
  8.4 2.6 collective-permute-start.5
  13.0 1.8 collective-permute-start
  15.6 1.6 collective-permute-done.4.refs_0_
  17.2 1.9 collective-permute-start.15
  19.1 6.5 %collective-permute-done.5.refs_1_ = bf16[128,768]{1,0:T(8,128)(2,1)S(1)} collective-permute-done((bf16[128,768]{1,0:T(8,128)(2,1)S(1)}, bf16[128,768]{1,0:T(8,128)(2,1)S(1)}, u32[]{:S(2)}, u32[]{:S(2)}) %collective-permute-start.5) | collective-permute-done | bytes 196640 | tf_op jit(solution)/shard_map/ppermute | solution.py:42
  25.6 2.5 collective-permute-start.16
  28.1 1.5 collective-permute-start.1
  30.3 1.6 collective-permute-start.7
  31.9 16.8 %collective-permute-done.15.refs_1_ = bf16[192,768]{1,0:T(8,128)(2,1)S(1)} collective-permute-done((bf16[192,768]{1,0:T(8,128)(2,1)S(1)}, bf16[192,768]{1,0:T(8,128)(2,1)S(1)}, u32[]{:S(2)}, u32[]{:S(2)}) %collective-permute-start.15) | collective-permute-done | bytes 294944 | tf_op jit(solution)/shard_map/ppermute | solution.py:42
  49.0 1.6 collective-permute-start.17
  50.6 1.5 collective-permute-start.8
  52.6 1.5 collective-permute-start.18
  54.1 16.0 %collective-permute-done.2.refs_3_ = bf16[320,768]{1,0:T(8,128)(2,1)S(1)} collective-permute-done((bf16[320,768]{1,0:T(8,128)(2,1)S(1)}, bf16[320,768]{1,0:T(8,128)(2,1)S(1)}, u32[]{:S(2)}, u32[]{:S(2)}) %collective-permute-start.2) | collective-permute-done | bytes 491552 | tf_op jit(solution)/shard_map/ppermute | solution.py:660
  70.1 1.5 collective-permute-start.9
  71.6 1.3 shard_map.229.refs_4_.refs_5_
  74.8 4.9 %collective-permute-done.18.refs_9_ = bf16[576,768]{1,0:T(8,128)(2,1)} collective-permute-done((bf16[576,768]{1,0:T(8,128)(2,1)S(1)}, bf16[576,768]{1,0:T(8,128)(2,1)}, u32[]{:S(2)}, u32[]{:S(2)}) %collective-permute-start.18) | collective-permute-done | bytes 884768 | tf_op jit(solution)/shard_map/ppermute | solution.py:660
  79.7 1.2 collective-permute-start.12
  80.9 5.0 %collective-permute-done.9.refs_9_ = bf16[384,768]{1,0:T(8,128)(2,1)S(1)} collective-permute-done((bf16[384,768]{1,0:T(8,128)(2,1)S(1)}, bf16[384,768]{1,0:T(8,128)(2,1)S(1)}, u32[]{:S(2)}, u32[]{:S(2)}) %collective-permute-start.9) | collective-permute-done | bytes 589856 | tf_op jit(solution)/shard_map/ppermute | solution.py:660
  85.9 1.4 collective-permute-start.13
  89.3 6.1 %collective-permute-done.19.refs_10_ = bf16[576,768]{1,0:T(8,128)(2,1)} collective-permute-done((bf16[576,768]{1,0:T(8,128)(2,1)}, bf16[576,768]{1,0:T(8,128)(2,1)}, u32[]{:S(2)}, u32[]{:S(2)}) %collective-permute-start.19) | collective-permute-done | bytes 884768 | tf_op jit(solution)/shard_map/ppermute | solution.py:660
  95.5 1.0 collective-permute-start.23
  96.5 1.8 copy.37.refs_3_.refs_1_.refs_2_
  99.8 13.5 %shard_map.231 = (bf16[12,512,128]{2,1,0:T(8,128)(2,1)}, bf16[12,512,128]{2,1,0:T(8,128)(2,1)}, bf16[12,512,128]{2,1,0:T(8,128)(2,1)}, bf16[3072,768]{1,0:T(8,12...) custom-call(s32[1]{0:T(128)} %bitcast.refs_0_, ...), custom_call_target="tpu_custom_call" | custom-call | tf_op jit(solution)/shard_map/pallas_call | solution.py:617
  113.3 12.3 %shard_map.232 = (bf16[512,768]{1,0:T(8,128)(2,1)}, bf16[512,192]{1,0:T(8,128)(2,1)}, f32[6,1,512]{2,1,0:T(1,128)}, f32[512,768]{1,0:T(8,128)}, f32[512,1]{1,0:T...) custom-call(bf16[512,768]{1,0:T(8,128)(2,1)} %refs_1_.3, bf16[512,192]{1,0:T(8,128)(2,1)} %copy.37.refs_3_.refs_1_.refs_2_, ...), custom_call_target="tpu_custom_call" | custom-call | tf_op jit(solution)/shard_map/pallas_call | solution.py:617
  125.7 33.1 %shard_map.234 = (bf16[512,768]{1,0:T(8,128)(2,1)}, f32[512,768]{1,0:T(8,128)}, f32[7,1,768]{2,1,0:T(1,128)}, bf16[16,192,768]{2,1,0:T(8,128)(2,1)}, bf16[16,192,768]{2,1,0:T(8,128)(2,1)}) custom-call(s32[1]{0:T(128)} %bitcast.refs_0_, f32[512,1]{1,0:T(8,128)} %copy.38.refs_1_.refs_0_, f32[512,768]{1,0:T(8,128)} %get-tuple-element.82.refs_2_.refs_8_, ...), custom_call_target="tpu_custom_call" | custom-call | tf_op jit(solution)/shard_map/pallas_call | solution.py:617
  158.8 1.1 collective-permute-start.32
  160.8 11.0 %shard_map.235 = (bf16[512,192]{1,0:T(8,128)(2,1)}, f32[7,1,192]{2,1,0:T(1,128)}, bf16[768,192]{1,0:T(8,128)(2,1)}, bf16[768,192]{1,0:T(8,128)(2,1)}, f32[512,76...) custom-call(f32[512,1]{1,0:T(8,128)} %copy.38.refs_1_.refs_0_, ...), custom_call_target="tpu_custom_call" | custom-call | tf_op jit(solution)/shard_map/pallas_call | solution.py:617
  171.8 1.4 copy-done.3
  173.2 1.4 copy-done.5
  174.6 9.6 %shard_map.237 = (bf16[6,512,128]{2,1,0:T(8,128)(2,1)S(1)}, bf16[6,512,128]{2,1,0:T(8,128)(2,1)S(1)}, bf16[6,512,128]{2,1,0:T(8,128)(2,1)S(1)}) custom-call(bf16[12,512,128]{2,1,0:T(8,128)(2,1)S(1)} %copy-done.1, bf16[12,512,128]{2,1,0:T(8,128)(2,1)S(1)} %copy-done.2, bf16[12,512,128]{2,1,0:T(8,128)(2,1)S(1)} %copy-done.3, f32[6,1,512]{2,1,0:T(1,128)S(1)} %copy-done.18, ...), custom_call_target="tpu_custom_call" | custom-call | tf_op jit(solution)/shard_map/pallas_call | solution.py:617
  184.3 9.4 %shard_map.236 = (bf16[6,512,128]{2,1,0:T(8,128)(2,1)S(1)}, bf16[6,512,128]{2,1,0:T(8,128)(2,1)S(1)}, bf16[6,512,128]{2,1,0:T(8,128)(2,1)S(1)}) custom-call(bf16[12,512,128]{2,1,0:T(8,128)(2,1)S(1)} %copy-done.1, bf16[12,512,128]{2,1,0:T(8,128)(2,1)S(1)} %copy-done.2, bf16[12,512,128]{2,1,0:T(8,128)(2,1)S(1)} %copy-done.3, f32[6,1,512]{2,1,0:T(1,128)S(1)} %copy-done.17, ...), custom_call_target="tpu_custom_call" | custom-call | tf_op jit(solution)/shard_map/pallas_call | solution.py:617
  193.8 5.8 %shard_map.238 = (bf16[3,512,768]{2,1,0:T(8,128)(2,1)S(1)}, bf16[3,512,192]{2,1,0:T(8,128)(2,1)S(1)}, bf16[16,128,768]{2,1,0:T(8,128)(2,1)S(1)}, bf16[16,128,768]{2,1,0:T(8,128)(2,1)S(1)}) custom-call(s32[1]{0:T(128)} %bitcast.refs_0_, bf16[512,768]{1,0:T(8,128)(2,1)S(1)} %copy-done.4, bf16[512,192]{1,0:T(8,128)(2,1)S(1)} %copy-done.6, ...), custom_call_target="tpu_custom_call" | custom-call | tf_op jit(solution)/shard_map/pallas_call | solution.py:617
  199.8 5.6 %collective-permute-done.24 = bf16[16,128,768]{2,1,0:T(8,128)(2,1)S(1)} collective-permute-done((bf16[16,128,768]{2,1,0:T(8,128)(2,1)S(1)}, bf16[16,128,768]{2,1,0:T(8,128)(2,1)S(1)}, u32[]{:S(2)}, u32[]{:S(2)}) %collective-permute-start.24) | collective-permute-done | bytes 3145760 | tf_op jit(solution)/shard_map/ppermute | solution.py:42
  205.7 1.6 collective-permute-start.25
  207.3 3.8 %add_convert_fusion = bf16[3,1,2,192,768]{4,3,2,1,0:T(8,128)(2,1)} fusion(bf16[4,2,2,192,768]{4,3,2,1,0:T(8,128)(2,1)} %bitcast.32, bf16[4,2,2,192,768]{4,3,2,1,0:T(8,128)(2,1)} %bitcast.176), kind=kLoop, calls=%fused_computation | loop fusion | flops 3538944 | bytes 5308416 | tf_op jit(solution)/shard_map/convert_element_type | solution.py:769
  211.7 10.3 %collective-permute-done.25 = bf16[6,128,768]{2,1,0:T(8,128)(2,1)S(1)} collective-permute-done((bf16[6,128,768]{2,1,0:T(8,128)(2,1)S(1)}, bf16[6,128,768]{2,1,0:T(8,128)(2,1)S(1)}, u32[]{:S(2)}, u32[]{:S(2)}) %collective-permute-start.25) | collective-permute-done | bytes 1179680 | tf_op jit(solution)/shard_map/ppermute | solution.py:660
  222.0 1.2 fusion.1
  223.2 1.4 collective-permute-start.26
  225.6 1.5 collective-permute-start.30
  227.1 4.6 %shard_map.239 = (bf16[512,768]{1,0:T(8,128)(2,1)}, bf16[512,192]{1,0:T(8,128)(2,1)S(1)}) custom-call(bf16[3,512,768]{2,1,0:T(8,128)(2,1)S(1)} %get-tuple-element.110.refs_0_, bf16[3,512,192]{2,1,0:T(8,128)(2,1)S(1)} %get-tuple-element.111.refs_1_, f32[512,768]{1,0:T(8,128)S(1)} %copy-done.10, f32[512,192]{1,0:T(8,128)S(1)} %copy-done.12, ...), custom_call_target="tpu_custom_call" | custom-call | tf_op jit(solution)/shard_map/pallas_call | solution.py:617
  232.5 1.8 copy.46
  234.2 5.5 %collective-permute-done.26 = bf16[3,128,768]{2,1,0:T(8,128)(2,1)} collective-permute-done((bf16[3,128,768]{2,1,0:T(8,128)(2,1)}, bf16[3,128,768]{2,1,0:T(8,128)(2,1)}, u32[]{:S(2)}, u32[]{:S(2)}) %collective-permute-start.26) | collective-permute-done | bytes 589856 | tf_op jit(solution)/shard_map/ppermute | solution.py:660
  239.8 1.8 fusion.15
  241.6 6.9 %collective-permute-start.27 = (bf16[128,768]{1,0:T(8,128)(2,1)S(1)}, bf16[128,768]{1,0:T(8,128)(2,1)S(1)}, u32[]{:S(2)}, u32[]{:S(2)}) collective-permute-start(bf16[128,768]{1,0:T(8,128)(2,1)S(1)} %get-tuple-element.163), channel_id=1, source_target_pairs={{0,2},{1,3},{2,0},{3,1},{4,6},{5,7},{6,4},{7,5},{8,10},{9,11},{10,... | collective-permute-start | bytes 589832 | tf_op jit(solution)/shard_map/ppermute | solution.py:42
  248.5 1.1 collective-permute-start.28
  249.6 1.4 collective-permute-start.29
  251.6 2.0 fusion
  253.6 1.5 collective-permute-start.34
  255.1 1.1 fusion.10
  256.9 1.4 fusion.2
  258.3 1.6 collective-permute-start.38
  259.9 5.1 %collective-permute-done.28 = bf16[128,768]{1,0:T(8,128)(2,1)S(1)} collective-permute-done((bf16[128,768]{1,0:T(8,128)(2,1)S(1)}, bf16[128,768]{1,0:T(8,128)(2,1)S(1)}, u32[]{:S(2)}, u32[]{:S(2)}) %collective-permute-start.28) | collective-permute-done | bytes 196640 | tf_op jit(solution)/shard_map/ppermute | solution.py:42
  264.9 10.2 %collective-permute-done.31 = bf16[128,768]{1,0:T(8,128)(2,1)S(1)} collective-permute-done((bf16[128,768]{1,0:T(8,128)(2,1)S(1)}, bf16[128,768]{1,0:T(8,128)(2,1)S(1)}, u32[]{:S(2)}, u32[]{:S(2)}) %collective-permute-start.31) | collective-permute-done | bytes 196640 | tf_op jit(solution)/shard_map/ppermute | solution.py:660
  275.2 1.2 fusion.12
  277.7 2.1 fusion.8
  279.8 6.9 %collective-permute-start.35 = (bf16[192,768]{1,0:T(8,128)(2,1)S(1)}, bf16[192,768]{1,0:T(8,128)(2,1)S(1)}, u32[]{:S(2)}, u32[]{:S(2)}) collective-permute-start(bf16[192,768]{1,0:T(8,128)(2,1)S(1)} %get-tuple-element.160), channel_id=1, source_target_pairs={{0,2},{1,3},{2,0},{3,1},{4,6},{5,7},{6,4},{7,5},{8,10},{9,11},{10,... | collective-permute-start | bytes 884744 | tf_op jit(solution)/shard_map/ppermute | solution.py:42
  286.7 1.1 collective-permute-start.36
  287.9 1.4 collective-permute-start.37
  289.3 1.2 fusion.3
  290.4 1.5 collective-permute-start.39
  293.2 2.4 collective-permute-done.35
  295.5 14.0 %collective-permute-done.36 = bf16[192,768]{1,0:T(8,128)(2,1)S(1)} collective-permute-done((bf16[192,768]{1,0:T(8,128)(2,1)S(1)}, bf16[192,768]{1,0:T(8,128)(2,1)S(1)}, u32[]{:S(2)}, u32[]{:S(2)}) %collective-permute-start.36) | collective-permute-done | bytes 294944 | tf_op jit(solution)/shard_map/ppermute | solution.py:42
  309.5 1.3 fusion.5
  (135 shorter events, 21.9 us)
Async XLA Ops:
  5.3 11.9 %collective-permute-start.4 = (bf16[128,768]{1,0:T(8,128)(2,1)S(1)}, bf16[128,768]{1,0:T(8,128)(2,1)S(1)}, u32[]{:S(2)}, u32[]{:S(2)}) collective-permute-start(bf16[128,768]{1,0:T(8,128)(2,1)S(1)} %pad.27), channel_id=1, source_target_pairs={{0,2},{1,3},{2,0},{3,1},{4,6},{5,7},{6,4},{7,5},{8,10},{9,11},{10,... | collective-permute-start | bytes 589832 | tf_op jit(solution)/shard_map/ppermute | solution.py:42
  8.4 17.1 %collective-permute-start.5 = (bf16[128,768]{1,0:T(8,128)(2,1)S(1)}, bf16[128,768]{1,0:T(8,128)(2,1)S(1)}, u32[]{:S(2)}, u32[]{:S(2)}) collective-permute-start(bf16[128,768]{1,0:T(8,128)(2,1)S(1)} %pad.27), channel_id=1, source_target_pairs={{0,4},{1,5},{2,6},{3,7},{4,0},{5,1},{6,2},{7,3},{8,12},{9,13},{10,... | collective-permute-start | bytes 589832 | tf_op jit(solution)/shard_map/ppermute | solution.py:42
  11.0 17.0 %collective-permute-start.6 = (bf16[128,768]{1,0:T(8,128)(2,1)S(1)}, bf16[128,768]{1,0:T(8,128)(2,1)S(1)}, u32[]{:S(2)}, u32[]{:S(2)}) collective-permute-start(bf16[128,768]{1,0:T(8,128)(2,1)S(1)} %pad.27), channel_id=1, source_target_pairs={{0,6},{1,7},{2,4},{3,5},{4,2},{5,3},{6,0},{7,1},{8,14},{9,15},{10,... | collective-permute-start | bytes 589832 | tf_op jit(solution)/shard_map/ppermute | solution.py:42
  13.0 39.0 %collective-permute-start = (bf16[320,768]{1,0:T(8,128)(2,1)S(1)}, bf16[320,768]{1,0:T(8,128)(2,1)S(1)}, u32[]{:S(2)}, u32[]{:S(2)}) collective-permute-start(bf16[320,768]{1,0:T(8,128)(2,1)S(1)} %pad_maximum_fusion.refs_0_), channel_id=1, source_target_pairs={{0,1},{1,0},{2,3},{3,2},{4,5},{5,4},{6,7},{7,6},{8,24},{9,25},{10,... | collective-permute-start | bytes 1474568 | tf_op jit(solution)/shard_map/ppermute | solution.py:660
  14.9 15.5 %collective-permute-start.14 = (bf16[192,768]{1,0:T(8,128)(2,1)S(1)}, bf16[192,768]{1,0:T(8,128)(2,1)S(1)}, u32[]{:S(2)}, u32[]{:S(2)}) collective-permute-start(bf16[192,768]{1,0:T(8,128)(2,1)S(1)} %pad_maximum_fusion.1), channel_id=1, source_target_pairs={{0,2},{1,3},{2,0},{3,1},{4,6},{5,7},{6,4},{7,5},{8,10},{9,11},{10,... | collective-permute-start | bytes 884744 | tf_op jit(solution)/shard_map/ppermute | solution.py:42
  17.2 31.5 %collective-permute-start.15 = (bf16[192,768]{1,0:T(8,128)(2,1)S(1)}, bf16[192,768]{1,0:T(8,128)(2,1)S(1)}, u32[]{:S(2)}, u32[]{:S(2)}) collective-permute-start(bf16[192,768]{1,0:T(8,128)(2,1)S(1)} %pad_maximum_fusion.1), channel_id=1, source_target_pairs={{0,4},{1,5},{2,6},{3,7},{4,0},{5,1},{6,2},{7,3},{8,12},{9,13},{10,... | collective-permute-start | bytes 884744 | tf_op jit(solution)/shard_map/ppermute | solution.py:42
  25.6 23.2 %collective-permute-start.16 = (bf16[192,768]{1,0:T(8,128)(2,1)S(1)}, bf16[192,768]{1,0:T(8,128)(2,1)S(1)}, u32[]{:S(2)}, u32[]{:S(2)}) collective-permute-start(bf16[192,768]{1,0:T(8,128)(2,1)S(1)} %pad_maximum_fusion.1), channel_id=1, source_target_pairs={{0,6},{1,7},{2,4},{3,5},{4,2},{5,3},{6,0},{7,1},{8,14},{9,15},{10,... | collective-permute-start | bytes 884744 | tf_op jit(solution)/shard_map/ppermute | solution.py:42
  28.1 24.6 %collective-permute-start.1 = (bf16[320,768]{1,0:T(8,128)(2,1)S(1)}, bf16[320,768]{1,0:T(8,128)(2,1)S(1)}, u32[]{:S(2)}, u32[]{:S(2)}) collective-permute-start(bf16[320,768]{1,0:T(8,128)(2,1)S(1)} %pad_maximum_fusion.refs_0_), channel_id=1, source_target_pairs={{0,16},{1,17},{2,18},{3,19},{4,20},{5,21},{6,22},{7,23},{8,9},{9,8... | collective-permute-start | bytes 1474568 | tf_op jit(solution)/shard_map/ppermute | solution.py:660
  30.3 42.6 %copy-start.9 = (bf16[384,768]{1,0:T(8,128)(2,1)}, bf16[384,768]{1,0:T(8,128)(2,1)S(1)}, u32[]{:S(2)}) copy-start(bf16[384,768]{1,0:T(8,128)(2,1)S(1)} %shard_map.230.refs_6_) | copy-start | bytes 1769476
  30.3 23.8 %collective-permute-start.7 = (bf16[384,768]{1,0:T(8,128)(2,1)S(1)}, bf16[384,768]{1,0:T(8,128)(2,1)S(1)}, u32[]{:S(2)}, u32[]{:S(2)}) collective-permute-start(bf16[384,768]{1,0:T(8,128)(2,1)S(1)} %shard_map.230.refs_6_), channel_id=1, source_target_pairs={{0,1},{1,0},{2,3},{3,2},{4,5},{5,4},{6,7},{7,6},{8,24},{9,25},{10,... | collective-permute-start | bytes 1769480 | tf_op jit(solution)/shard_map/ppermute | solution.py:660
  49.0 64.3 %copy-start.8 = (bf16[576,768]{1,0:T(8,128)(2,1)}, bf16[576,768]{1,0:T(8,128)(2,1)S(1)}, u32[]{:S(2)}) copy-start(bf16[576,768]{1,0:T(8,128)(2,1)S(1)} %shard_map.233.refs_7_) | copy-start | bytes 2654212
  49.0 50.0 %copy-start.32 = (s32[512]{0:T(512)S(1)}, s32[512]{0:T(512)}, u32[]{:S(2)}) copy-start(s32[512]{0:T(512)} %param.17) | copy-start | bytes 6148
  49.0 24.9 %collective-permute-start.17 = (bf16[576,768]{1,0:T(8,128)(2,1)S(1)}, bf16[576,768]{1,0:T(8,128)(2,1)}, u32[]{:S(2)}, u32[]{:S(2)}) collective-permute-start(bf16[576,768]{1,0:T(8,128)(2,1)S(1)} %shard_map.233.refs_7_), channel_id=1, source_target_pairs={{0,1},{1,0},{2,3},{3,2},{4,5},{5,4},{6,7},{7,6},{8,24},{9,25},{10,... | collective-permute-start | bytes 2654216 | tf_op jit(solution)/shard_map/ppermute | solution.py:660
  50.6 22.3 %collective-permute-start.8 = (bf16[384,768]{1,0:T(8,128)(2,1)S(1)}, bf16[384,768]{1,0:T(8,128)(2,1)S(1)}, u32[]{:S(2)}, u32[]{:S(2)}) collective-permute-start(bf16[384,768]{1,0:T(8,128)(2,1)S(1)} %shard_map.230.refs_6_), channel_id=1, source_target_pairs={{0,16},{1,17},{2,18},{3,19},{4,20},{5,21},{6,22},{7,23},{8,9},{9,8... | collective-permute-start | bytes 1769480 | tf_op jit(solution)/shard_map/ppermute | solution.py:660
  52.1 18.0 %collective-permute-start.2 = (bf16[320,768]{1,0:T(8,128)(2,1)S(1)}, bf16[320,768]{1,0:T(8,128)(2,1)S(1)}, u32[]{:S(2)}, u32[]{:S(2)}) collective-permute-start(bf16[320,768]{1,0:T(8,128)(2,1)S(1)} %collective-permute-done.refs_1_), channel_id=1, source_target_pairs={{0,16},{1,17},{2,18},{3,19},{4,20},{5,21},{6,22},{7,23},{8,9},{9,8... | collective-permute-start | bytes 1474568 | tf_op jit(solution)/shard_map/ppermute | solution.py:660
  52.6 27.1 %collective-permute-start.18 = (bf16[576,768]{1,0:T(8,128)(2,1)S(1)}, bf16[576,768]{1,0:T(8,128)(2,1)}, u32[]{:S(2)}, u32[]{:S(2)}) collective-permute-start(bf16[576,768]{1,0:T(8,128)(2,1)S(1)} %shard_map.233.refs_7_), channel_id=1, source_target_pairs={{0,16},{1,17},{2,18},{3,19},{4,20},{5,21},{6,22},{7,23},{8,9},{9,8... | collective-permute-start | bytes 2654216 | tf_op jit(solution)/shard_map/ppermute | solution.py:660
  54.1 45.7 %copy-start.24 = (bf16[384,768]{1,0:T(8,128)(2,1)}, bf16[384,768]{1,0:T(8,128)(2,1)S(1)}, u32[]{:S(2)}) copy-start(bf16[384,768]{1,0:T(8,128)(2,1)S(1)} %collective-permute-done.7.refs_7_) | copy-start | bytes 1769476
  54.1 19.8 %collective-permute-start.10 = (bf16[384,768]{1,0:T(8,128)(2,1)S(1)}, bf16[384,768]{1,0:T(8,128)(2,1)S(1)}, u32[]{:S(2)}, u32[]{:S(2)}) collective-permute-start(bf16[384,768]{1,0:T(8,128)(2,1)S(1)} %shard_map.230.refs_6_), channel_id=1, source_target_pairs={{0,8},{1,9},{2,10},{3,11},{4,12},{5,13},{6,14},{7,15},{8,0},{9,1},... | collective-permute-start | bytes 1769480 | tf_op jit(solution)/shard_map/ppermute | solution.py:42
  70.1 15.8 %collective-permute-start.9 = (bf16[384,768]{1,0:T(8,128)(2,1)S(1)}, bf16[384,768]{1,0:T(8,128)(2,1)S(1)}, u32[]{:S(2)}, u32[]{:S(2)}) collective-permute-start(bf16[384,768]{1,0:T(8,128)(2,1)S(1)} %collective-permute-done.7.refs_7_), channel_id=1, source_target_pairs={{0,16},{1,17},{2,18},{3,19},{4,20},{5,21},{6,22},{7,23},{8,9},{9,8... | collective-permute-start | bytes 1769480 | tf_op jit(solution)/shard_map/ppermute | solution.py:660
  72.9 26.9 %copy-start = (bf16[1280,768]{1,0:T(8,128)(2,1)}, bf16[1280,768]{1,0:T(8,128)(2,1)S(1)}, u32[]{:S(2)}) copy-start(bf16[1280,768]{1,0:T(8,128)(2,1)S(1)} %shard_map.229.refs_4_.refs_5_) | copy-start | bytes 5898244
  72.9 14.4 %copy-start.25 = (bf16[384,768]{1,0:T(8,128)(2,1)}, bf16[384,768]{1,0:T(8,128)(2,1)S(1)}, u32[]{:S(2)}) copy-start(bf16[384,768]{1,0:T(8,128)(2,1)S(1)} %collective-permute-done.8.refs_8_) | copy-start | bytes 1769476
  72.9 26.9 %collective-permute-start.3 = (bf16[1280,768]{1,0:T(8,128)(2,1)S(1)}, bf16[1280,768]{1,0:T(8,128)(2,1)}, u32[]{:S(2)}, u32[]{:S(2)}) collective-permute-start(bf16[1280,768]{1,0:T(8,128)(2,1)S(1)} %shard_map.229.refs_4_.refs_5_), channel_id=1, source_target_pairs={{0,8},{1,9},{2,10},{3,11},{4,12},{5,13},{6,14},{7,15},{8,0},{9,1},... | collective-permute-start | bytes 5898248 | tf_op jit(solution)/shard_map/ppermute | solution.py:42
  73.9 21.6 %collective-permute-start.19 = (bf16[576,768]{1,0:T(8,128)(2,1)}, bf16[576,768]{1,0:T(8,128)(2,1)}, u32[]{:S(2)}, u32[]{:S(2)}) collective-permute-start(bf16[576,768]{1,0:T(8,128)(2,1)} %collective-permute-done.17.refs_8_), channel_id=1, source_target_pairs={{0,16},{1,17},{2,18},{3,19},{4,20},{5,21},{6,22},{7,23},{8,9},{9,8... | collective-permute-start | bytes 2654216 | tf_op jit(solution)/shard_map/ppermute | solution.py:660
  73.9 13.5 %copy-start.26 = (bf16[384,768]{1,0:T(8,128)(2,1)}, bf16[384,768]{1,0:T(8,128)(2,1)S(1)}, u32[]{:S(2)}) copy-start(bf16[384,768]{1,0:T(8,128)(2,1)S(1)} %collective-permute-done.10.refs_10_) | copy-start | bytes 1769476
  73.9 13.4 %collective-permute-start.11 = (bf16[384,768]{1,0:T(8,128)(2,1)S(1)}, bf16[384,768]{1,0:T(8,128)(2,1)S(1)}, u32[]{:S(2)}, u32[]{:S(2)}) collective-permute-start(bf16[384,768]{1,0:T(8,128)(2,1)S(1)} %collective-permute-done.7.refs_7_), channel_id=1, source_target_pairs={{0,8},{1,9},{2,10},{3,11},{4,12},{5,13},{6,14},{7,15},{8,0},{9,1},... | collective-permute-start | bytes 1769480 | tf_op jit(solution)/shard_map/ppermute | solution.py:42
  79.7 7.7 %collective-permute-start.12 = (bf16[384,768]{1,0:T(8,128)(2,1)S(1)}, bf16[384,768]{1,0:T(8,128)(2,1)S(1)}, u32[]{:S(2)}, u32[]{:S(2)}) collective-permute-start(bf16[384,768]{1,0:T(8,128)(2,1)S(1)} %collective-permute-done.8.refs_8_), channel_id=1, source_target_pairs={{0,8},{1,9},{2,10},{3,11},{4,12},{5,13},{6,14},{7,15},{8,0},{9,1},... | collective-permute-start | bytes 1769480 | tf_op jit(solution)/shard_map/ppermute | solution.py:42
  85.9 3.1 collective-permute-start.13
  87.3 38.3 %collective-permute-start.20 = (bf16[576,768]{1,0:T(8,128)(2,1)S(1)}, bf16[576,768]{1,0:T(8,128)(2,1)}, u32[]{:S(2)}, u32[]{:S(2)}) collective-permute-start(bf16[576,768]{1,0:T(8,128)(2,1)S(1)} %shard_map.233.refs_7_), channel_id=1, source_target_pairs={{0,8},{1,9},{2,10},{3,11},{4,12},{5,13},{6,14},{7,15},{8,0},{9,1},... | collective-permute-start | bytes 2654216 | tf_op jit(solution)/shard_map/ppermute | solution.py:42
  87.4 38.2 %collective-permute-start.21 = (bf16[576,768]{1,0:T(8,128)(2,1)}, bf16[576,768]{1,0:T(8,128)(2,1)}, u32[]{:S(2)}, u32[]{:S(2)}) collective-permute-start(bf16[576,768]{1,0:T(8,128)(2,1)} %collective-permute-done.17.refs_8_), channel_id=1, source_target_pairs={{0,8},{1,9},{2,10},{3,11},{4,12},{5,13},{6,14},{7,15},{8,0},{9,1},... | collective-permute-start | bytes 2654216 | tf_op jit(solution)/shard_map/ppermute | solution.py:42
  89.0 36.7 %collective-permute-start.22 = (bf16[576,768]{1,0:T(8,128)(2,1)}, bf16[576,768]{1,0:T(8,128)(2,1)}, u32[]{:S(2)}, u32[]{:S(2)}) collective-permute-start(bf16[576,768]{1,0:T(8,128)(2,1)} %collective-permute-done.18.refs_9_), channel_id=1, source_target_pairs={{0,8},{1,9},{2,10},{3,11},{4,12},{5,13},{6,14},{7,15},{8,0},{9,1},... | collective-permute-start | bytes 2654216 | tf_op jit(solution)/shard_map/ppermute | solution.py:42
  95.5 30.2 %collective-permute-start.23 = (bf16[576,768]{1,0:T(8,128)(2,1)}, bf16[576,768]{1,0:T(8,128)(2,1)}, u32[]{:S(2)}, u32[]{:S(2)}) collective-permute-start(bf16[576,768]{1,0:T(8,128)(2,1)} %collective-permute-done.19.refs_10_), channel_id=1, source_target_pairs={{0,8},{1,9},{2,10},{3,11},{4,12},{5,13},{6,14},{7,15},{8,0},{9,1},... | collective-permute-start | bytes 2654216 | tf_op jit(solution)/shard_map/ppermute | solution.py:42
  125.7 34.2 %copy-start.31 = (bf16[512,192]{0,1:T(8,128)(2,1)S(1)}, bf16[512,192]{0,1:T(8,128)(2,1)}, u32[]{:S(2)}) copy-start(bf16[512,192]{0,1:T(8,128)(2,1)} %param.27) | copy-start | bytes 589828
  158.8 48.5 %collective-permute-start.32 = (bf16[16,192,768]{2,1,0:T(8,128)(2,1)}, bf16[16,192,768]{2,1,0:T(8,128)(2,1)}, u32[]{:S(2)}, u32[]{:S(2)}) collective-permute-start(bf16[16,192,768]{2,1,0:T(8,128)(2,1)} %get-tuple-element.127), channel_id=1, source_target_pairs={{0,8},{1,9},{2,10},{3,11},{4,12},{5,13},{6,14},{7,15},{8,0},{9,1},... | collective-permute-start | bytes 14155784 | tf_op jit(solution)/shard_map/ppermute | solution.py:42
  160.7 11.0 %copy-start.1 = (bf16[12,512,128]{2,1,0:T(8,128)(2,1)S(1)}, bf16[12,512,128]{2,1,0:T(8,128)(2,1)}, u32[]{:S(2)}) copy-start(bf16[12,512,128]{2,1,0:T(8,128)(2,1)} %get-tuple-element.74.refs_2_.q_any) | copy-start | bytes 4718596
  160.8 11.0 %copy-start.2 = (bf16[12,512,128]{2,1,0:T(8,128)(2,1)S(1)}, bf16[12,512,128]{2,1,0:T(8,128)(2,1)}, u32[]{:S(2)}) copy-start(bf16[12,512,128]{2,1,0:T(8,128)(2,1)} %get-tuple-element.75.refs_3_.k_any) | copy-start | bytes 4718596
  160.8 11.0 %copy-start.18 = (f32[6,1,512]{2,1,0:T(1,128)S(1)}, f32[6,1,512]{2,1,0:T(1,128)}, u32[]{:S(2)}) copy-start(f32[6,1,512]{2,1,0:T(1,128)} %get-tuple-element.98.lse_any) | copy-start | bytes 36868
  174.6 9.6 %copy-start.17 = (f32[6,1,512]{2,1,0:T(1,128)S(1)}, f32[6,1,512]{2,1,0:T(1,128)}, u32[]{:S(2)}) copy-start(f32[6,1,512]{2,1,0:T(1,128)} %get-tuple-element.93.lse_any) | copy-start | bytes 36868
  184.2 9.5 %copy-start.4 = (bf16[512,768]{1,0:T(8,128)(2,1)S(1)}, bf16[512,768]{1,0:T(8,128)(2,1)}, u32[]{:S(2)}) copy-start(bf16[512,768]{1,0:T(8,128)(2,1)} %refs_1_.3) | copy-start | bytes 2359300
  184.2 9.5 %copy-start.6 = (bf16[512,192]{1,0:T(8,128)(2,1)S(1)}, bf16[512,192]{1,0:T(8,128)(2,1)}, u32[]{:S(2)}) copy-start(bf16[512,192]{1,0:T(8,128)(2,1)} %copy.37.refs_3_.refs_1_.refs_2_) | copy-start | bytes 589828
  184.2 9.5 %copy-start.11 = (bf16[768,768]{1,0:T(8,128)(2,1)S(1)}, bf16[768,768]{1,0:T(8,128)(2,1)}, u32[]{:S(2)}) copy-start(bf16[768,768]{1,0:T(8,128)(2,1)} %get-tuple-element.102.refs_9_) | copy-start | bytes 3538948
  184.3 9.5 %copy-start.13 = (bf16[768,192]{1,0:T(8,128)(2,1)S(1)}, bf16[768,192]{1,0:T(8,128)(2,1)}, u32[]{:S(2)}) copy-start(bf16[768,192]{1,0:T(8,128)(2,1)} %get-tuple-element.104.refs_11_) | copy-start | bytes 884740
  184.3 9.5 %copy-start.14 = (bf16[768,192]{1,0:T(8,128)(2,1)S(1)}, bf16[768,192]{1,0:T(8,128)(2,1)}, u32[]{:S(2)}) copy-start(bf16[768,192]{1,0:T(8,128)(2,1)} %get-tuple-element.105.refs_12_) | copy-start | bytes 884740
  199.7 5.7 %collective-permute-start.24 = (bf16[16,128,768]{2,1,0:T(8,128)(2,1)S(1)}, bf16[16,128,768]{2,1,0:T(8,128)(2,1)S(1)}, u32[]{:S(2)}, u32[]{:S(2)}) collective-permute-start(bf16[16,128,768]{2,1,0:T(8,128)(2,1)S(1)} %get-tuple-element.117), channel_id=1, source_target_pairs={{0,8},{1,9},{2,10},{3,11},{4,12},{5,13},{6,14},{7,15},{8,0},{9,1},... | collective-permute-start | bytes 9437192 | tf_op jit(solution)/shard_map/ppermute | solution.py:42
  205.4 19.3 %copy-start.22 = (bf16[16,128,768]{2,1,0:T(8,128)(2,1)}, bf16[16,128,768]{2,1,0:T(8,128)(2,1)S(1)}, u32[]{:S(2)}) copy-start(bf16[16,128,768]{2,1,0:T(8,128)(2,1)S(1)} %collective-permute-done.24) | copy-start | bytes 9437188
  205.7 16.3 %collective-permute-start.25 = (bf16[6,128,768]{2,1,0:T(8,128)(2,1)S(1)}, bf16[6,128,768]{2,1,0:T(8,128)(2,1)S(1)}, u32[]{:S(2)}, u32[]{:S(2)}) collective-permute-start(bf16[6,128,768]{2,1,0:T(8,128)(2,1)S(1)} %bitcast.188), channel_id=1, source_target_pairs={{0,1},{1,0},{2,3},{3,2},{4,5},{5,4},{6,7},{7,6},{8,24},{9,25},{10,... | collective-permute-start | bytes 3538952 | tf_op jit(solution)/shard_map/ppermute | solution.py:660
  207.3 19.8 %slice-start = ((s8[4718592]{0:T(1024)(128)(4,1)}), s8[4194304]{0:T(1024)(128)(4,1)S(1)}, s32[]{:S(2)}) async-start(s8[4718592]{0:T(1024)(128)(4,1)} %bitcast.168), calls=%async_computation | async-start | bytes 8388608
  207.3 19.8 %slice-start.1 = ((s8[4718592]{0:T(1024)(128)(4,1)}), s8[524288]{0:T(1024)(128)(4,1)S(1)}, s32[]{:S(2)}) async-start(s8[4718592]{0:T(1024)(128)(4,1)} %bitcast.168), calls=%async_computation.1 | async-start | bytes 1048576
  211.1 15.9 %copy-start.7 = (bf16[768,192]{1,0:T(8,128)(2,1)S(1)}, bf16[768,192]{1,0:T(8,128)(2,1)}, u32[]{:S(2)}) copy-start(bf16[768,192]{1,0:T(8,128)(2,1)} %get-tuple-element.79.refs_7_.refs_11_.refs_5_) | copy-start | bytes 884740
  211.1 15.9 %copy-start.10 = (f32[512,768]{1,0:T(8,128)S(1)}, f32[512,768]{1,0:T(8,128)}, u32[]{:S(2)}) copy-start(f32[512,768]{1,0:T(8,128)} %get-tuple-element.112.refs_2_) | copy-start | bytes 4718596
  211.1 15.9 %copy-start.12 = (f32[512,192]{1,0:T(8,128)S(1)}, f32[512,192]{1,0:T(8,128)}, u32[]{:S(2)}) copy-start(f32[512,192]{1,0:T(8,128)} %get-tuple-element.113.refs_3_) | copy-start | bytes 1179652
  211.1 40.5 %collective-permute-start.33 = (bf16[6,192,768]{2,1,0:T(8,128)(2,1)}, bf16[6,192,768]{2,1,0:T(8,128)(2,1)}, u32[]{:S(2)}, u32[]{:S(2)}) collective-permute-start(bf16[6,192,768]{2,1,0:T(8,128)(2,1)} %bitcast.33), channel_id=1, source_target_pairs={{0,1},{1,0},{2,3},{3,2},{4,5},{5,4},{6,7},{7,6},{8,24},{9,25},{10,... | collective-permute-start | bytes 5308424 | tf_op jit(solution)/shard_map/ppermute | solution.py:660
  222.0 9.7 %copy-start.23 = (bf16[6,128,768]{2,1,0:T(8,128)(2,1)}, bf16[6,128,768]{2,1,0:T(8,128)(2,1)S(1)}, u32[]{:S(2)}) copy-start(bf16[6,128,768]{2,1,0:T(8,128)(2,1)S(1)} %collective-permute-done.25) | copy-start | bytes 3538948
  223.2 16.5 %collective-permute-start.26 = (bf16[3,128,768]{2,1,0:T(8,128)(2,1)}, bf16[3,128,768]{2,1,0:T(8,128)(2,1)}, u32[]{:S(2)}, u32[]{:S(2)}) collective-permute-start(bf16[3,128,768]{2,1,0:T(8,128)(2,1)} %fusion.1), channel_id=1, source_target_pairs={{0,16},{1,17},{2,18},{3,19},{4,20},{5,21},{6,22},{7,23},{8,9},{9,8... | collective-permute-start | bytes 1769480 | tf_op jit(solution)/shard_map/ppermute | solution.py:660
  225.6 26.0 %collective-permute-start.30 = (bf16[2,128,768]{2,1,0:T(8,128)(2,1)}, bf16[2,128,768]{2,1,0:T(8,128)(2,1)}, u32[]{:S(2)}, u32[]{:S(2)}) collective-permute-start(bf16[2,128,768]{2,1,0:T(8,128)(2,1)} %fusion.9), channel_id=1, source_target_pairs={{0,1},{1,0},{2,3},{3,2},{4,5},{5,4},{6,7},{7,6},{8,24},{9,25},{10,... | collective-permute-start | bytes 1179656 | tf_op jit(solution)/shard_map/ppermute | solution.py:660
  241.6 16.7 %collective-permute-start.27 = (bf16[128,768]{1,0:T(8,128)(2,1)S(1)}, bf16[128,768]{1,0:T(8,128)(2,1)S(1)}, u32[]{:S(2)}, u32[]{:S(2)}) collective-permute-start(bf16[128,768]{1,0:T(8,128)(2,1)S(1)} %get-tuple-element.163), channel_id=1, source_target_pairs={{0,2},{1,3},{2,0},{3,1},{4,6},{5,7},{6,4},{7,5},{8,10},{9,11},{10,... | collective-permute-start | bytes 589832 | tf_op jit(solution)/shard_map/ppermute | solution.py:42
  248.5 16.4 %collective-permute-start.28 = (bf16[128,768]{1,0:T(8,128)(2,1)S(1)}, bf16[128,768]{1,0:T(8,128)(2,1)S(1)}, u32[]{:S(2)}, u32[]{:S(2)}) collective-permute-start(bf16[128,768]{1,0:T(8,128)(2,1)S(1)} %get-tuple-element.165), channel_id=1, source_target_pairs={{0,4},{1,5},{2,6},{3,7},{4,0},{5,1},{6,2},{7,3},{8,12},{9,13},{10,... | collective-permute-start | bytes 589832 | tf_op jit(solution)/shard_map/ppermute | solution.py:42
  249.6 15.3 %collective-permute-start.29 = (bf16[128,768]{1,0:T(8,128)(2,1)S(1)}, bf16[128,768]{1,0:T(8,128)(2,1)S(1)}, u32[]{:S(2)}, u32[]{:S(2)}) collective-permute-start(bf16[128,768]{1,0:T(8,128)(2,1)S(1)} %get-tuple-element.164), channel_id=1, source_target_pairs={{0,6},{1,7},{2,4},{3,5},{4,2},{5,3},{6,0},{7,1},{8,14},{9,15},{10,... | collective-permute-start | bytes 589832 | tf_op jit(solution)/shard_map/ppermute | solution.py:42
  253.6 24.1 %collective-permute-start.34 = (bf16[3,192,768]{2,1,0:T(8,128)(2,1)S(1)}, bf16[3,192,768]{2,1,0:T(8,128)(2,1)S(1)}, u32[]{:S(2)}, u32[]{:S(2)}) collective-permute-start(bf16[3,192,768]{2,1,0:T(8,128)(2,1)S(1)} %fusion), channel_id=1, source_target_pairs={{0,16},{1,17},{2,18},{3,19},{4,20},{5,21},{6,22},{7,23},{8,9},{9,8... | collective-permute-start | bytes 2654216 | tf_op jit(solution)/shard_map/ppermute | solution.py:660
  256.2 18.9 %collective-permute-start.31 = (bf16[128,768]{1,0:T(8,128)(2,1)S(1)}, bf16[128,768]{1,0:T(8,128)(2,1)S(1)}, u32[]{:S(2)}, u32[]{:S(2)}) collective-permute-start(bf16[128,768]{1,0:T(8,128)(2,1)S(1)} %fusion.10), channel_id=1, source_target_pairs={{0,16},{1,17},{2,18},{3,19},{4,20},{5,21},{6,22},{7,23},{8,9},{9,8... | collective-permute-start | bytes 589832 | tf_op jit(solution)/shard_map/ppermute | solution.py:660
  258.3 31.0 %collective-permute-start.38 = (bf16[2,192,768]{2,1,0:T(8,128)(2,1)S(1)}, bf16[2,192,768]{2,1,0:T(8,128)(2,1)S(1)}, u32[]{:S(2)}, u32[]{:S(2)}) collective-permute-start(bf16[2,192,768]{2,1,0:T(8,128)(2,1)S(1)} %fusion.2), channel_id=1, source_target_pairs={{0,1},{1,0},{2,3},{3,2},{4,5},{5,4},{6,7},{7,6},{8,24},{9,25},{10,... | collective-permute-start | bytes 1769480 | tf_op jit(solution)/shard_map/ppermute | solution.py:660
  279.8 15.7 %collective-permute-start.35 = (bf16[192,768]{1,0:T(8,128)(2,1)S(1)}, bf16[192,768]{1,0:T(8,128)(2,1)S(1)}, u32[]{:S(2)}, u32[]{:S(2)}) collective-permute-start(bf16[192,768]{1,0:T(8,128)(2,1)S(1)} %get-tuple-element.160), channel_id=1, source_target_pairs={{0,2},{1,3},{2,0},{3,1},{4,6},{5,7},{6,4},{7,5},{8,10},{9,11},{10,... | collective-permute-start | bytes 884744 | tf_op jit(solution)/shard_map/ppermute | solution.py:42
  286.7 22.7 %collective-permute-start.36 = (bf16[192,768]{1,0:T(8,128)(2,1)S(1)}, bf16[192,768]{1,0:T(8,128)(2,1)S(1)}, u32[]{:S(2)}, u32[]{:S(2)}) collective-permute-start(bf16[192,768]{1,0:T(8,128)(2,1)S(1)} %get-tuple-element.162), channel_id=1, source_target_pairs={{0,4},{1,5},{2,6},{3,7},{4,0},{5,1},{6,2},{7,3},{8,12},{9,13},{10,... | collective-permute-start | bytes 884744 | tf_op jit(solution)/shard_map/ppermute | solution.py:42
  287.9 21.6 %collective-permute-start.37 = (bf16[192,768]{1,0:T(8,128)(2,1)S(1)}, bf16[192,768]{1,0:T(8,128)(2,1)S(1)}, u32[]{:S(2)}, u32[]{:S(2)}) collective-permute-start(bf16[192,768]{1,0:T(8,128)(2,1)S(1)} %get-tuple-element.161), channel_id=1, source_target_pairs={{0,6},{1,7},{2,4},{3,5},{4,2},{5,3},{6,0},{7,1},{8,14},{9,15},{10,... | collective-permute-start | bytes 884744 | tf_op jit(solution)/shard_map/ppermute | solution.py:42
  290.4 19.1 %collective-permute-start.39 = (bf16[192,768]{1,0:T(8,128)(2,1)S(1)}, bf16[192,768]{1,0:T(8,128)(2,1)S(1)}, u32[]{:S(2)}, u32[]{:S(2)}) collective-permute-start(bf16[192,768]{1,0:T(8,128)(2,1)S(1)} %fusion.3), channel_id=1, source_target_pairs={{0,16},{1,17},{2,18},{3,19},{4,20},{5,21},{6,22},{7,23},{8,9},{9,8... | collective-permute-start | bytes 884744 | tf_op jit(solution)/shard_map/ppermute | solution.py:660
  (11 other events, 62.5 us)
